TPU v7x, 32 devices: a whole 2x2x4 slice. The times are simulated.
32 devices in a mesh: grp: 2 (over y), cls: 8 (over z, x), ori: 2 (over core).
Axes of the slice: x: 2, y: 2, z: 4, core: 2. Of those that a mesh axis runs over, the one named last changes fastest.
Arguments:
- particles: bfloat16 [512, 16384], P(('grp', 'cls')), parts along dimension 0, may hold values from -6 to 6
- tau: bfloat16 [512], P(('grp', 'cls')), parts along dimension 0, may hold values from 0.019897461 to 0.079589844
- candidates: int32 [512, 2], P(('grp', 'cls')), parts along dimension 0, may hold values from 0 to 7, all different within a row; in each aligned block of 32 rows (0 to 31, 32 to 63, ...) at most 16 rows name the same one
- prune: int32 [512, 256], P(('grp', 'cls'), 'ori'), parts along dimension 0, may hold values from 0 to 1, as said below
- projections: bfloat16 [8, 256, 16384], P('cls', 'ori'), may hold values from -6 to 6
Outputs:
- expected: bfloat16 [512, 16384], P(('grp', 'cls'), 'ori'), parts along dimension 0
There are 2 independent parts, one for each index of `grp`. A program takes and returns all parts, laid end to end along the dimension named above; an argument that names none is the same for every part. Nothing has to cross between parts.
Inputs may be any that keep to these rules, and one draw needn't show every extreme that they name: `candidates`: within the rows of one device no class is named by more than 16 rows, a bound that some block reaches; the 2 classes of a row differ. `prune`: every particle keeps at least one orientation.
All inputs are finite; a program needn't handle non-finite values.
Results may differ from a plain program's by a relative error of at most 0.0034.
Values may be sent and summed in bfloat16 or wider, within the bound.
No kernel may reach another device: no remote copies, remote signals or barrier semaphores. Data moves between devices by JAX's collectives and lax.ppermute only.
A program may use at most 128 MiB of HBM per device.

v0:
```python
import jax
import jax.numpy as jnp
from jax import lax
from jax.sharding import PartitionSpec as P

BOX = 128


shift_table = ((0, 0), (1, 0), (-1, 0), (0, 1), (0, -1))


def on_device(particles, tau, candidates, prune, projections):
    class_count = lax.axis_size("cls")
    ori_count = lax.axis_size("ori")
    part_rows = particles.shape[0]
    choose_count = candidates.shape[1]
    pixels = particles.shape[1]
    orient_rows = prune.shape[1]
    shift_count = len(shift_table)
    capacity = 2 * part_rows * choose_count // class_count
    slot_count = class_count * capacity
    record_count = part_rows * choose_count
    destination = candidates.reshape(record_count)
    onehot = (destination[:, None] == jnp.arange(class_count, dtype=jnp.int32)[None, :]).astype(
        jnp.int32
    )
    before = jnp.cumsum(onehot, axis=0) - onehot
    slot_rank = jnp.sum(before * onehot, axis=1)
    slot_of = destination * capacity + slot_rank
    matched = slot_of[None, :] == jnp.arange(slot_count, dtype=jnp.int32)[:, None]
    occupied = jnp.any(matched, axis=1)
    source_row = (
        jnp.sum(jnp.where(matched, jnp.arange(record_count, dtype=jnp.int32)[None, :], 0), axis=1)
        // choose_count
    )
    send_images = jnp.where(occupied[:, None], particles[source_row], jnp.zeros((), jnp.bfloat16))
    send_images = send_images.reshape(class_count, capacity, pixels)
    send_tau = jnp.where(occupied, tau[source_row], jnp.zeros((), jnp.bfloat16)).reshape(
        class_count, capacity
    )
    send_keep = jnp.where(occupied[:, None], prune[source_row], 0).astype(jnp.bfloat16)
    send_keep = send_keep.reshape(class_count, capacity, orient_rows)
    own_rows = projections[0]
    grid_rows = own_rows.reshape(orient_rows, BOX, BOX)
    shifted = jnp.stack([jnp.roll(grid_rows, offset, axis=(1, 2)) for offset in shift_table])
    shifted = shifted.reshape(shift_count * orient_rows, pixels)
    row_norms = jnp.sum(jnp.square(own_rows.astype(jnp.float32)), axis=1)
    norms_all = jnp.tile(row_norms, shift_count)
    images = lax.all_to_all(send_images, "cls", split_axis=0, concat_axis=0, tiled=True)
    scales = lax.all_to_all(send_tau, "cls", split_axis=0, concat_axis=0, tiled=True)
    keep_rows = lax.all_to_all(send_keep, "cls", split_axis=0, concat_axis=0, tiled=True)
    lead_count = images.shape[0]
    item_count = images.shape[1]
    row_count = lead_count * item_count
    flat_images = images.reshape(row_count, pixels)
    products = lax.dot_general(
        flat_images, shifted, (((1,), (1,)), ((), ())), preferred_element_type=jnp.float32
    )
    scores = scales.reshape(row_count).astype(jnp.float32)[:, None] * (
        products - 0.5 * norms_all[None, :]
    )
    keep_all = jnp.tile(keep_rows.reshape(row_count, orient_rows), (1, shift_count)) > 0
    local_peak = jnp.max(jnp.where(keep_all, scores, jnp.float32(-1e30)), axis=1)
    peak_score = lax.pmax(local_peak, "ori")
    weights = jnp.exp(jnp.where(keep_all, scores - peak_score[:, None], -jnp.inf)).astype(
        jnp.bfloat16
    )
    weight_total = jnp.sum(weights.astype(jnp.float32), axis=1)
    summed = jnp.dot(weights, shifted, preferred_element_type=jnp.float32)
    spread = jnp.broadcast_to(weight_total[:, None], (row_count, ori_count))
    part_sum = lax.psum_scatter(summed, "ori", scatter_dimension=1, tiled=True)
    part_total = lax.psum_scatter(spread, "ori", scatter_dimension=1, tiled=True)
    safe_total = jnp.where(part_total[:, 0] > 0, part_total[:, 0], 1.0)
    unit_image = part_sum / safe_total[:, None]
    log_weight = peak_score + jnp.log(safe_total)
    back_unit = lax.all_to_all(
        unit_image.reshape(lead_count, item_count, -1),
        "cls",
        split_axis=0,
        concat_axis=0,
        tiled=True,
    )
    back_log = lax.all_to_all(
        log_weight.reshape(lead_count, item_count), "cls", split_axis=0, concat_axis=0, tiled=True
    )
    flat_unit = back_unit.reshape(slot_count, -1)
    flat_log = back_log.reshape(slot_count)
    record_unit = flat_unit[slot_of].reshape(part_rows, choose_count, -1)
    record_log = flat_log[slot_of].reshape(part_rows, choose_count)
    best_log = jnp.max(record_log, axis=1, keepdims=True)
    factors = jnp.exp(record_log - best_log)
    expected = (
        jnp.sum(factors[:, :, None] * record_unit, axis=1) / jnp.sum(factors, axis=1)[:, None]
    )
    return expected.astype(jnp.bfloat16)


def solution(mesh):
    placed = (
        P(("grp", "cls"), None),
        P(("grp", "cls")),
        P(("grp", "cls"), None),
        P(("grp", "cls"), "ori"),
        P("cls", "ori", None),
    )
    return jax.shard_map(
        on_device, mesh=mesh, in_specs=placed, out_specs=P(("grp", "cls"), "ori"), check_vma=False
    )
```

profile of v0, /device:TPU:0, one launch (start us, length us, event | category | flops | bytes accessed | tf_op | source)
XLA Modules:
  0.0 329.2 jit_solution(2726485296542667512)
XLA Ops:
  8.1 1.6 gather_fusion.1
  10.4 7.3 %all-to-all-start.1 = ((bf16[8,1,16]{2,1,0:T(2,128)(2,1)}), bf16[8,1,16]{2,1,0:T(2,128)(2,1)S(1)}, u32[]{:S(2)}, u32[]{:S(2)}) async-start(bf16[8,1,16]{2,1,0:T(2,128)(2,1)} %select_n.91), calls=%async_computation.1 | async-start | bytes 8192 | tf_op jit(solution)/shard_map/all_to_all | solution.py:50
  17.7 1.4 gather_fusion
  19.8 5.1 %gather_fusion.2 = bf16[128,16384]{1,0:T(8,128)(2,1)} fusion(bf16[32,16384]{1,0:T(8,128)(2,1)S(1)} %copy-done, s32[1024]{0:T(1024)S(1)} %pad_clamp_fusion.1), kind=kCustom, calls=%fused_computation.2 | custom fusion | bytes 8389120 | tf_op jit(solution)/shard_map/gather | solution.py:36
  24.9 6.0 %all-to-all-start = ((bf16[8,16,128]{2,1,0:T(8,128)(2,1)}), bf16[8,16,128]{2,1,0:T(8,128)(2,1)S(1)}, u32[]{:S(2)}, u32[]{:S(2)}) async-start(bf16[8,16,128]{2,1,0:T(8,128)(2,1)} %select_convert_fusion), calls=%async_computation | async-start | bytes 65536 | tf_op jit(solution)/shard_map/all_to_all | solution.py:51
  30.9 4.5 %broadcast_select_fusion = bf16[8,16,16384]{2,1,0:T(8,128)(2,1)} fusion(bf16[8,16,16384]{2,1,0:T(8,128)(2,1)} %bitcast.78, pred[8,16]{1,0:T(8,128)(4,1)S(1)} %broadcast_in_dim.79), kind=kLoop, calls=%fused_computation.21 | loop fusion | flops 2097152 | bytes 8388736 | tf_op jit(solution)/shard_map/jit(_where)/select_n | solution.py:36
  35.4 2.2 all-to-all-done
  37.6 4.6 %all-to-all-start.2 = ((bf16[8,16,16384]{2,1,0:T(8,128)(2,1)}), bf16[8,16,16384]{2,1,0:T(8,128)(2,1)}, u32[]{:S(2)}, u32[]{:S(2)}) async-start(bf16[8,16,16384]{2,1,0:T(8,128)(2,1)} %broadcast_select_fusion), calls=%async_computation.2 | async-start | bytes 8388608 | tf_op jit(solution)/shard_map/all_to_all | solution.py:49
  42.8 3.4 %copy.27 = bf16[16,8,128,128]{3,2,1,0:T(8,128)(2,1)S(1)} copy(bf16[16,8,128,128]{3,1,2,0:T(8,128)(2,1)} %bitcast.79) | data formatting | bytes 8388608
  46.2 2.6 bitcast_dynamic-update-slice_fusion
  48.8 1.1 copy-done.2
  50.9 2.8 fusion.26
  53.7 4.3 %fusion.6 = bf16[5,128,128,128]{3,2,1,0:T(8,128)(2,1)} fusion(bf16[5,128,128,128]{3,2,1,0:T(8,128)(2,1)} %bitcast_dynamic-update-slice_fusion, bf16[128,127,128]{2,1,0:T(8,128)(2,1)S(1)} %get-tuple-element.14, bf16[128,1,128]{2,1,0:T(2,128)(2,1)S(1)} %get-tuple-element.16), kind=kLoop, calls=%fused_computation.14 | loop fusion | flops 8388608 | bytes 8388608
  58.0 2.6 fusion.7
  60.6 2.0 fusion.24
  62.6 2.0 fusion.25
  64.6 3.7 %fusion.8 = bf16[5,128,128,128]{3,2,1,0:T(8,128)(2,1)} fusion(bf16[5,128,128,128]{3,2,1,0:T(8,128)(2,1)} %fusion.7, bf16[128,128,127]{2,1,0:T(8,128)(2,1)S(1)} %get-tuple-element.10, bf16[128,128,1]{2,1,0:T(8,128)(2,1)S(1)} %get-tuple-element.12), kind=kLoop, calls=%fused_computation.18 | loop fusion | flops 8388608 | bytes 8388608
  68.3 3.7 %fusion.9 = bf16[5,128,128,128]{3,2,1,0:T(8,128)(2,1)} fusion(bf16[5,128,128,128]{3,2,1,0:T(8,128)(2,1)} %fusion.8, bf16[128,128,1]{2,1,0:T(8,128)(2,1)S(1)} %get-tuple-element.11, bf16[128,128,127]{2,1,0:T(8,128)(2,1)S(1)} %get-tuple-element.9), kind=kLoop, calls=%fused_computation.20 | loop fusion | flops 8388608 | bytes 8388608 | tf_op jit(solution)/shard_map/stack | solution.py:45
  72.5 61.2 %all-to-all-done.2 = bf16[8,16,16384]{2,1,0:T(8,128)(2,1)} async-done(((bf16[8,16,16384]{2,1,0:T(8,128)(2,1)}), bf16[8,16,16384]{2,1,0:T(8,128)(2,1)}, u32[]{:S(2)}, u32[]{:S(2)}) %all-to-all-start.2) | async-done | bytes 4194336 | tf_op jit(solution)/shard_map/all_to_all | solution.py:49
  133.7 28.6 %select_reduce_fusion = (f32[128]{0:T(128)S(1)}, f32[128,640]{1,0:T(8,128)S(1)}) fusion(pred[128,640]{1,0:T(32,128)(4,1)S(1)} %copy.23, f32[640]{0:T(1024)S(1)} %broadcast_bitcast_fusion, bf16[128,16384]{1,0:T(8,128)(2,1)} %bitcast.6, bf16[80,8,128,128]{3,2,1,0:T(8,128)(2,1)} %bitcast.81, f32[128]{0:T(128)S(1)} %reshape.224), kind=kOutput, calls=%fused_computation.29 | convolution fusion | flops 2684682240 | bytes 25579008 | tf_op jit(solution)/shard_map/dot_general | solution.py:56
  162.3 2.5 pmax.7
  165.0 24.6 %fusion = f32[128,16384]{1,0:T(8,128)} fusion(bf16[128,640]{1,0:T(8,128)(2,1)S(1)} %get-tuple-element.8, bf16[80,8,128,128]{3,2,1,0:T(8,128)(2,1)} %bitcast.82), kind=kOutput, calls=%fused_computation.5 | convolution fusion | flops 2684354560 | bytes 29523968 | tf_op jit(solution)/shard_map/dot_general | solution.py:69
  190.8 2.4 all-reduce
  194.6 3.6 %all-to-all-start.3 = ((f32[8,1,16]{2,1,0:T(1,128)}), f32[8,1,16]{2,1,0:T(1,128)S(1)}, u32[]{:S(2)}, u32[]{:S(2)}) async-start(f32[8,1,16]{2,1,0:T(1,128)} %bitcast.13), calls=%async_computation.3 | async-start | bytes 8192 | tf_op jit(solution)/shard_map/all_to_all | solution.py:83
  198.8 6.8 %reduce-scatter.2.cloned.1.call-done = f32[128,8192]{1,0:T(8,128)} async-done(((f32[128,16384]{1,0:T(8,128)}), f32[128,8192]{1,0:T(8,128)}) %reduce-scatter.2.cloned.1.call-update) | async-done | bytes 4194320 | tf_op jit(solution)/shard_map/reduce_scatter | solution.py:71
  205.6 4.6 %broadcast_divide_fusion = f32[128,8192]{1,0:T(8,128)} fusion(f32[128,8192]{1,0:T(8,128)} %reduce-scatter.2.cloned.1.call-done, f32[128]{0:T(128)S(1)} %fusion.22), kind=kLoop, calls=%fused_computation.23 | loop fusion | flops 1048576 | bytes 8389120 | tf_op jit(solution)/shard_map/div | solution.py:74
  210.2 6.3 %all-to-all-start.4 = ((f32[8,16,8192]{2,1,0:T(8,128)}), f32[8,16,8192]{2,1,0:T(8,128)}, u32[]{:S(2)}, u32[]{:S(2)}) async-start(f32[8,16,8192]{2,1,0:T(8,128)} %bitcast.80), calls=%async_computation.5 | async-start | bytes 8388608 | tf_op jit(solution)/shard_map/all_to_all | solution.py:76
  219.3 90.9 %all-to-all-done.4 = f32[8,16,8192]{2,1,0:T(8,128)} async-done(((f32[8,16,8192]{2,1,0:T(8,128)}), f32[8,16,8192]{2,1,0:T(8,128)}, u32[]{:S(2)}, u32[]{:S(2)}) %all-to-all-start.4) | async-done | bytes 4194336 | tf_op jit(solution)/shard_map/all_to_all | solution.py:76
  310.1 5.7 %gather_fusion.4 = f32[64,8192]{1,0:T(8,128)} fusion(f32[128,8192]{1,0:T(8,128)} %bitcast.18, s32[1024]{0:T(1024)S(1)} %pad_clamp_fusion), kind=kCustom, calls=%fused_computation.4 | custom fusion | bytes 4194560 | tf_op jit(solution)/shard_map/gather | solution.py:88
  315.8 2.5 reshape.223
  318.3 2.8 multiply_reduce_fusion.1
  321.1 0.9 divide_convert_fusion
  (55 shorter events, 11.0 us)
Async XLA Ops:
  6.5 13.3 %copy-start = (bf16[32,16384]{1,0:T(8,128)(2,1)S(1)}, bf16[32,16384]{1,0:T(8,128)(2,1)}, u32[]{:S(2)}) copy-start(bf16[32,16384]{1,0:T(8,128)(2,1)} %param.5) | copy-start | bytes 3145732
  10.4 14.5 %all-to-all-start.1 = ((bf16[8,1,16]{2,1,0:T(2,128)(2,1)}), bf16[8,1,16]{2,1,0:T(2,128)(2,1)S(1)}, u32[]{:S(2)}, u32[]{:S(2)}) async-start(bf16[8,1,16]{2,1,0:T(2,128)(2,1)} %select_n.91), calls=%async_computation.1 | async-start | bytes 8192 | tf_op jit(solution)/shard_map/all_to_all | solution.py:50
  24.9 12.7 %all-to-all-start = ((bf16[8,16,128]{2,1,0:T(8,128)(2,1)}), bf16[8,16,128]{2,1,0:T(8,128)(2,1)S(1)}, u32[]{:S(2)}, u32[]{:S(2)}) async-start(bf16[8,16,128]{2,1,0:T(8,128)(2,1)} %select_convert_fusion), calls=%async_computation | async-start | bytes 65536 | tf_op jit(solution)/shard_map/all_to_all | solution.py:51
  37.6 96.1 %all-to-all-start.2 = ((bf16[8,16,16384]{2,1,0:T(8,128)(2,1)}), bf16[8,16,16384]{2,1,0:T(8,128)(2,1)}, u32[]{:S(2)}, u32[]{:S(2)}) async-start(bf16[8,16,16384]{2,1,0:T(8,128)(2,1)} %broadcast_select_fusion), calls=%async_computation.2 | async-start | bytes 8388608 | tf_op jit(solution)/shard_map/all_to_all | solution.py:49
  42.2 163.4 %reduce-scatter.2.cloned.1.call-start = ((), (), s32[]{:S(2)}) async-start(), calls=%async_computation.6 | async-start | bytes 12582912 | tf_op jit(solution)/shard_map/reduce_scatter | solution.py:71
  46.2 3.7 %copy-start.2 = (bf16[1,128,16384]{2,1,0:T(8,128)(2,1)S(1)}, bf16[1,128,16384]{2,1,0:T(8,128)(2,1)}, u32[]{:S(2)}) copy-start(bf16[1,128,16384]{2,1,0:T(8,128)(2,1)} %param.9) | copy-start | bytes 12582916
  189.6 0.7 copy-start.4
  194.6 15.7 %all-to-all-start.3 = ((f32[8,1,16]{2,1,0:T(1,128)}), f32[8,1,16]{2,1,0:T(1,128)S(1)}, u32[]{:S(2)}, u32[]{:S(2)}) async-start(f32[8,1,16]{2,1,0:T(1,128)} %bitcast.13), calls=%async_computation.3 | async-start | bytes 8192 | tf_op jit(solution)/shard_map/all_to_all | solution.py:83
  210.2 6.3 %copy-start.3 = (s32[32,2]{0,1:T(2,128)S(1)}, s32[32,2]{0,1:T(2,128)}, u32[]{:S(2)}) copy-start(s32[32,2]{0,1:T(2,128)} %param.7) | copy-start | bytes 772
  210.2 99.9 %all-to-all-start.4 = ((f32[8,16,8192]{2,1,0:T(8,128)}), f32[8,16,8192]{2,1,0:T(8,128)}, u32[]{:S(2)}, u32[]{:S(2)}) async-start(f32[8,16,8192]{2,1,0:T(8,128)} %bitcast.80), calls=%async_computation.5 | async-start | bytes 8388608 | tf_op jit(solution)/shard_map/all_to_all | solution.py:76
  310.1 11.9 %copy-start.1 = (bf16[32,16384]{1,0:T(8,128)(2,1)S(1)}, bf16[32,16384]{1,0:T(8,128)(2,1)}, u32[]{:S(2)}) copy-start(bf16[32,16384]{1,0:T(8,128)(2,1)} %param.5) | copy-start | bytes 3145732
Sparse Core Ops, SparseCore 0:
  189.7 15.8 reduce-scatter.1
where the time goes:
time: 333 us; the launch traced here: 329 us
  waiting for transfers between devices  161 us (48%)
  matrix products  53.2 us (16%)
  local copies, waits for them, and re-layouts  35.9 us (11%)
  other arithmetic  31.8 us (10%)
  starting transfers between devices  28.4 us (9%)
  between operations  13.9 us (4%)
  blocking collectives  4.91 us (1%)
    all_to_all x1, waiting for transfers between devices, on_device(): lax.all_to_all(unit_image.reshape(lead_count, item_count, -1), 'cls', spl...  90.9 us
    all_to_all x1, waiting for transfers between devices, on_device(): lax.all_to_all(send_images, 'cls', split_axis=0, concat_axis=0, tiled=True)  61.2 us
    dot_general x1, matrix products, on_device(): lax.dot_general(flat_images, shifted, (((1,), (1,)), ((), ())), preferred...  28.6 us
    dot_general x1, matrix products, on_device(): summed = jnp.dot(weights, shifted, preferred_element_type=jnp.float32)  24.6 us
    unnamed x3, other arithmetic  10.6 us
    unnamed x14, local copies, waits for them, and re-layouts  9.19 us
    all_to_all x1, starting transfers between devices, on_device(): lax.all_to_all(send_tau, 'cls', split_axis=0, concat_axis=0, tiled=True)  7.25 us
    slice x4, local copies, waits for them, and re-layouts, on_device(): jnp.roll(grid_rows, offset, axis=(1, 2))  6.88 us
  transfers between devices with their start and end apart: 6, of which 4 were waited for; matrix products, arithmetic and copies ran while one was open for 15% of the time, Pallas kernels for 0%

commit v1 on v0

v1 whole, which is shorter than its diff:
```python
import functools

import jax
import jax.numpy as jnp
from jax import lax
from jax.experimental import pallas as pl
from jax.experimental.pallas import tpu as pltpu
from jax.sharding import Mesh
from jax.sharding import PartitionSpec as P

BOX = 128
LANES = 128
NEG = -1e30
shift_count = 5
VMEM_LIMIT = 48 * 1024 * 1024


def split3(value):
    high = value.astype(jnp.bfloat16)
    rest = value - high.astype(jnp.float32)
    middle = rest.astype(jnp.bfloat16)
    low = (rest - middle.astype(jnp.float32)).astype(jnp.bfloat16)
    return high, middle, low


def put_log(value, rows):
    high, middle, low = split3(value)
    lane = lax.broadcasted_iota(jnp.int32, (rows, LANES), 1)
    pieces = jnp.where(
        lane == 0,
        high.astype(jnp.float32),
        jnp.where(
            lane == 1,
            middle.astype(jnp.float32),
            jnp.where(lane == 2, low.astype(jnp.float32), 0.0),
        ),
    )
    return pieces.astype(jnp.bfloat16)


def get_log(pieces):
    wide = pieces.astype(jnp.float32)
    return (wide[:, 0:1] + wide[:, 1:2]) + wide[:, 2:3]


def column_to_row(column, count):
    eye = lax.broadcasted_iota(jnp.int32, (count, count), 0) == lax.broadcasted_iota(
        jnp.int32, (count, count), 1
    )
    return jnp.sum(jnp.where(eye, column, 0.0), axis=0, keepdims=True)


def roll_lanes(block, amount):
    pieces = [
        pltpu.roll(block[:, start : start + LANES], amount % LANES, 1)
        for start in range(0, block.shape[1], LANES)
    ]
    return jnp.concatenate(pieces, axis=1)


def pack_kernel(base_ref, meta_ref, x_ref, out_ref, choice_ref, choice_scr, *, classes, cap, choose):
    @pl.when(pl.program_id(0) == 0)
    def _():
        rows = meta_ref.shape[0]
        slots = classes * cap
        meta = meta_ref[...].astype(jnp.float32)
        base = base_ref[0]
        ids = (lax.broadcasted_iota(jnp.int32, (rows, classes), 1) + base).astype(jnp.float32)
        named = jnp.zeros((rows, classes), jnp.float32)
        for j in range(choose):
            named = jnp.where(meta[:, 1 + j : 2 + j] == ids, 1.0, named)
        earlier = (
            lax.broadcasted_iota(jnp.int32, (rows, rows), 0)
            > lax.broadcasted_iota(jnp.int32, (rows, rows), 1)
        ).astype(jnp.float32)
        rank = jnp.dot(earlier, named, preferred_element_type=jnp.float32)
        slot = lax.broadcasted_iota(jnp.int32, (classes, slots), 1)
        first = lax.broadcasted_iota(jnp.int32, (classes, slots), 0) * cap
        spread = ((slot >= first) & (slot < first + cap)).astype(jnp.float32)
        rank_at = jnp.dot(rank, spread, preferred_element_type=jnp.float32)
        named_at = jnp.dot(named, spread, preferred_element_type=jnp.float32)
        place = (lax.broadcasted_iota(jnp.int32, (rows, slots), 1) % cap).astype(jnp.float32)
        choice = jnp.where((named_at > 0.5) & (rank_at == place), 1.0, 0.0)
        choice_scr[...] = choice
        choice_ref[...] = choice

    out_ref[...] = lax.dot_general(
        choice_scr[...].astype(jnp.bfloat16),
        x_ref[...],
        (((0,), (0,)), ((), ())),
        preferred_element_type=jnp.float32,
    ).astype(jnp.bfloat16)


def pack(base, payload, classes, cap, choose):
    rows, width = payload.shape
    slots = classes * cap
    tile = 1408
    return pl.pallas_call(
        functools.partial(pack_kernel, classes=classes, cap=cap, choose=choose),
        grid_spec=pltpu.PrefetchScalarGridSpec(
            num_scalar_prefetch=1,
            grid=(width // tile,),
            in_specs=[
                pl.BlockSpec((rows, LANES), lambda i, b: (0, width // LANES - 1)),
                pl.BlockSpec((rows, tile), lambda i, b: (0, i)),
            ],
            out_specs=[
                pl.BlockSpec((slots, tile), lambda i, b: (0, i)),
                pl.BlockSpec((rows, slots), lambda i, b: (0, 0)),
            ],
            scratch_shapes=[pltpu.VMEM((rows, slots), jnp.float32)],
        ),
        out_shape=[
            jax.ShapeDtypeStruct((slots, width), jnp.bfloat16),
            jax.ShapeDtypeStruct((rows, slots), jnp.float32),
        ],
        compiler_params=pltpu.CompilerParams(vmem_limit_bytes=VMEM_LIMIT),
        name="pack",
    )(base, payload, payload)


def norm_kernel(own_ref, other_ref, out_ref, acc):
    step = pl.program_id(0)

    @pl.when(step == 0)
    def _():
        acc[...] = jnp.zeros_like(acc)

    both = jnp.concatenate([own_ref[...], other_ref[...]], axis=0).astype(jnp.float32)
    square = both * both
    total = square[:, 0:LANES]
    for start in range(LANES, square.shape[1], LANES):
        total = total + square[:, start : start + LANES]
    acc[...] += total

    @pl.when(step == pl.num_programs(0) - 1)
    def _():
        out_ref[...] = column_to_row(jnp.sum(acc[...], axis=1, keepdims=True), acc.shape[0])


def half_norms(own, other, pixels):
    count = own.shape[0]
    tile = 1024
    window = pl.BlockSpec((pl.Element(count), pl.Element(tile)), lambda k: (0, (k * (tile // LANES) + 1) * LANES))
    return pl.pallas_call(
        norm_kernel,
        grid=(pixels // tile,),
        in_specs=[window, window],
        out_specs=pl.BlockSpec((1, 2 * count), lambda k: (0, 0)),
        out_shape=jax.ShapeDtypeStruct((1, 2 * count), jnp.float32),
        scratch_shapes=[pltpu.VMEM((2 * count, LANES), jnp.float32)],
        compiler_params=pltpu.CompilerParams(vmem_limit_bytes=VMEM_LIMIT),
        name="half_norms",
    )(own, other)


def score_kernel(x_ref, keep_ref, own_ref, other_ref, norm_ref, out_ref):
    step = pl.program_id(0)
    rows, tile = x_ref.shape
    count = own_ref.shape[0]

    @pl.when(step == 0)
    def _():
        out_ref[...] = jnp.zeros_like(out_ref)

    image = x_ref[...]
    wide = image.astype(jnp.float32)
    left = roll_lanes(wide, -1).astype(jnp.bfloat16)
    right = roll_lanes(wide, 1).astype(jnp.bfloat16)
    both = jnp.concatenate([own_ref[...], other_ref[...]], axis=0)
    dims = (((1,), (1,)), ((), ()))

    def product(lhs, start):
        return lax.dot_general(
            lhs, both[:, start : start + tile], dims, preferred_element_type=jnp.float32
        )

    stacked = product(jnp.concatenate([image, left, right], axis=0), LANES)
    span = 2 * count
    out_ref[:, 0:span] += stacked[0:rows]
    out_ref[:, span : 2 * span] += product(image, 0)
    out_ref[:, 2 * span : 3 * span] += product(image, 2 * LANES)
    out_ref[:, 3 * span : 4 * span] += stacked[rows : 2 * rows]
    out_ref[:, 4 * span : 5 * span] += stacked[2 * rows : 3 * rows]

    @pl.when(step == pl.num_programs(0) - 1)
    def _():
        barred = jnp.where(keep_ref[...].astype(jnp.float32) > 0.5, 0.0, NEG)
        offset = jnp.concatenate([barred, jnp.zeros_like(barred)], axis=1) - 0.5 * norm_ref[...]
        for index in range(shift_count):
            out_ref[:, index * span : (index + 1) * span] += offset


def half_scores(records, own, other, norms, pixels):
    rows, width = records.shape
    count = own.shape[0]
    tile = 1024
    window = pl.BlockSpec((pl.Element(count), pl.Element(tile + 2 * LANES)), lambda k: (0, k * tile))
    return pl.pallas_call(
        score_kernel,
        grid=(pixels // tile,),
        in_specs=[
            pl.BlockSpec((rows, tile), lambda k: (0, k)),
            pl.BlockSpec((rows, count), lambda k: (0, pixels // count)),
            window,
            window,
            pl.BlockSpec((1, 2 * count), lambda k: (0, 0)),
        ],
        out_specs=pl.BlockSpec((rows, 2 * shift_count * count), lambda k: (0, 0)),
        out_shape=jax.ShapeDtypeStruct((rows, 2 * shift_count * count), jnp.float32),
        compiler_params=pltpu.CompilerParams(vmem_limit_bytes=VMEM_LIMIT),
        name="half_scores",
    )(records, records, own, other, norms)


def mean_kernel(mine_ref, theirs_ref, meta_ref, own_ref, other_ref, out_ref, weight_scr, inv_scr, log_scr):
    step = pl.program_id(0)
    rows, tile = out_ref.shape
    count = own_ref.shape[0]
    span = 2 * count

    @pl.when(step == 0)
    def _():
        tau = meta_ref[:, 0:1].astype(jnp.float32)
        scores = []
        peak = jnp.full((rows, 1), NEG, jnp.float32)
        for index in range(shift_count):
            mine = mine_ref[:, index * span : (index + 1) * span]
            theirs = theirs_ref[:, index * span : (index + 1) * span]
            swapped = jnp.concatenate([theirs[:, count:], theirs[:, :count]], axis=1)
            full = mine + swapped
            score = jnp.where(full > -1e29, tau * full, NEG)
            scores.append(score)
            peak = jnp.maximum(peak, jnp.max(score, axis=1, keepdims=True))
        total = jnp.zeros((rows, 1), jnp.float32)
        for index, place in enumerate((0, 3, 4, 1, 2)):
            score = scores[index]
            weight = jnp.where(score > -1e28, jnp.exp(score - peak), 0.0).astype(jnp.bfloat16)
            total = total + jnp.sum(weight.astype(jnp.float32), axis=1, keepdims=True)
            weight_scr[place * rows : (place + 1) * rows, :] = weight
        filled = total > 0
        safe = jnp.where(filled, total, 1.0)
        inv_scr[...] = jnp.broadcast_to(1.0 / safe, inv_scr.shape)
        log_scr[...] = put_log(jnp.where(filled, peak + jnp.log(safe), NEG), rows)

    both = jnp.concatenate([own_ref[...], other_ref[...]], axis=0)

    def product(lhs, start):
        return jnp.dot(lhs, both[:, start : start + tile], preferred_element_type=jnp.float32)

    stacked = product(weight_scr[0 : 3 * rows, :], LANES)
    mean = stacked[0:rows]
    mean = mean + product(weight_scr[3 * rows : 4 * rows, :], 0)
    mean = mean + product(weight_scr[4 * rows : 5 * rows, :], 2 * LANES)
    mean = mean + roll_lanes(stacked[rows : 2 * rows], 1)
    mean = mean + roll_lanes(stacked[2 * rows : 3 * rows], -1)
    out_ref[...] = (mean * inv_scr[:, 0:1]).astype(jnp.bfloat16)

    @pl.when(step == pl.num_programs(0) - 1)
    def _():
        out_ref[:, tile - LANES :] = log_scr[...]


def weighted_means(mine, theirs, records, own, other, pixels):
    rows, width = records.shape
    count = own.shape[0]
    out_width = pixels + LANES
    tile = 13 * LANES
    window = pl.BlockSpec((pl.Element(count), pl.Element(tile + 2 * LANES)), lambda k: (0, k * tile))
    whole = pl.BlockSpec(mine.shape, lambda k: (0, 0))
    return pl.pallas_call(
        mean_kernel,
        grid=(out_width // tile,),
        in_specs=[
            whole,
            whole,
            pl.BlockSpec((rows, LANES), lambda k: (0, width // LANES - 1)),
            window,
            window,
        ],
        out_specs=pl.BlockSpec((rows, tile), lambda k: (0, k)),
        out_shape=jax.ShapeDtypeStruct((rows, out_width), jnp.bfloat16),
        scratch_shapes=[
            pltpu.VMEM((shift_count * rows, 2 * count), jnp.bfloat16),
            pltpu.VMEM((rows, LANES), jnp.float32),
            pltpu.VMEM((rows, LANES), jnp.bfloat16),
        ],
        compiler_params=pltpu.CompilerParams(vmem_limit_bytes=VMEM_LIMIT),
        name="weighted_means",
    )(mine, theirs, records, own, other)


def mix_kernel(*refs, dense, logs):
    if dense:
        choice_ref, back_log_ref, back_ref, part_log_ref, part_ref, out_ref, mix_scr, log_scr = refs
    else:
        choice_ref, back_log_ref, back_ref, out_ref, mix_scr, log_scr = refs
    step = pl.program_id(0)
    rows, slots = choice_ref.shape

    @pl.when(step == 0)
    def _():
        chosen = choice_ref[...] > 0.5
        row = column_to_row(get_log(back_log_ref[...]), slots)
        value = jnp.where(chosen, row, NEG)
        best = jnp.max(value, axis=1, keepdims=True)
        if dense:
            part = get_log(part_log_ref[...])
            best = jnp.maximum(best, part)
        factor = jnp.where(chosen, jnp.exp(value - best), 0.0)
        total = jnp.sum(factor, axis=1, keepdims=True)
        if dense:
            part_factor = jnp.where(part > -1e29, jnp.exp(part - best), 0.0)
            total = total + part_factor
            eye = lax.broadcasted_iota(jnp.int32, (rows, rows), 0) == lax.broadcasted_iota(
                jnp.int32, (rows, rows), 1
            )
            factor = jnp.concatenate([factor, jnp.where(eye, part_factor, 0.0)], axis=1)
        filled = total > 0
        safe = jnp.where(filled, total, 1.0)
        high, middle, low = split3(factor / safe)
        mix_scr[0:rows, :] = high
        mix_scr[rows : 2 * rows, :] = middle
        mix_scr[2 * rows : 3 * rows, :] = low
        log_scr[...] = put_log(jnp.where(filled, best + jnp.log(safe), NEG), rows)

    images = back_ref[...]
    if dense:
        images = jnp.concatenate([images, part_ref[...]], axis=0)
    mixed = jnp.dot(mix_scr[...], images, preferred_element_type=jnp.float32)
    mixed = mixed[0:rows] + (mixed[rows : 2 * rows] + mixed[2 * rows : 3 * rows])
    out_ref[...] = mixed.astype(jnp.bfloat16)
    if logs:

        @pl.when(step == pl.num_programs(0) - 1)
        def _():
            out_ref[:, out_ref.shape[1] - LANES :] = log_scr[...]


def mix(choice, back, part, pixels):
    rows, slots = choice.shape
    width = back.shape[1]
    dense = part is not None
    logs = not dense
    out_width = pixels + LANES if logs else pixels
    tile = 13 * LANES if logs else 16 * LANES
    last = width // LANES - 1
    in_specs = [
        pl.BlockSpec((rows, slots), lambda k: (0, 0)),
        pl.BlockSpec((slots, LANES), lambda k: (0, last)),
        pl.BlockSpec((slots, tile), lambda k: (0, k)),
    ]
    args = [choice, back, back]
    if dense:
        in_specs += [
            pl.BlockSpec((rows, LANES), lambda k: (0, last)),
            pl.BlockSpec((rows, tile), lambda k: (0, k)),
        ]
        args += [part, part]
    terms = slots + (rows if dense else 0)
    return pl.pallas_call(
        functools.partial(mix_kernel, dense=dense, logs=logs),
        grid=(out_width // tile,),
        in_specs=in_specs,
        out_specs=pl.BlockSpec((rows, tile), lambda k: (0, k)),
        out_shape=jax.ShapeDtypeStruct((rows, out_width), jnp.bfloat16),
        scratch_shapes=[
            pltpu.VMEM((3 * rows, terms), jnp.bfloat16),
            pltpu.VMEM((rows, LANES), jnp.bfloat16),
        ],
        compiler_params=pltpu.CompilerParams(vmem_limit_bytes=VMEM_LIMIT),
        name="mix_final" if dense else "mix_half",
    )(*args)


def trade(block, peers):
    cap = block.shape[0] // peers
    if peers > 4:
        parts = block.reshape(peers, cap, block.shape[1])
        parts = lax.all_to_all(parts, "lo", split_axis=0, concat_axis=0, tiled=True)
        return parts.reshape(block.shape)
    own = lax.axis_index("lo")
    got = [lax.dynamic_slice_in_dim(block, own * cap, cap, axis=0)]
    for flip in range(1, peers):
        piece = lax.dynamic_slice_in_dim(block, (own ^ flip) * cap, cap, axis=0)
        got.append(lax.ppermute(piece, "lo", [(i, i ^ flip) for i in range(peers)]))
    return jnp.concatenate(got, axis=0)


def restore(block, peers):
    cap = block.shape[0] // peers
    if peers > 4:
        parts = block.reshape(peers, cap, block.shape[1])
        parts = lax.all_to_all(parts, "lo", split_axis=0, concat_axis=0, tiled=True)
        return parts.reshape(block.shape)
    own = lax.axis_index("lo")
    got = [block[:cap]]
    for flip in range(1, peers):
        piece = block[flip * cap : (flip + 1) * cap]
        got.append(lax.ppermute(piece, "lo", [(i, i ^ flip) for i in range(peers)]))
    out = jnp.zeros_like(block)
    for flip in range(peers):
        out = lax.dynamic_update_slice_in_dim(out, got[flip], (own ^ flip) * cap, axis=0)
    return out


def on_device(particles, tau, candidates, prune, projections):
    halves = lax.axis_size("hi")
    peers = lax.axis_size("lo")
    cores = lax.axis_size("ori")
    core = lax.axis_index("ori")
    part_rows, choose = candidates.shape
    pixels = particles.shape[1] // cores
    count = prune.shape[1]
    cap = 2 * part_rows * choose // (halves * peers)
    base = (lax.axis_index("hi") * peers).astype(jnp.int32).reshape(1)
    across = [(i, (i + 1) % halves) for i in range(halves)]
    swap = [(i, (i + 1) % cores) for i in range(cores)]

    image_part = lax.dynamic_slice_in_dim(particles, core * pixels, pixels, axis=1)
    meta = jnp.concatenate([tau[:, None], candidates.astype(jnp.bfloat16)], axis=1)
    meta = jnp.pad(meta, ((0, 0), (0, LANES - meta.shape[1])))
    payload = jnp.concatenate([image_part, prune.astype(jnp.bfloat16), meta], axis=1)
    far_payload = lax.ppermute(payload, "hi", across)

    sent_near, choice_near = pack(base, payload, peers, cap, choose)
    records_near = trade(sent_near, peers)

    views = projections[0]
    wide = jnp.concatenate([views[:, -BOX:], views, views[:, : 2 * BOX]], axis=1)
    length = pixels + 3 * BOX
    own_views = lax.dynamic_slice_in_dim(wide, core * pixels, length, axis=1)
    lent_views = lax.dynamic_slice_in_dim(wide, (1 - core) * pixels, length, axis=1)
    other_views = lax.ppermute(lent_views, "ori", swap)
    norms = half_norms(own_views, other_views, pixels)

    def answer(records):
        mine = half_scores(records, own_views, other_views, norms, pixels)
        theirs = lax.ppermute(mine, "ori", swap)
        return weighted_means(mine, theirs, records, own_views, other_views, pixels)

    back_near = restore(answer(records_near), peers)

    sent_far, choice_far = pack(base, far_payload, peers, cap, choose)
    records_far = trade(sent_far, peers)
    back_far = restore(answer(records_far), peers)
    far_mix = mix(choice_far, back_far, None, pixels)
    part_mix = lax.ppermute(far_mix, "hi", across)
    return mix(choice_near, back_near, part_mix, pixels)


def solution(mesh):
    grp, cls, ori = (mesh.shape[name] for name in ("grp", "cls", "ori"))
    inner = Mesh(mesh.devices.reshape(grp, 2, cls // 2, ori), ("grp", "hi", "lo", "ori"))
    rows = ("grp", "hi", "lo")
    placed = (
        P(rows, None),
        P(rows),
        P(rows, None),
        P(rows, "ori"),
        P(("hi", "lo"), "ori", None),
    )
    return jax.shard_map(
        on_device, mesh=inner, in_specs=placed, out_specs=P(rows, "ori"), check_vma=False
    )
```

time: 333 us -> 143 us (0.43)
  waiting for transfers between devices: 161 us -> 63.5 us
  matrix products: 53.2 us -> 0 us
  Pallas kernels: 0 us -> 43.3 us
  local copies, waits for them, and re-layouts: 35.9 us -> 7.36 us
  other arithmetic: 31.8 us -> 6.88 us
  between operations: 13.9 us -> 0.22 us
  starting transfers between devices: 28.4 us -> 20.5 us
  blocking collectives: 4.91 us -> 0 us
    all_to_all x5 -> x0, waiting for transfers between devices: 154 us -> none  [the longest x1 90.9 us: on_device(): lax.all_to_all(unit_image.reshape(lead_count, item_count, -1), 'cls', spl...]
    ppermute x0 -> x17, waiting for transfers between devices: none -> 63.5 us  [the longest x1 22.5 us: on_device(): part_mix = lax.ppermute(far_mix, 'hi', across)]
    dot_general x2 -> x0, matrix products: 53.2 us -> none  [the longest x1 28.6 us: on_device(): lax.dot_general(flat_images, shifted, (((1,), (1,)), ((), ())), preferred...]
    pallas_call x0 -> x9, Pallas kernels: none -> 43.3 us  [the longest x2 15 us: half_scores(): pl.pallas_call(score_kernel, grid=(pixels // tile,), in_specs=[pl.BlockSp...]
    all_to_all x5 -> x0, starting transfers between devices: 27.8 us -> none  [the longest x1 7.25 us: on_device(): lax.all_to_all(send_tau, 'cls', split_axis=0, concat_axis=0, tiled=True)]
    ppermute x0 -> x17, starting transfers between devices: none -> 20.5 us  [the longest x6 7.11 us: restore(): got.append(lax.ppermute(piece, 'lo', [(i, i ^ flip) for i in range(peers)]))]
    gather x5 -> x0, local copies, waits for them, and re-layouts: 14.5 us -> none  [the longest x1 5.66 us: on_device(): record_unit = flat_unit[slot_of].reshape(part_rows, choose_count, -1)]
    unnamed x3 -> x0, other arithmetic: 10.6 us -> none
  transfers between devices with their start and end apart: 6 -> 17, of which waited for: 4 -> 6; matrix products, arithmetic and copies ran while one was open for 15% -> 7% of each run, Pallas kernels for 0% -> 28%
where the time goes in v1:
time: 143 us; the launch traced here: 142 us
  waiting for transfers between devices  63.5 us (44%)
  Pallas kernels  43.3 us (30%)
  starting transfers between devices  20.5 us (14%)
  local copies, waits for them, and re-layouts  7.36 us (5%)
  other arithmetic  6.88 us (5%)
    ppermute x1, waiting for transfers between devices, on_device(): part_mix = lax.ppermute(far_mix, 'hi', across)  22.5 us
    ppermute x6, waiting for transfers between devices, restore(): got.append(lax.ppermute(piece, 'lo', [(i, i ^ flip) for i in range(peers)]))  20.9 us
    pallas_call x2, Pallas kernels, half_scores(): pl.pallas_call(score_kernel, grid=(pixels // tile,), in_specs=[pl.BlockSp...  15 us
    pallas_call x2, Pallas kernels, weighted_means(): pl.pallas_call(mean_kernel, grid=(out_width // tile,), in_specs=[whole, w...  11 us
    ppermute x6, waiting for transfers between devices, trade(): got.append(lax.ppermute(piece, 'lo', [(i, i ^ flip) for i in range(peers)]))  10.3 us
    ppermute x1, waiting for transfers between devices, on_device(): far_payload = lax.ppermute(payload, 'hi', across)  9.81 us
    pallas_call x2, Pallas kernels, pack(): pl.pallas_call(functools.partial(pack_kernel, classes=classes, cap=cap, c...  8.08 us
    ppermute x6, starting transfers between devices, restore(): got.append(lax.ppermute(piece, 'lo', [(i, i ^ flip) for i in range(peers)]))  7.11 us
  transfers between devices with their start and end apart: 17, of which 6 were waited for; matrix products, arithmetic and copies ran while one was open for 7% of the time, Pallas kernels for 28%

profile of v1, /device:TPU:0, one launch (start us, length us, event | category | flops | bytes accessed | tf_op | source)
XLA Modules:
  0.0 141.7 jit_solution(815926241683955924)
XLA Ops:
  0.0 0.8 convert_element_type.9
  0.8 0.7 pad_maximum_fusion.3
  1.5 0.7 convert_element_type.8
  2.3 0.8 fusion.1.meta_ref.x_ref
  3.2 4.0 %collective-permute-start.8 = (bf16[32,8448]{1,0:T(8,128)(2,1)}, bf16[32,8448]{1,0:T(8,128)(2,1)}, u32[]{:S(2)}, u32[]{:S(2)}) collective-permute-start(bf16[32,8448]{1,0:T(8,128)(2,1)} %fusion.1.meta_ref.x_ref), channel_id=1, source_target_pairs={{0,8},{8,0},{1,9},{9,1},{2,10},{10,2},{3,11},{11,3},{4,12},{12,4},... | collective-permute-start | bytes 1622024 | tf_op jit(solution)/shard_map/ppermute | solution.py:425
  7.2 0.8 slice.41
  8.0 0.8 slice.40
  8.8 3.7 %pad_maximum_fusion = bf16[128,16768]{1,0:T(8,128)(2,1)} fusion(bf16[128,256]{1,0:T(8,128)(2,1)S(1)} %slice.41, bf16[128,16384]{1,0:T(8,128)(2,1)} %bitcast.5, bf16[128,128]{1,0:T(8,128)(2,1)S(1)} %slice.40), kind=kLoop, calls=%fused_computation | loop fusion | flops 12877824 | bytes 8585216 | tf_op jit(solution)/shard_map/concatenate | solution.py:431
  12.5 4.0 %constant_dynamic-slice_fusion.4 = (bf16[128,8576]{1,0:T(8,128)(2,1)}, bf16[128,8576]{1,0:T(8,128)(2,1)S(1)}) fusion(bf16[128,16768]{1,0:T(8,128)(2,1)} %pad_maximum_fusion, s32[]{:T(128)S(6)} %select_n.39, s32[]{:T(128)S(6)} %select_n.38), kind=kLoop, calls=%fused_computation.18 | loop fusion | bytes 8781832 | tf_op jit(solution)/shard_map/dynamic_slice | solution.py:434
  16.5 4.0 %pack.2 = (bf16[64,8448]{1,0:T(8,128)(2,1)S(1)}, f32[32,64]{1,0:T(8,128)S(1)}) custom-call(s32[1]{0:T(128)} %bitcast.base_ref, bf16[32,8448]{1,0:T(8,128)(2,1)} %fusion.1.meta_ref.x_ref, bf16[32,8448]{1,0:T(8,128)(2,1)} %fusion.1.meta_ref.x_ref), custom_call_target="tpu_custom_call" | custom-call | tf_op jit(solution)/shard_map/pack/pallas_call | solution.py:99
  20.6 1.0 copy-done.1
  21.6 9.8 %collective-permute-done.8.meta_ref.x_ref = bf16[32,8448]{1,0:T(8,128)(2,1)} collective-permute-done((bf16[32,8448]{1,0:T(8,128)(2,1)}, bf16[32,8448]{1,0:T(8,128)(2,1)}, u32[]{:S(2)}, u32[]{:S(2)}) %collective-permute-start.8) | collective-permute-done | bytes 540704 | tf_op jit(solution)/shard_map/ppermute | solution.py:425
  31.4 4.0 %pack.3 = (bf16[64,8448]{1,0:T(8,128)(2,1)S(1)}, f32[32,64]{1,0:T(8,128)S(1)}) custom-call(s32[1]{0:T(128)} %bitcast.base_ref, bf16[32,8448]{1,0:T(8,128)(2,1)} %collective-permute-done.8.meta_ref.x_ref, bf16[32,8448]{1,0:T(8,128)(2,1)} %collective-permute-done.8.meta_ref.x_ref), custom_call_target="tpu_custom_call" | custom-call | tf_op jit(solution)/shard_map/pack/pallas_call | solution.py:99
  35.5 1.7 %collective-permute-start.11 = (bf16[16,8448]{1,0:T(8,128)(2,1)S(1)}, bf16[16,8448]{1,0:T(8,128)(2,1)S(1)}, u32[]{:S(2)}, u32[]{:S(2)}) collective-permute-start(bf16[16,8448]{1,0:T(8,128)(2,1)S(1)} %get-tuple-element.16), channel_id=1, source_target_pairs={{0,6},{2,4},{4,2},{6,0},{1,7},{3,5},{5,3},{7,1},{8,14},{10,12},{12... | collective-permute-start | bytes 811016 | tf_op jit(solution)/shard_map/ppermute | solution.py:387
  37.2 1.4 collective-permute-start.10
  39.2 1.7 %collective-permute-start.2 = (bf16[16,8448]{1,0:T(8,128)(2,1)S(1)}, bf16[16,8448]{1,0:T(8,128)(2,1)S(1)}, u32[]{:S(2)}, u32[]{:S(2)}) collective-permute-start(bf16[16,8448]{1,0:T(8,128)(2,1)S(1)} %get-tuple-element.20), channel_id=1, source_target_pairs={{0,6},{2,4},{4,2},{6,0},{1,7},{3,5},{5,3},{7,1},{8,14},{10,12},{12... | collective-permute-start | bytes 811016 | tf_op jit(solution)/shard_map/ppermute | solution.py:387
  40.9 5.1 %collective-permute-done.11 = bf16[16,8448]{1,0:T(8,128)(2,1)S(1)} collective-permute-done((bf16[16,8448]{1,0:T(8,128)(2,1)S(1)}, bf16[16,8448]{1,0:T(8,128)(2,1)S(1)}, u32[]{:S(2)}, u32[]{:S(2)}) %collective-permute-start.11) | collective-permute-done | bytes 270368 | tf_op jit(solution)/shard_map/ppermute | solution.py:387
  46.6 5.2 %collective-permute-done.10 = bf16[16,8448]{1,0:T(8,128)(2,1)S(1)} collective-permute-done((bf16[16,8448]{1,0:T(8,128)(2,1)S(1)}, bf16[16,8448]{1,0:T(8,128)(2,1)S(1)}, u32[]{:S(2)}, u32[]{:S(2)}) %collective-permute-start.10) | collective-permute-done | bytes 270368 | tf_op jit(solution)/shard_map/ppermute | solution.py:387
  52.4 4.5 %half_norms.1.norm_ref = f32[1,256]{1,0:T(1,128)S(1)} custom-call(bf16[128,8576]{1,0:T(8,128)(2,1)S(1)} %get-tuple-element.14.own_ref, bf16[128,8576]{1,0:T(8,128)(2,1)} %collective-permute-done.3.other_ref), custom_call_target="tpu_custom_call" | custom-call | tf_op jit(solution)/shard_map/half_norms/pallas_call | solution.py:146
  56.9 7.5 %half_scores.3.mine_ref = f32[64,1280]{1,0:T(8,128)S(1)} custom-call(bf16[64,8448]{1,0:T(8,128)(2,1)S(1)} %pad_maximum_fusion.2.x_ref.keep_ref.meta_ref, bf16[64,8448]{1,0:T(8,128)(2,1)S(1)} %pad_maximum_fusion.2.x_ref.keep_ref.meta_ref, bf16[128,8576]{1,0:T(8,128)(2,1)S(1)} %get-tuple-element.14.own_ref, ...), custom_call_target="tpu_custom_call" | custom-call | tf_op jit(solution)/shard_map/half_scores/pallas_call | solution.py:200
  64.6 7.5 %half_scores.2.mine_ref = f32[64,1280]{1,0:T(8,128)S(1)} custom-call(bf16[64,8448]{1,0:T(8,128)(2,1)S(1)} %pad_maximum_fusion.1.x_ref.keep_ref.meta_ref, bf16[64,8448]{1,0:T(8,128)(2,1)S(1)} %pad_maximum_fusion.1.x_ref.keep_ref.meta_ref, bf16[128,8576]{1,0:T(8,128)(2,1)S(1)} %get-tuple-element.14.own_ref, ...), custom_call_target="tpu_custom_call" | custom-call | tf_op jit(solution)/shard_map/half_scores/pallas_call | solution.py:200
  72.6 5.5 %weighted_means.3 = bf16[64,8320]{1,0:T(8,128)(2,1)S(1)} custom-call(f32[64,1280]{1,0:T(8,128)S(1)} %half_scores.3.mine_ref, f32[64,1280]{1,0:T(8,128)S(1)} %collective-permute-done.12.theirs_ref, bf16[64,8448]{1,0:T(8,128)(2,1)S(1)} %pad_maximum_fusion.2.x_ref.keep_ref.meta_ref, bf16[128,8576]{1,0:T(8,128)(2,1)S(1)} %get-tuple-element.14.own_ref, ...), custom_call_target="tpu_custom_call" | custom-call | tf_op jit(solution)/shard_map/weighted_means/pallas_call | solution.py:272
  78.3 1.6 %collective-permute-start.13 = (bf16[16,8320]{1,0:T(8,128)(2,1)S(1)}, bf16[16,8320]{1,0:T(8,128)(2,1)S(1)}, u32[]{:S(2)}, u32[]{:S(2)}) collective-permute-start(bf16[16,8320]{1,0:T(8,128)(2,1)S(1)} %get-tuple-element.25), channel_id=1, source_target_pairs={{0,2},{2,0},{4,6},{6,4},{1,3},{3,1},{5,7},{7,5},{8,10},{10,8},{12,... | collective-permute-start | bytes 798728 | tf_op jit(solution)/shard_map/ppermute | solution.py:401
  79.9 5.5 %weighted_means.2 = bf16[64,8320]{1,0:T(8,128)(2,1)S(1)} custom-call(f32[64,1280]{1,0:T(8,128)S(1)} %half_scores.2.mine_ref, f32[64,1280]{1,0:T(8,128)S(1)} %collective-permute-done.4.theirs_ref, bf16[64,8448]{1,0:T(8,128)(2,1)S(1)} %pad_maximum_fusion.1.x_ref.keep_ref.meta_ref, bf16[128,8576]{1,0:T(8,128)(2,1)S(1)} %get-tuple-element.14.own_ref, ...), custom_call_target="tpu_custom_call" | custom-call | tf_op jit(solution)/shard_map/weighted_means/pallas_call | solution.py:272
  86.8 2.4 %collective-permute-start.7 = (bf16[16,8320]{1,0:T(8,128)(2,1)S(1)}, bf16[16,8320]{1,0:T(8,128)(2,1)S(1)}, u32[]{:S(2)}, u32[]{:S(2)}) collective-permute-start(bf16[16,8320]{1,0:T(8,128)(2,1)S(1)} %get-tuple-element.27), channel_id=1, source_target_pairs={{0,6},{2,4},{4,2},{6,0},{1,7},{3,5},{5,3},{7,1},{8,14},{10,12},{12... | collective-permute-start | bytes 798728 | tf_op jit(solution)/shard_map/ppermute | solution.py:401
  89.8 1.3 collective-permute-start.15
  91.1 15.8 %collective-permute-done.14 = bf16[16,8320]{1,0:T(8,128)(2,1)S(1)} collective-permute-done((bf16[16,8320]{1,0:T(8,128)(2,1)S(1)}, bf16[16,8320]{1,0:T(8,128)(2,1)S(1)}, u32[]{:S(2)}, u32[]{:S(2)}) %collective-permute-start.14) | collective-permute-done | bytes 266272 | tf_op jit(solution)/shard_map/ppermute | solution.py:401
  106.9 5.1 %collective-permute-done.15 = bf16[16,8320]{1,0:T(8,128)(2,1)S(1)} collective-permute-done((bf16[16,8320]{1,0:T(8,128)(2,1)S(1)}, bf16[16,8320]{1,0:T(8,128)(2,1)S(1)}, u32[]{:S(2)}, u32[]{:S(2)}) %collective-permute-start.15) | collective-permute-done | bytes 266272 | tf_op jit(solution)/shard_map/ppermute | solution.py:401
  112.1 1.8 %mix_half.1 = bf16[32,8320]{1,0:T(8,128)(2,1)S(1)} custom-call(f32[32,64]{1,0:T(8,128)S(1)} %get-tuple-element.11.refs_0_, bf16[64,8320]{1,0:T(8,128)(2,1)S(1)} %constant_dynamic-update-slice_fusion.refs_1_.refs_2_, bf16[64,8320]{1,0:T(8,128)(2,1)S(1)} %constant_dynamic-update-slice_fusion.refs_1_.refs_2_), custom_call_target="tpu_custom_call" | custom-call | tf_op jit(solution)/shard_map/mix_half/pallas_call | solution.py:362
  113.8 2.3 %collective-permute-start.16 = (bf16[32,8320]{1,0:T(8,128)(2,1)S(1)}, bf16[32,8320]{1,0:T(8,128)(2,1)S(1)}, u32[]{:S(2)}, u32[]{:S(2)}) collective-permute-start(bf16[32,8320]{1,0:T(8,128)(2,1)S(1)} %mix_half.1), channel_id=1, source_target_pairs={{0,8},{8,0},{1,9},{9,1},{2,10},{10,2},{3,11},{11,3},{4,12},{12,4},... | collective-permute-start | bytes 1597448 | tf_op jit(solution)/shard_map/ppermute | solution.py:449
  116.3 22.5 %collective-permute-done.16.refs_3_.refs_4_ = bf16[32,8320]{1,0:T(8,128)(2,1)S(1)} collective-permute-done((bf16[32,8320]{1,0:T(8,128)(2,1)S(1)}, bf16[32,8320]{1,0:T(8,128)(2,1)S(1)}, u32[]{:S(2)}, u32[]{:S(2)}) %collective-permute-start.16) | collective-permute-done | bytes 532512 | tf_op jit(solution)/shard_map/ppermute | solution.py:449
  138.8 2.9 %mix_final.1 = bf16[32,8192]{1,0:T(8,128)(2,1)} custom-call(f32[32,64]{1,0:T(8,128)S(1)} %get-tuple-element.9.refs_0_, bf16[64,8320]{1,0:T(8,128)(2,1)S(1)} %constant_dynamic-update-slice_fusion.3.refs_1_.refs_2_, bf16[64,8320]{1,0:T(8,128)(2,1)S(1)} %constant_dynamic-update-slice_fusion.3.refs_1_.refs_2_, ...), custom_call_target="tpu_custom_call" | custom-call | tf_op jit(solution)/shard_map/mix_final/pallas_call | solution.py:362
  (41 shorter events, 5.0 us)
Async XLA Ops:
  0.0 2.3 %copy-start = (bf16[32,16384]{1,0:T(8,128)(2,1)S(1)}, bf16[32,16384]{1,0:T(8,128)(2,1)}, u32[]{:S(2)}) copy-start(bf16[32,16384]{1,0:T(8,128)(2,1)} %param.5) | copy-start | bytes 3145732
  3.2 28.2 %collective-permute-start.8 = (bf16[32,8448]{1,0:T(8,128)(2,1)}, bf16[32,8448]{1,0:T(8,128)(2,1)}, u32[]{:S(2)}, u32[]{:S(2)}) collective-permute-start(bf16[32,8448]{1,0:T(8,128)(2,1)} %fusion.1.meta_ref.x_ref), channel_id=1, source_target_pairs={{0,8},{8,0},{1,9},{9,1},{2,10},{10,2},{3,11},{11,3},{4,12},{12,4},... | collective-permute-start | bytes 1622024 | tf_op jit(solution)/shard_map/ppermute | solution.py:425
  16.5 35.9 %collective-permute-start.3 = (bf16[128,8576]{1,0:T(8,128)(2,1)}, bf16[128,8576]{1,0:T(8,128)(2,1)}, u32[]{:S(2)}, u32[]{:S(2)}) collective-permute-start(bf16[128,8576]{1,0:T(8,128)(2,1)} %get-tuple-element.13), channel_id=1, source_target_pairs={{0,1},{1,0},{2,3},{3,2},{4,5},{5,4},{6,7},{7,6},{8,9},{9,8},{10,11... | collective-permute-start | bytes 6586376 | tf_op jit(solution)/shard_map/ppermute | solution.py:435
  20.6 1.0 copy-start.1
  35.4 3.7 %copy-start.2 = (bf16[64,8448]{1,0:T(8,128)(2,1)S(1)}, bf16[64,8448]{1,0:T(8,128)(2,1)}, u32[]{:S(2)}) copy-start(bf16[64,8448]{1,0:T(8,128)(2,1)} %copy-done.1) | copy-start | bytes 3244036
  35.5 10.4 %collective-permute-start.11 = (bf16[16,8448]{1,0:T(8,128)(2,1)S(1)}, bf16[16,8448]{1,0:T(8,128)(2,1)S(1)}, u32[]{:S(2)}, u32[]{:S(2)}) collective-permute-start(bf16[16,8448]{1,0:T(8,128)(2,1)S(1)} %get-tuple-element.16), channel_id=1, source_target_pairs={{0,6},{2,4},{4,2},{6,0},{1,7},{3,5},{5,3},{7,1},{8,14},{10,12},{12... | collective-permute-start | bytes 811016 | tf_op jit(solution)/shard_map/ppermute | solution.py:387
  37.2 14.6 %collective-permute-start.10 = (bf16[16,8448]{1,0:T(8,128)(2,1)S(1)}, bf16[16,8448]{1,0:T(8,128)(2,1)S(1)}, u32[]{:S(2)}, u32[]{:S(2)}) collective-permute-start(bf16[16,8448]{1,0:T(8,128)(2,1)S(1)} %get-tuple-element.17), channel_id=1, source_target_pairs={{0,4},{2,6},{4,0},{6,2},{1,5},{3,7},{5,1},{7,3},{8,12},{10,14},{12... | collective-permute-start | bytes 811016 | tf_op jit(solution)/shard_map/ppermute | solution.py:387
  38.6 13.7 %collective-permute-start.9 = (bf16[16,8448]{1,0:T(8,128)(2,1)S(1)}, bf16[16,8448]{1,0:T(8,128)(2,1)S(1)}, u32[]{:S(2)}, u32[]{:S(2)}) collective-permute-start(bf16[16,8448]{1,0:T(8,128)(2,1)S(1)} %get-tuple-element.18), channel_id=1, source_target_pairs={{0,2},{2,0},{4,6},{6,4},{1,3},{3,1},{5,7},{7,5},{8,10},{10,8},{12,... | collective-permute-start | bytes 811016 | tf_op jit(solution)/shard_map/ppermute | solution.py:387
  39.2 25.3 %collective-permute-start.2 = (bf16[16,8448]{1,0:T(8,128)(2,1)S(1)}, bf16[16,8448]{1,0:T(8,128)(2,1)S(1)}, u32[]{:S(2)}, u32[]{:S(2)}) collective-permute-start(bf16[16,8448]{1,0:T(8,128)(2,1)S(1)} %get-tuple-element.20), channel_id=1, source_target_pairs={{0,6},{2,4},{4,2},{6,0},{1,7},{3,5},{5,3},{7,1},{8,14},{10,12},{12... | collective-permute-start | bytes 811016 | tf_op jit(solution)/shard_map/ppermute | solution.py:387
  45.9 18.5 %collective-permute-start.1 = (bf16[16,8448]{1,0:T(8,128)(2,1)S(1)}, bf16[16,8448]{1,0:T(8,128)(2,1)S(1)}, u32[]{:S(2)}, u32[]{:S(2)}) collective-permute-start(bf16[16,8448]{1,0:T(8,128)(2,1)S(1)} %get-tuple-element.21), channel_id=1, source_target_pairs={{0,4},{2,6},{4,0},{6,2},{1,5},{3,7},{5,1},{7,3},{8,12},{10,14},{12... | collective-permute-start | bytes 811016 | tf_op jit(solution)/shard_map/ppermute | solution.py:387
  51.8 12.6 %collective-permute-start = (bf16[16,8448]{1,0:T(8,128)(2,1)S(1)}, bf16[16,8448]{1,0:T(8,128)(2,1)S(1)}, u32[]{:S(2)}, u32[]{:S(2)}) collective-permute-start(bf16[16,8448]{1,0:T(8,128)(2,1)S(1)} %get-tuple-element.22), channel_id=1, source_target_pairs={{0,2},{2,0},{4,6},{6,4},{1,3},{3,1},{5,7},{7,5},{8,10},{10,8},{12,... | collective-permute-start | bytes 811016 | tf_op jit(solution)/shard_map/ppermute | solution.py:387
  64.4 8.2 %collective-permute-start.12 = (f32[64,1280]{1,0:T(8,128)S(1)}, f32[64,1280]{1,0:T(8,128)S(1)}, u32[]{:S(2)}, u32[]{:S(2)}) collective-permute-start(f32[64,1280]{1,0:T(8,128)S(1)} %half_scores.3.mine_ref), channel_id=1, source_target_pairs={{0,1},{1,0},{2,3},{3,2},{4,5},{5,4},{6,7},{7,6},{8,9},{9,8},{10,11... | collective-permute-start | bytes 983048 | tf_op jit(solution)/shard_map/ppermute | solution.py:440
  72.0 7.9 %collective-permute-start.4 = (f32[64,1280]{1,0:T(8,128)S(1)}, f32[64,1280]{1,0:T(8,128)S(1)}, u32[]{:S(2)}, u32[]{:S(2)}) collective-permute-start(f32[64,1280]{1,0:T(8,128)S(1)} %half_scores.2.mine_ref), channel_id=1, source_target_pairs={{0,1},{1,0},{2,3},{3,2},{4,5},{5,4},{6,7},{7,6},{8,9},{9,8},{10,11... | collective-permute-start | bytes 983048 | tf_op jit(solution)/shard_map/ppermute | solution.py:440
  78.3 11.5 %collective-permute-start.13 = (bf16[16,8320]{1,0:T(8,128)(2,1)S(1)}, bf16[16,8320]{1,0:T(8,128)(2,1)S(1)}, u32[]{:S(2)}, u32[]{:S(2)}) collective-permute-start(bf16[16,8320]{1,0:T(8,128)(2,1)S(1)} %get-tuple-element.25), channel_id=1, source_target_pairs={{0,2},{2,0},{4,6},{6,4},{1,3},{3,1},{5,7},{7,5},{8,10},{10,8},{12,... | collective-permute-start | bytes 798728 | tf_op jit(solution)/shard_map/ppermute | solution.py:401
  85.6 30.5 %collective-permute-start.5 = (bf16[16,8320]{1,0:T(8,128)(2,1)S(1)}, bf16[16,8320]{1,0:T(8,128)(2,1)S(1)}, u32[]{:S(2)}, u32[]{:S(2)}) collective-permute-start(bf16[16,8320]{1,0:T(8,128)(2,1)S(1)} %get-tuple-element.29), channel_id=1, source_target_pairs={{0,2},{2,0},{4,6},{6,4},{1,3},{3,1},{5,7},{7,5},{8,10},{10,8},{12,... | collective-permute-start | bytes 798728 | tf_op jit(solution)/shard_map/ppermute | solution.py:401
  86.2 30.0 %collective-permute-start.6 = (bf16[16,8320]{1,0:T(8,128)(2,1)S(1)}, bf16[16,8320]{1,0:T(8,128)(2,1)S(1)}, u32[]{:S(2)}, u32[]{:S(2)}) collective-permute-start(bf16[16,8320]{1,0:T(8,128)(2,1)S(1)} %get-tuple-element.28), channel_id=1, source_target_pairs={{0,4},{2,6},{4,0},{6,2},{1,5},{3,7},{5,1},{7,3},{8,12},{10,14},{12... | collective-permute-start | bytes 798728 | tf_op jit(solution)/shard_map/ppermute | solution.py:401
  86.8 29.4 %collective-permute-start.7 = (bf16[16,8320]{1,0:T(8,128)(2,1)S(1)}, bf16[16,8320]{1,0:T(8,128)(2,1)S(1)}, u32[]{:S(2)}, u32[]{:S(2)}) collective-permute-start(bf16[16,8320]{1,0:T(8,128)(2,1)S(1)} %get-tuple-element.27), channel_id=1, source_target_pairs={{0,6},{2,4},{4,2},{6,0},{1,7},{3,5},{5,3},{7,1},{8,14},{10,12},{12... | collective-permute-start | bytes 798728 | tf_op jit(solution)/shard_map/ppermute | solution.py:401
  89.2 17.7 %collective-permute-start.14 = (bf16[16,8320]{1,0:T(8,128)(2,1)S(1)}, bf16[16,8320]{1,0:T(8,128)(2,1)S(1)}, u32[]{:S(2)}, u32[]{:S(2)}) collective-permute-start(bf16[16,8320]{1,0:T(8,128)(2,1)S(1)} %get-tuple-element.24), channel_id=1, source_target_pairs={{0,4},{2,6},{4,0},{6,2},{1,5},{3,7},{5,1},{7,3},{8,12},{10,14},{12... | collective-permute-start | bytes 798728 | tf_op jit(solution)/shard_map/ppermute | solution.py:401
  89.8 22.3 %collective-permute-start.15 = (bf16[16,8320]{1,0:T(8,128)(2,1)S(1)}, bf16[16,8320]{1,0:T(8,128)(2,1)S(1)}, u32[]{:S(2)}, u32[]{:S(2)}) collective-permute-start(bf16[16,8320]{1,0:T(8,128)(2,1)S(1)} %get-tuple-element.23), channel_id=1, source_target_pairs={{0,6},{2,4},{4,2},{6,0},{1,7},{3,5},{5,3},{7,1},{8,14},{10,12},{12... | collective-permute-start | bytes 798728 | tf_op jit(solution)/shard_map/ppermute | solution.py:401
  113.8 24.9 %collective-permute-start.16 = (bf16[32,8320]{1,0:T(8,128)(2,1)S(1)}, bf16[32,8320]{1,0:T(8,128)(2,1)S(1)}, u32[]{:S(2)}, u32[]{:S(2)}) collective-permute-start(bf16[32,8320]{1,0:T(8,128)(2,1)S(1)} %mix_half.1), channel_id=1, source_target_pairs={{0,8},{8,0},{1,9},{9,1},{2,10},{10,2},{3,11},{11,3},{4,12},{12,4},... | collective-permute-start | bytes 1597448 | tf_op jit(solution)/shard_map/ppermute | solution.py:449

commit v2 on v0

v2 whole, which is shorter than its diff:
```python
import functools

import jax
import jax.numpy as jnp
from jax import lax
from jax.experimental import pallas as pl
from jax.experimental.pallas import tpu as pltpu
from jax.sharding import Mesh
from jax.sharding import PartitionSpec as P

BOX = 128
LANES = 128
NEG = -1e30
shift_count = 5
VMEM_LIMIT = 24 * 1024 * 1024
IN_HBM = pl.BlockSpec(memory_space=pltpu.HBM)
IN_VMEM = pl.BlockSpec(memory_space=pltpu.VMEM)


def in_hbm(array):
    return pltpu.with_memory_space_constraint(array, pltpu.HBM)


def joined(refs, start, stop):
    if len(refs) == 1:
        return refs[0][:, start:stop]
    return jnp.concatenate([ref[:, start:stop] for ref in refs], axis=0)


def piece_count(peers):
    return peers if peers <= 4 else 1


def split3(value):
    high = value.astype(jnp.bfloat16)
    rest = value - high.astype(jnp.float32)
    middle = rest.astype(jnp.bfloat16)
    low = (rest - middle.astype(jnp.float32)).astype(jnp.bfloat16)
    return high, middle, low


def put_log(value, rows):
    high, middle, low = split3(value)
    lane = lax.broadcasted_iota(jnp.int32, (rows, LANES), 1)
    pieces = jnp.where(
        lane == 0,
        high.astype(jnp.float32),
        jnp.where(
            lane == 1,
            middle.astype(jnp.float32),
            jnp.where(lane == 2, low.astype(jnp.float32), 0.0),
        ),
    )
    return pieces.astype(jnp.bfloat16)


def get_log(pieces):
    wide = pieces.astype(jnp.float32)
    return (wide[:, 0:1] + wide[:, 1:2]) + wide[:, 2:3]


def column_to_row(column, count):
    eye = lax.broadcasted_iota(jnp.int32, (count, count), 0) == lax.broadcasted_iota(
        jnp.int32, (count, count), 1
    )
    return jnp.sum(jnp.where(eye, column, 0.0), axis=0, keepdims=True)


def roll_lanes(block, amount):
    pieces = [
        pltpu.roll(block[:, start : start + LANES], amount % LANES, 1)
        for start in range(0, block.shape[1], LANES)
    ]
    return jnp.concatenate(pieces, axis=1)


def payload_kernel(
    core_ref, x_ref, tau_ref, classes_ref, keep_ref, out_ref, tau_scr, classes_scr, keep_scr, sems
):
    rows, width = out_ref.shape
    count = keep_scr.shape[1]
    pixels = width - count - LANES
    start = pl.multiple_of(core_ref[0] * pixels, pixels)
    copies = [
        pltpu.make_async_copy(
            x_ref.at[:, pl.ds(start, pixels)], out_ref.at[:, pl.ds(0, pixels)], sems.at[0]
        ),
        pltpu.make_async_copy(tau_ref, tau_scr, sems.at[1]),
        pltpu.make_async_copy(classes_ref, classes_scr, sems.at[2]),
        pltpu.make_async_copy(keep_ref, keep_scr, sems.at[3]),
    ]
    for copy in copies:
        copy.start()
    for copy in copies[1:]:
        copy.wait()
    keep = keep_scr[...].astype(jnp.float32).astype(jnp.bfloat16)
    out_ref[:, pixels : pixels + count] = keep
    eye = lax.broadcasted_iota(jnp.int32, (rows, rows), 0) == lax.broadcasted_iota(
        jnp.int32, (rows, rows), 1
    )
    tau = jnp.sum(
        jnp.where(eye, tau_scr[...].astype(jnp.float32), 0.0), axis=1, keepdims=True
    )
    lane = lax.broadcasted_iota(jnp.int32, (rows, LANES), 1)
    meta = jnp.where(lane == 0, tau, 0.0)
    for j in range(classes_scr.shape[0]):
        named = classes_scr[j : j + 1, :].astype(jnp.float32)
        named = jnp.sum(jnp.where(eye, named, 0.0), axis=1, keepdims=True)
        meta = jnp.where(lane == 1 + j, named, meta)
    out_ref[:, pixels + count :] = meta.astype(jnp.bfloat16)
    copies[0].wait()


def make_payload(core, particles, tau, candidates, prune, pixels):
    rows, choose = candidates.shape
    count = prune.shape[1]
    width = pixels + count + LANES
    return pl.pallas_call(
        payload_kernel,
        in_specs=[pl.BlockSpec(memory_space=pltpu.SMEM)] + [IN_HBM] * 4,
        out_specs=IN_VMEM,
        out_shape=jax.ShapeDtypeStruct((rows, width), jnp.bfloat16),
        scratch_shapes=[
            pltpu.VMEM((1, rows), jnp.bfloat16),
            pltpu.VMEM((choose, rows), jnp.int32),
            pltpu.VMEM((rows, count), jnp.int32),
            pltpu.SemaphoreType.DMA((4,)),
        ],
        compiler_params=pltpu.CompilerParams(vmem_limit_bytes=VMEM_LIMIT),
        name="make_payload",
    )(core, *(in_hbm(x) for x in (particles, tau.reshape(1, rows), candidates.T, prune)))


def pack_kernel(place_ref, x_ref, *out_refs, classes, cap, choose):
    *piece_refs, choice_ref = out_refs
    rows, width = x_ref.shape
    slots = classes * cap
    meta = x_ref[:, width - LANES :].astype(jnp.float32)
    base, flip = place_ref[0], place_ref[1]
    ids = base + (lax.broadcasted_iota(jnp.int32, (rows, classes), 1) ^ flip)
    ids = ids.astype(jnp.float32)
    named = jnp.zeros((rows, classes), jnp.float32)
    for j in range(choose):
        named = jnp.where(meta[:, 1 + j : 2 + j] == ids, 1.0, named)
    earlier = (
        lax.broadcasted_iota(jnp.int32, (rows, rows), 0)
        > lax.broadcasted_iota(jnp.int32, (rows, rows), 1)
    ).astype(jnp.float32)
    rank = jnp.dot(earlier, named, preferred_element_type=jnp.float32)
    slot = lax.broadcasted_iota(jnp.int32, (classes, slots), 1)
    first = lax.broadcasted_iota(jnp.int32, (classes, slots), 0) * cap
    spread = ((slot >= first) & (slot < first + cap)).astype(jnp.float32)
    rank_at = jnp.dot(rank, spread, preferred_element_type=jnp.float32)
    named_at = jnp.dot(named, spread, preferred_element_type=jnp.float32)
    place = (lax.broadcasted_iota(jnp.int32, (rows, slots), 1) % cap).astype(jnp.float32)
    choice = jnp.where((named_at > 0.5) & (rank_at == place), 1.0, 0.0)
    choice_ref[...] = choice
    picks = choice.astype(jnp.bfloat16)
    tile = 11 * LANES
    length = slots // len(piece_refs)
    for start in range(0, width, tile):
        stop = min(start + tile, width)
        packed = lax.dot_general(
            picks,
            x_ref[:, start:stop],
            (((0,), (0,)), ((), ())),
            preferred_element_type=jnp.float32,
        ).astype(jnp.bfloat16)
        for index, piece_ref in enumerate(piece_refs):
            piece_ref[:, start:stop] = packed[index * length : (index + 1) * length]


def pack(place, payload, classes, cap, choose):
    rows, width = payload.shape
    slots = classes * cap
    pieces = piece_count(classes)
    outs = [jax.ShapeDtypeStruct((slots // pieces, width), jnp.bfloat16)] * pieces
    outs.append(jax.ShapeDtypeStruct((rows, slots), jnp.float32))
    *packed, choice = pl.pallas_call(
        functools.partial(pack_kernel, classes=classes, cap=cap, choose=choose),
        in_specs=[pl.BlockSpec(memory_space=pltpu.SMEM), IN_VMEM],
        out_specs=[IN_VMEM] * len(outs),
        out_shape=outs,
        compiler_params=pltpu.CompilerParams(vmem_limit_bytes=VMEM_LIMIT),
        name="pack",
    )(place, payload)
    return packed, choice


def views_kernel(core_ref, mine_ref, theirs_ref, own_ref, other_ref, norm_ref, rest, sems):
    core = core_ref[0]
    _, count, total = mine_ref.shape
    half = total // 2
    images = total // BOX
    before = (core * (images // 2) + images - 1) % images * BOX
    after = (core + 1) * (images // 2) % images * BOX
    copies = []

    def fetch(source_ref, source, target, length):
        source = pl.multiple_of(source, BOX)
        copy = pltpu.make_async_copy(
            source_ref.at[0, :, pl.ds(source, length)], target, sems.at[len(copies)]
        )
        copy.start()
        copies.append(copy)

    for source_ref, out_ref in ((mine_ref, own_ref), (theirs_ref, other_ref)):
        fetch(source_ref, core * half, out_ref.at[:, pl.ds(BOX, half)], half)
        fetch(source_ref, before, out_ref.at[:, pl.ds(0, BOX)], BOX)
        fetch(source_ref, after, out_ref.at[:, pl.ds(BOX + half, BOX)], BOX)
        if source_ref is mine_ref:
            fetch(source_ref, (1 - core) * half, rest, half)
    for copy in copies[:4]:
        copy.wait()
    sums = jnp.zeros((count, LANES), jnp.float32)
    for start in range(0, half, LANES):
        for piece in (own_ref[:, BOX + start : BOX + start + LANES], rest[:, start : start + LANES]):
            piece = piece.astype(jnp.float32)
            sums = sums + piece * piece
    norm_ref[...] = column_to_row(jnp.sum(sums, axis=1, keepdims=True), count)
    for copy in copies[4:]:
        copy.wait()


def make_views(core, mine, theirs):
    _, count, total = mine.shape
    ext = jax.ShapeDtypeStruct((count, total // 2 + 2 * BOX), jnp.bfloat16)
    return pl.pallas_call(
        views_kernel,
        in_specs=[pl.BlockSpec(memory_space=pltpu.SMEM), IN_HBM, IN_HBM],
        out_specs=[IN_VMEM, IN_VMEM, IN_VMEM],
        out_shape=[ext, ext, jax.ShapeDtypeStruct((1, count), jnp.float32)],
        scratch_shapes=[
            pltpu.VMEM((count, total // 2), jnp.bfloat16),
            pltpu.SemaphoreType.DMA((7,)),
        ],
        compiler_params=pltpu.CompilerParams(vmem_limit_bytes=VMEM_LIMIT),
        name="make_views",
    )(core, in_hbm(mine), in_hbm(theirs))


def score_kernel(*refs, pixels):
    *x_refs, own_ref, other_ref, norm_ref, out_ref = refs
    rows = sum(ref.shape[0] for ref in x_refs)
    count = own_ref.shape[0]
    span = 2 * count
    tile = 16 * LANES
    one = jnp.zeros((rows, LANES), jnp.bfloat16)
    two = jnp.zeros((rows, 2 * LANES), jnp.bfloat16)
    total = None
    for start in range(0, pixels, tile):
        image = joined(x_refs, start, start + tile)
        stack = [
            [one, image, one],
            [image, two],
            [two, image],
            [one, roll_lanes(image, -1), one],
            [one, roll_lanes(image, 1), one],
        ]
        stack = jnp.concatenate([jnp.concatenate(line, axis=1) for line in stack], axis=0)
        stop = start + tile + 2 * LANES
        both = jnp.concatenate([own_ref[:, start:stop], other_ref[:, start:stop]], axis=0)
        part = lax.dot_general(
            stack, both, (((1,), (1,)), ((), ())), preferred_element_type=jnp.float32
        )
        total = part if total is None else total + part
    keep = joined(x_refs, pixels, pixels + count).astype(jnp.float32)
    offset = jnp.where(keep > 0.5, 0.0, NEG) - 0.5 * norm_ref[...]
    offset = jnp.concatenate([offset, jnp.zeros_like(offset)], axis=1)
    for index in range(shift_count):
        out_ref[:, index * span : (index + 1) * span] = (
            total[index * rows : (index + 1) * rows] + offset
        )


def half_scores(records, own, other, norms, pixels):
    rows = sum(piece.shape[0] for piece in records)
    count = own.shape[0]
    return pl.pallas_call(
        functools.partial(score_kernel, pixels=pixels),
        in_specs=[IN_VMEM] * (len(records) + 3),
        out_specs=IN_VMEM,
        out_shape=jax.ShapeDtypeStruct((rows, 2 * shift_count * count), jnp.float32),
        compiler_params=pltpu.CompilerParams(vmem_limit_bytes=VMEM_LIMIT),
        name="half_scores",
    )(*records, own, other, norms)


def mean_kernel(mine_ref, theirs_ref, *refs, pixels, pieces):
    x_refs = refs[:pieces]
    own_ref, other_ref = refs[pieces : pieces + 2]
    out_refs = refs[pieces + 2 : 2 * pieces + 2]
    weight_scr = refs[-1]
    length, width = x_refs[0].shape
    rows = length * pieces
    count = own_ref.shape[0]
    span = 2 * count
    tau = joined(x_refs, width - LANES, width)[:, 0:1].astype(jnp.float32)
    scores = []
    peak = jnp.full((rows, 1), NEG, jnp.float32)
    for index in range(shift_count):
        mine = mine_ref[:, index * span : (index + 1) * span]
        theirs = theirs_ref[:, index * span : (index + 1) * span]
        swapped = jnp.concatenate([theirs[:, count:], theirs[:, :count]], axis=1)
        full = mine + swapped
        score = jnp.where(full > -1e29, tau * full, NEG)
        scores.append(score)
        peak = jnp.maximum(peak, jnp.max(score, axis=1, keepdims=True))
    total = jnp.zeros((rows, 1), jnp.float32)
    for index, score in enumerate(scores):
        weight = jnp.where(score > -1e28, jnp.exp(score - peak), 0.0).astype(jnp.bfloat16)
        total = total + jnp.sum(weight.astype(jnp.float32), axis=1, keepdims=True)
        weight_scr[index * rows : (index + 1) * rows, :] = weight
    filled = total > 0
    safe = jnp.where(filled, total, 1.0)
    inverse = 1.0 / safe
    logs = put_log(jnp.where(filled, peak + jnp.log(safe), NEG), rows)
    for index, out_ref in enumerate(out_refs):
        out_ref[:, pixels:] = logs[index * length : (index + 1) * length]

    weights = weight_scr[...]
    tile = 16 * LANES
    for start in range(0, pixels, tile):
        stop = start + tile + 2 * LANES
        both = jnp.concatenate([own_ref[:, start:stop], other_ref[:, start:stop]], axis=0)
        sums = jnp.dot(weights, both, preferred_element_type=jnp.float32)
        inner = slice(LANES, LANES + tile)
        mean = sums[0:rows, inner] + sums[rows : 2 * rows, 0:tile]
        mean = mean + sums[2 * rows : 3 * rows, 2 * LANES : 2 * LANES + tile]
        mean = mean + roll_lanes(sums[3 * rows : 4 * rows, inner], 1)
        mean = mean + roll_lanes(sums[4 * rows : 5 * rows, inner], -1)
        mean = (mean * inverse).astype(jnp.bfloat16)
        for index, out_ref in enumerate(out_refs):
            out_ref[:, start : start + tile] = mean[index * length : (index + 1) * length]


def weighted_means(mine, theirs, records, own, other, pixels):
    length = records[0].shape[0]
    pieces = len(records)
    count = own.shape[0]
    return pl.pallas_call(
        functools.partial(mean_kernel, pixels=pixels, pieces=pieces),
        in_specs=[IN_VMEM] * (pieces + 4),
        out_specs=[IN_VMEM] * pieces,
        out_shape=[jax.ShapeDtypeStruct((length, pixels + LANES), jnp.bfloat16)] * pieces,
        scratch_shapes=[pltpu.VMEM((shift_count * pieces * length, 2 * count), jnp.bfloat16)],
        compiler_params=pltpu.CompilerParams(vmem_limit_bytes=VMEM_LIMIT),
        name="weighted_means",
    )(mine, theirs, *records, own, other)


def mix_kernel(*refs, dense, pixels):
    choice_ref, *back_refs, out_ref = refs
    if dense:
        *back_refs, part_ref = back_refs
    rows, slots = choice_ref.shape
    chosen = choice_ref[...] > 0.5
    row = column_to_row(get_log(joined(back_refs, pixels, pixels + LANES)), slots)
    value = jnp.where(chosen, row, NEG)
    best = jnp.max(value, axis=1, keepdims=True)
    if dense:
        part = get_log(part_ref[:, pixels:])
        best = jnp.maximum(best, part)
    factor = jnp.where(chosen, jnp.exp(value - best), 0.0)
    total = jnp.sum(factor, axis=1, keepdims=True)
    if dense:
        part_factor = jnp.where(part > -1e29, jnp.exp(part - best), 0.0)
        total = total + part_factor
    filled = total > 0
    safe = jnp.where(filled, total, 1.0)
    mixer = jnp.concatenate(split3(factor / safe), axis=0)
    tile = 16 * LANES
    for start in range(0, pixels, tile):
        span = slice(start, start + tile)
        images = joined(back_refs, start, start + tile)
        mixed = jnp.dot(mixer, images, preferred_element_type=jnp.float32)
        mixed = mixed[0:rows] + (mixed[rows : 2 * rows] + mixed[2 * rows : 3 * rows])
        if dense:
            mixed = mixed + (part_factor / safe) * part_ref[:, span].astype(jnp.float32)
        out_ref[:, span] = mixed.astype(jnp.bfloat16)
    if not dense:
        out_ref[:, pixels:] = put_log(jnp.where(filled, best + jnp.log(safe), NEG), rows)


def mix(choice, back, part, pixels):
    rows = choice.shape[0]
    dense = part is not None
    args = [choice, *back, part] if dense else [choice, *back]
    width = pixels if dense else pixels + LANES
    return pl.pallas_call(
        functools.partial(mix_kernel, dense=dense, pixels=pixels),
        in_specs=[IN_VMEM] * len(args),
        out_specs=IN_VMEM,
        out_shape=jax.ShapeDtypeStruct((rows, width), jnp.bfloat16),
        compiler_params=pltpu.CompilerParams(vmem_limit_bytes=VMEM_LIMIT),
        name="mix_final" if dense else "mix_half",
    )(*args)


def trade(pieces, peers):
    if len(pieces) == peers:
        return [pieces[0]] + [
            lax.ppermute(pieces[flip], "lo", [(i, i ^ flip) for i in range(peers)])
            for flip in range(1, peers)
        ]
    whole = pieces[0]
    parts = whole.reshape(peers, whole.shape[0] // peers, whole.shape[1])
    parts = lax.all_to_all(parts, "lo", split_axis=0, concat_axis=0, tiled=True)
    return [parts.reshape(whole.shape)]


def on_device(particles, tau, candidates, prune, projections):
    halves = lax.axis_size("hi")
    peers = lax.axis_size("lo")
    cores = lax.axis_size("ori")
    core = lax.axis_index("ori")
    part_rows, choose = candidates.shape
    pixels = particles.shape[1] // cores
    count = prune.shape[1]
    cap = 2 * part_rows * choose // (halves * peers)
    lo = lax.axis_index("lo").astype(jnp.int32)
    base = lax.axis_index("hi").astype(jnp.int32) * peers
    place = jnp.stack([base, lo if piece_count(peers) == peers else jnp.zeros_like(lo)])
    across = [(i, (i + 1) % halves) for i in range(halves)]
    swap = [(i, (i + 1) % cores) for i in range(cores)]

    core_id = core.astype(jnp.int32).reshape(1)
    payload = make_payload(core_id, particles, tau, candidates, prune, pixels)
    far_payload = lax.ppermute(payload, "hi", across)

    sent_near, choice_near = pack(place, payload, peers, cap, choose)
    records_near = trade(sent_near, peers)

    other = lax.ppermute(projections, "ori", swap)
    own_views, other_views, norms = make_views(core_id, projections, other)

    sent_far, choice_far = pack(place, far_payload, peers, cap, choose)
    sent_far, records_near = lax.optimization_barrier((sent_far, records_near))
    records_far = trade(sent_far, peers)

    def scores(records):
        mine = half_scores(records, own_views, other_views, norms, pixels)
        return mine, lax.ppermute(mine, "ori", swap)

    def means(sums, records):
        return weighted_means(*sums, records, own_views, other_views, pixels)

    far_means = means(scores(records_far), records_far)
    back_far = trade(far_means, peers)

    records_near, far_means = lax.optimization_barrier((records_near, far_means))
    near_means = means(scores(records_near), records_near)
    near_means, back_far = lax.optimization_barrier((near_means, back_far))

    far_mix = mix(choice_far, back_far, None, pixels)
    part_mix = lax.ppermute(far_mix, "hi", across)
    back_near = trade(near_means, peers)
    return mix(choice_near, back_near, part_mix, pixels)


def solution(mesh):
    grp, cls, ori = (mesh.shape[name] for name in ("grp", "cls", "ori"))
    inner = Mesh(mesh.devices.reshape(grp, 2, cls // 2, ori), ("grp", "hi", "lo", "ori"))
    rows = ("grp", "hi", "lo")
    placed = (
        P(rows, None),
        P(rows),
        P(rows, None),
        P(rows, "ori"),
        P(("hi", "lo"), "ori", None),
    )
    return jax.shard_map(
        on_device, mesh=inner, in_specs=placed, out_specs=P(rows, "ori"), check_vma=False
    )
```

time: 333 us -> 99.9 us (0.30); the launches traced: 329 us -> 99.7 us
  waiting for transfers between devices: 161 us -> 62.1 us
  matrix products: 53.2 us -> 0 us
  local copies, waits for them, and re-layouts: 35.9 us -> 0 us
  other arithmetic: 31.8 us -> 0.07 us
  Pallas kernels: 0 us -> 17.1 us
  between operations: 13.9 us -> 0.1 us
  starting transfers between devices: 28.4 us -> 20.3 us
  blocking collectives: 4.91 us -> 0 us
    all_to_all x5 -> x0, waiting for transfers between devices: 154 us -> none  [the longest x1 90.9 us: on_device(): lax.all_to_all(unit_image.reshape(lead_count, item_count, -1), 'cls', spl...]
    ppermute x0 -> x17, waiting for transfers between devices: none -> 62.1 us  [the longest x12 40.8 us: trade(): lax.ppermute(pieces[flip], 'lo', [(i, i ^ flip) for i in range(peers)])]
    dot_general x2 -> x0, matrix products: 53.2 us -> none  [the longest x1 28.6 us: on_device(): lax.dot_general(flat_images, shifted, (((1,), (1,)), ((), ())), preferred...]
    all_to_all x5 -> x0, starting transfers between devices: 27.8 us -> none  [the longest x1 7.25 us: on_device(): lax.all_to_all(send_tau, 'cls', split_axis=0, concat_axis=0, tiled=True)]
    ppermute x0 -> x17, starting transfers between devices: none -> 20.3 us  [the longest x12 14 us: trade(): lax.ppermute(pieces[flip], 'lo', [(i, i ^ flip) for i in range(peers)])]
    pallas_call x0 -> x10, Pallas kernels: none -> 17.1 us  [the longest x2 3.93 us: weighted_means(): pl.pallas_call(functools.partial(mean_kernel, pixels=pixels, pieces=piece...]
    gather x5 -> x0, local copies, waits for them, and re-layouts: 14.5 us -> none  [the longest x1 5.66 us: on_device(): record_unit = flat_unit[slot_of].reshape(part_rows, choose_count, -1)]
    unnamed x3 -> x0, other arithmetic: 10.6 us -> none
  transfers between devices with their start and end apart: 6 -> 17, of which waited for: 4 -> 12; matrix products, arithmetic and copies ran while one was open for 15% -> 0% of each run, Pallas kernels for 0% -> 9%
where the time goes in v2:
time: 99.9 us; the launch traced here: 99.7 us
  waiting for transfers between devices  62.1 us (62%)
  starting transfers between devices  20.3 us (20%)
  Pallas kernels  17.1 us (17%)
    ppermute x12, waiting for transfers between devices, trade(): lax.ppermute(pieces[flip], 'lo', [(i, i ^ flip) for i in range(peers)])  40.8 us
    ppermute x1, waiting for transfers between devices, on_device(): far_payload = lax.ppermute(payload, 'hi', across)  19.7 us
    ppermute x12, starting transfers between devices, trade(): lax.ppermute(pieces[flip], 'lo', [(i, i ^ flip) for i in range(peers)])  14 us
    pallas_call x2, Pallas kernels, weighted_means(): pl.pallas_call(functools.partial(mean_kernel, pixels=pixels, pieces=piece...  3.93 us
    ppermute x1, starting transfers between devices, on_device(): far_payload = lax.ppermute(payload, 'hi', across)  3.65 us
    pallas_call x2, Pallas kernels, half_scores(): pl.pallas_call(functools.partial(score_kernel, pixels=pixels), in_specs=[...  3.46 us
    pallas_call x1, Pallas kernels, make_views(): pl.pallas_call(views_kernel, in_specs=[pl.BlockSpec(memory_space=pltpu.SM...  3.27 us
    pallas_call x2, Pallas kernels, mix(): pl.pallas_call(functools.partial(mix_kernel, dense=dense, pixels=pixels),...  2.74 us
  transfers between devices with their start and end apart: 17, of which 12 were waited for; matrix products, arithmetic and copies ran while one was open for 0% of the time, Pallas kernels for 9%

profile of v2, /device:TPU:0, one launch (start us, length us, event | category | flops | bytes accessed | tf_op | source)
XLA Modules:
  0.0 99.7 jit_solution(17392628684200582956)
XLA Ops:
  0.5 1.1 %make_payload.1.x_ref = bf16[32,8448]{1,0:T(8,128)(2,1)S(1)} custom-call(s32[1]{0:T(128)} %bitcast.2.core_ref, bf16[32,16384]{1,0:T(8,128)(2,1)} %x_ref.1, bf16[1,32]{1,0:T(2,128)(2,1)} %bitcast.6, s32[2,32]{1,0:T(2,128)} %bitcast.5, s32[32,128]{1,0:T(8,128)} %keep_ref.1), custom_call_target="tpu_custom_call" | custom-call | tf_op jit(solution)/shard_map/make_payload/pallas_call | solution.py:118
  1.6 3.7 %collective-permute-start = (bf16[32,8448]{1,0:T(8,128)(2,1)S(1)}, bf16[32,8448]{1,0:T(8,128)(2,1)S(1)}, u32[]{:S(2)}, u32[]{:S(2)}) collective-permute-start(bf16[32,8448]{1,0:T(8,128)(2,1)S(1)} %make_payload.1.x_ref), channel_id=1, source_target_pairs={{0,8},{8,0},{1,9},{9,1},{2,10},{10,2},{3,11},{11,3},{4,12},{12,4},... | collective-permute-start | bytes 1622024 | tf_op jit(solution)/shard_map/ppermute | solution.py:429
  5.3 1.3 %pack.2 = (bf16[16,8448]{1,0:T(8,128)(2,1)S(1)}, bf16[16,8448]{1,0:T(8,128)(2,1)S(1)}, bf16[16,8448]{1,0:T(8,128)(2,1)S(1)}, bf16[16,8448]{1,0:T(8,128)(2,1)S(1)}, f32[32,64]{1,0:T(8,128)S(1)}) custom-call(s32[2]{0:T(128)S(1)} %pad_add_fusion.place_ref, bf16[32,8448]{1,0:T(8,128)(2,1)S(1)} %make_payload.1.x_ref), custom_call_target="tpu_custom_call" | custom-call | tf_op jit(solution)/shard_map/pack/pallas_call | solution.py:179
  6.6 1.6 %collective-permute-start.1 = (bf16[16,8448]{1,0:T(8,128)(2,1)S(1)}, bf16[16,8448]{1,0:T(8,128)(2,1)S(1)}, u32[]{:S(2)}, u32[]{:S(2)}) collective-permute-start(bf16[16,8448]{1,0:T(8,128)(2,1)S(1)} %get-tuple-element.52), channel_id=1, source_target_pairs={{0,2},{2,0},{4,6},{6,4},{1,3},{3,1},{5,7},{7,5},{8,10},{10,8},{12,... | collective-permute-start | bytes 811016 | tf_op jit(solution)/shard_map/ppermute | solution.py:403
  8.2 1.6 %collective-permute-start.2 = (bf16[16,8448]{1,0:T(8,128)(2,1)S(1)}, bf16[16,8448]{1,0:T(8,128)(2,1)S(1)}, u32[]{:S(2)}, u32[]{:S(2)}) collective-permute-start(bf16[16,8448]{1,0:T(8,128)(2,1)S(1)} %get-tuple-element.53), channel_id=1, source_target_pairs={{0,4},{2,6},{4,0},{6,2},{1,5},{3,7},{5,1},{7,3},{8,12},{10,14},{12... | collective-permute-start | bytes 811016 | tf_op jit(solution)/shard_map/ppermute | solution.py:403
  10.2 19.7 %collective-permute-done.x_ref = bf16[32,8448]{1,0:T(8,128)(2,1)S(1)} collective-permute-done((bf16[32,8448]{1,0:T(8,128)(2,1)S(1)}, bf16[32,8448]{1,0:T(8,128)(2,1)S(1)}, u32[]{:S(2)}, u32[]{:S(2)}) %collective-permute-start) | collective-permute-done | bytes 540704 | tf_op jit(solution)/shard_map/ppermute | solution.py:429
  29.8 1.3 %pack.3 = (bf16[16,8448]{1,0:T(8,128)(2,1)S(1)}, bf16[16,8448]{1,0:T(8,128)(2,1)S(1)}, bf16[16,8448]{1,0:T(8,128)(2,1)S(1)}, bf16[16,8448]{1,0:T(8,128)(2,1)S(1)}, f32[32,64]{1,0:T(8,128)S(1)}) custom-call(s32[2]{0:T(128)S(1)} %pad_add_fusion.place_ref, bf16[32,8448]{1,0:T(8,128)(2,1)S(1)} %collective-permute-done.x_ref), custom_call_target="tpu_custom_call" | custom-call | tf_op jit(solution)/shard_map/pack/pallas_call | solution.py:179
  31.2 1.6 %collective-permute-done.3.refs_3_ = bf16[16,8448]{1,0:T(8,128)(2,1)S(1)} collective-permute-done((bf16[16,8448]{1,0:T(8,128)(2,1)S(1)}, bf16[16,8448]{1,0:T(8,128)(2,1)S(1)}, u32[]{:S(2)}, u32[]{:S(2)}) %collective-permute-start.3) | collective-permute-done | bytes 270368 | tf_op jit(solution)/shard_map/ppermute | solution.py:403
  32.7 1.4 %collective-permute-start.4 = (bf16[16,8448]{1,0:T(8,128)(2,1)S(1)}, bf16[16,8448]{1,0:T(8,128)(2,1)S(1)}, u32[]{:S(2)}, u32[]{:S(2)}) collective-permute-start(bf16[16,8448]{1,0:T(8,128)(2,1)S(1)} %get-tuple-element.60), channel_id=1, source_target_pairs={{0,2},{2,0},{4,6},{6,4},{1,3},{3,1},{5,7},{7,5},{8,10},{10,8},{12,... | collective-permute-start | bytes 811016 | tf_op jit(solution)/shard_map/ppermute | solution.py:403
  34.2 2.0 %collective-permute-start.6 = (bf16[16,8448]{1,0:T(8,128)(2,1)S(1)}, bf16[16,8448]{1,0:T(8,128)(2,1)S(1)}, u32[]{:S(2)}, u32[]{:S(2)}) collective-permute-start(bf16[16,8448]{1,0:T(8,128)(2,1)S(1)} %get-tuple-element.62), channel_id=1, source_target_pairs={{0,6},{2,4},{4,2},{6,0},{1,7},{3,5},{5,3},{7,1},{8,14},{10,12},{12... | collective-permute-start | bytes 811016 | tf_op jit(solution)/shard_map/ppermute | solution.py:403
  36.2 3.3 %make_views.1 = (bf16[128,8448]{1,0:T(8,128)(2,1)S(1)}, bf16[128,8448]{1,0:T(8,128)(2,1)S(1)}, f32[1,128]{1,0:T(1,128)S(1)}) custom-call(s32[1]{0:T(128)} %bitcast.2.core_ref, bf16[1,128,16384]{2,1,0:T(8,128)(2,1)} %mine_ref.1, bf16[1,128,16384]{2,1,0:T(8,128)(2,1)} %collective-permute-done.7.theirs_ref), custom_call_target="tpu_custom_call" | custom-call | tf_op jit(solution)/shard_map/make_views/pallas_call | solution.py:228
  39.5 1.7 %collective-permute-done.4.refs_1_ = bf16[16,8448]{1,0:T(8,128)(2,1)S(1)} collective-permute-done((bf16[16,8448]{1,0:T(8,128)(2,1)S(1)}, bf16[16,8448]{1,0:T(8,128)(2,1)S(1)}, u32[]{:S(2)}, u32[]{:S(2)}) %collective-permute-start.4) | collective-permute-done | bytes 270368 | tf_op jit(solution)/shard_map/ppermute | solution.py:403
  41.2 2.4 %collective-permute-done.5.refs_2_ = bf16[16,8448]{1,0:T(8,128)(2,1)S(1)} collective-permute-done((bf16[16,8448]{1,0:T(8,128)(2,1)S(1)}, bf16[16,8448]{1,0:T(8,128)(2,1)S(1)}, u32[]{:S(2)}, u32[]{:S(2)}) %collective-permute-start.5) | collective-permute-done | bytes 270368 | tf_op jit(solution)/shard_map/ppermute | solution.py:403
  43.6 3.6 %collective-permute-done.6.refs_3_ = bf16[16,8448]{1,0:T(8,128)(2,1)S(1)} collective-permute-done((bf16[16,8448]{1,0:T(8,128)(2,1)S(1)}, bf16[16,8448]{1,0:T(8,128)(2,1)S(1)}, u32[]{:S(2)}, u32[]{:S(2)}) %collective-permute-start.6) | collective-permute-done | bytes 270368 | tf_op jit(solution)/shard_map/ppermute | solution.py:403
  47.1 1.7 %half_scores.2.mine_ref = f32[64,1280]{1,0:T(8,128)S(1)} custom-call(bf16[16,8448]{1,0:T(8,128)(2,1)S(1)} %get-tuple-element.59.refs_0_, bf16[16,8448]{1,0:T(8,128)(2,1)S(1)} %collective-permute-done.4.refs_1_, bf16[16,8448]{1,0:T(8,128)(2,1)S(1)} %collective-permute-done.5.refs_2_, bf16[16,8448]{1,0:T(8,128)(2,1)S(1)} %collective-permute-done.6.refs_3_, ...), custom_call_target="tpu_custom_call" | custom-call | tf_op jit(solution)/shard_map/half_scores/pallas_call | solution.py:279
  48.9 1.6 %collective-permute-done.8.theirs_ref = f32[64,1280]{1,0:T(8,128)S(1)} collective-permute-done((f32[64,1280]{1,0:T(8,128)S(1)}, f32[64,1280]{1,0:T(8,128)S(1)}, u32[]{:S(2)}, u32[]{:S(2)}) %collective-permute-start.8) | collective-permute-done | bytes 327712 | tf_op jit(solution)/shard_map/ppermute | solution.py:443
  50.6 2.0 %weighted_means.2 = (bf16[16,8320]{1,0:T(8,128)(2,1)S(1)}, bf16[16,8320]{1,0:T(8,128)(2,1)S(1)}, bf16[16,8320]{1,0:T(8,128)(2,1)S(1)}, bf16[16,8320]{1,0:T(8,128)(2,1)S(1)}) custom-call(f32[64,1280]{1,0:T(8,128)S(1)} %half_scores.2.mine_ref, f32[64,1280]{1,0:T(8,128)S(1)} %collective-permute-done.8.theirs_ref, ...), custom_call_target="tpu_custom_call" | custom-call | tf_op jit(solution)/shard_map/weighted_means/pallas_call | solution.py:341
  52.5 1.7 %half_scores.3.mine_ref = f32[64,1280]{1,0:T(8,128)S(1)} custom-call(bf16[16,8448]{1,0:T(8,128)(2,1)S(1)} %get-tuple-element.70.refs_0_, bf16[16,8448]{1,0:T(8,128)(2,1)S(1)} %collective-permute-done.1.refs_1_, bf16[16,8448]{1,0:T(8,128)(2,1)S(1)} %collective-permute-done.2.refs_2_, bf16[16,8448]{1,0:T(8,128)(2,1)S(1)} %collective-permute-done.3.refs_3_, ...), custom_call_target="tpu_custom_call" | custom-call | tf_op jit(solution)/shard_map/half_scores/pallas_call | solution.py:279
  54.5 1.5 %collective-permute-start.10 = (bf16[16,8320]{1,0:T(8,128)(2,1)S(1)}, bf16[16,8320]{1,0:T(8,128)(2,1)S(1)}, u32[]{:S(2)}, u32[]{:S(2)}) collective-permute-start(bf16[16,8320]{1,0:T(8,128)(2,1)S(1)} %get-tuple-element.67), channel_id=1, source_target_pairs={{0,2},{2,0},{4,6},{6,4},{1,3},{3,1},{5,7},{7,5},{8,10},{10,8},{12,... | collective-permute-start | bytes 798728 | tf_op jit(solution)/shard_map/ppermute | solution.py:403
  56.2 1.7 %collective-permute-start.12 = (bf16[16,8320]{1,0:T(8,128)(2,1)S(1)}, bf16[16,8320]{1,0:T(8,128)(2,1)S(1)}, u32[]{:S(2)}, u32[]{:S(2)}) collective-permute-start(bf16[16,8320]{1,0:T(8,128)(2,1)S(1)} %get-tuple-element.69), channel_id=1, source_target_pairs={{0,6},{2,4},{4,2},{6,0},{1,7},{3,5},{5,3},{7,1},{8,14},{10,12},{12... | collective-permute-start | bytes 798728 | tf_op jit(solution)/shard_map/ppermute | solution.py:403
  58.0 2.0 %weighted_means.3 = (bf16[16,8320]{1,0:T(8,128)(2,1)S(1)}, bf16[16,8320]{1,0:T(8,128)(2,1)S(1)}, bf16[16,8320]{1,0:T(8,128)(2,1)S(1)}, bf16[16,8320]{1,0:T(8,128)(2,1)S(1)}) custom-call(f32[64,1280]{1,0:T(8,128)S(1)} %half_scores.3.mine_ref, f32[64,1280]{1,0:T(8,128)S(1)} %collective-permute-done.9.theirs_ref, ...), custom_call_target="tpu_custom_call" | custom-call | tf_op jit(solution)/shard_map/weighted_means/pallas_call | solution.py:341
  60.0 3.2 %collective-permute-done.10.refs_2_ = bf16[16,8320]{1,0:T(8,128)(2,1)S(1)} collective-permute-done((bf16[16,8320]{1,0:T(8,128)(2,1)S(1)}, bf16[16,8320]{1,0:T(8,128)(2,1)S(1)}, u32[]{:S(2)}, u32[]{:S(2)}) %collective-permute-start.10) | collective-permute-done | bytes 266272 | tf_op jit(solution)/shard_map/ppermute | solution.py:403
  63.1 2.0 %collective-permute-done.11.refs_3_ = bf16[16,8320]{1,0:T(8,128)(2,1)S(1)} collective-permute-done((bf16[16,8320]{1,0:T(8,128)(2,1)S(1)}, bf16[16,8320]{1,0:T(8,128)(2,1)S(1)}, u32[]{:S(2)}, u32[]{:S(2)}) %collective-permute-start.11) | collective-permute-done | bytes 266272 | tf_op jit(solution)/shard_map/ppermute | solution.py:403
  65.2 4.8 %collective-permute-done.12.refs_4_ = bf16[16,8320]{1,0:T(8,128)(2,1)S(1)} collective-permute-done((bf16[16,8320]{1,0:T(8,128)(2,1)S(1)}, bf16[16,8320]{1,0:T(8,128)(2,1)S(1)}, u32[]{:S(2)}, u32[]{:S(2)}) %collective-permute-start.12) | collective-permute-done | bytes 266272 | tf_op jit(solution)/shard_map/ppermute | solution.py:403
  70.0 0.9 mix_half.1
  70.9 1.9 %collective-permute-start.16 = (bf16[32,8320]{1,0:T(8,128)(2,1)S(1)}, bf16[32,8320]{1,0:T(8,128)(2,1)S(1)}, u32[]{:S(2)}, u32[]{:S(2)}) collective-permute-start(bf16[32,8320]{1,0:T(8,128)(2,1)S(1)} %mix_half.1), channel_id=1, source_target_pairs={{0,8},{8,0},{1,9},{9,1},{2,10},{10,2},{3,11},{11,3},{4,12},{12,4},... | collective-permute-start | bytes 1597448 | tf_op jit(solution)/shard_map/ppermute | solution.py:456
  72.9 1.5 %collective-permute-start.13 = (bf16[16,8320]{1,0:T(8,128)(2,1)S(1)}, bf16[16,8320]{1,0:T(8,128)(2,1)S(1)}, u32[]{:S(2)}, u32[]{:S(2)}) collective-permute-start(bf16[16,8320]{1,0:T(8,128)(2,1)S(1)} %get-tuple-element.79), channel_id=1, source_target_pairs={{0,2},{2,0},{4,6},{6,4},{1,3},{3,1},{5,7},{7,5},{8,10},{10,8},{12,... | collective-permute-start | bytes 798728 | tf_op jit(solution)/shard_map/ppermute | solution.py:403
  74.4 1.7 %collective-permute-start.14 = (bf16[16,8320]{1,0:T(8,128)(2,1)S(1)}, bf16[16,8320]{1,0:T(8,128)(2,1)S(1)}, u32[]{:S(2)}, u32[]{:S(2)}) collective-permute-start(bf16[16,8320]{1,0:T(8,128)(2,1)S(1)} %get-tuple-element.80), channel_id=1, source_target_pairs={{0,4},{2,6},{4,0},{6,2},{1,5},{3,7},{5,1},{7,3},{8,12},{10,14},{12... | collective-permute-start | bytes 798728 | tf_op jit(solution)/shard_map/ppermute | solution.py:403
  76.4 4.9 %collective-permute-done.13.refs_2_ = bf16[16,8320]{1,0:T(8,128)(2,1)S(1)} collective-permute-done((bf16[16,8320]{1,0:T(8,128)(2,1)S(1)}, bf16[16,8320]{1,0:T(8,128)(2,1)S(1)}, u32[]{:S(2)}, u32[]{:S(2)}) %collective-permute-start.13) | collective-permute-done | bytes 266272 | tf_op jit(solution)/shard_map/ppermute | solution.py:403
  81.3 9.9 %collective-permute-done.14.refs_3_ = bf16[16,8320]{1,0:T(8,128)(2,1)S(1)} collective-permute-done((bf16[16,8320]{1,0:T(8,128)(2,1)S(1)}, bf16[16,8320]{1,0:T(8,128)(2,1)S(1)}, u32[]{:S(2)}, u32[]{:S(2)}) %collective-permute-start.14) | collective-permute-done | bytes 266272 | tf_op jit(solution)/shard_map/ppermute | solution.py:403
  91.2 6.7 %collective-permute-done.15.refs_4_ = bf16[16,8320]{1,0:T(8,128)(2,1)S(1)} collective-permute-done((bf16[16,8320]{1,0:T(8,128)(2,1)S(1)}, bf16[16,8320]{1,0:T(8,128)(2,1)S(1)}, u32[]{:S(2)}, u32[]{:S(2)}) %collective-permute-start.15) | collective-permute-done | bytes 266272 | tf_op jit(solution)/shard_map/ppermute | solution.py:403
  97.9 1.8 %mix_final.1 = bf16[32,8192]{1,0:T(8,128)(2,1)} custom-call(f32[32,64]{1,0:T(8,128)S(1)} %get-tuple-element.46.refs_0_, bf16[16,8320]{1,0:T(8,128)(2,1)S(1)} %get-tuple-element.78.refs_1_, bf16[16,8320]{1,0:T(8,128)(2,1)S(1)} %collective-permute-done.13.refs_2_, bf16[16,8320]{1,0:T(8,128)(2,1)S(1)} %collective-permute-done.14.refs_3_, ...), custom_call_target="tpu_custom_call" | custom-call | tf_op jit(solution)/shard_map/mix_final/pallas_call | solution.py:390
  (13 shorter events, 1.8 us)
Async XLA Ops:
  0.0 36.2 %collective-permute-start.7 = (bf16[1,128,16384]{2,1,0:T(8,128)(2,1)}, bf16[1,128,16384]{2,1,0:T(8,128)(2,1)}, u32[]{:S(2)}, u32[]{:S(2)}) collective-permute-start(bf16[1,128,16384]{2,1,0:T(8,128)(2,1)} %mine_ref.1), channel_id=1, source_target_pairs={{0,1},{1,0},{2,3},{3,2},{4,5},{5,4},{6,7},{7,6},{8,9},{9,8},{10,11... | collective-permute-start | bytes 12582920 | tf_op jit(solution)/shard_map/ppermute | solution.py:434
  1.6 28.3 %collective-permute-start = (bf16[32,8448]{1,0:T(8,128)(2,1)S(1)}, bf16[32,8448]{1,0:T(8,128)(2,1)S(1)}, u32[]{:S(2)}, u32[]{:S(2)}) collective-permute-start(bf16[32,8448]{1,0:T(8,128)(2,1)S(1)} %make_payload.1.x_ref), channel_id=1, source_target_pairs={{0,8},{8,0},{1,9},{9,1},{2,10},{10,2},{3,11},{11,3},{4,12},{12,4},... | collective-permute-start | bytes 1622024 | tf_op jit(solution)/shard_map/ppermute | solution.py:429
  6.6 24.5 %collective-permute-start.1 = (bf16[16,8448]{1,0:T(8,128)(2,1)S(1)}, bf16[16,8448]{1,0:T(8,128)(2,1)S(1)}, u32[]{:S(2)}, u32[]{:S(2)}) collective-permute-start(bf16[16,8448]{1,0:T(8,128)(2,1)S(1)} %get-tuple-element.52), channel_id=1, source_target_pairs={{0,2},{2,0},{4,6},{6,4},{1,3},{3,1},{5,7},{7,5},{8,10},{10,8},{12,... | collective-permute-start | bytes 811016 | tf_op jit(solution)/shard_map/ppermute | solution.py:403
  8.2 23.0 %collective-permute-start.2 = (bf16[16,8448]{1,0:T(8,128)(2,1)S(1)}, bf16[16,8448]{1,0:T(8,128)(2,1)S(1)}, u32[]{:S(2)}, u32[]{:S(2)}) collective-permute-start(bf16[16,8448]{1,0:T(8,128)(2,1)S(1)} %get-tuple-element.53), channel_id=1, source_target_pairs={{0,4},{2,6},{4,0},{6,2},{1,5},{3,7},{5,1},{7,3},{8,12},{10,14},{12... | collective-permute-start | bytes 811016 | tf_op jit(solution)/shard_map/ppermute | solution.py:403
  9.7 23.0 %collective-permute-start.3 = (bf16[16,8448]{1,0:T(8,128)(2,1)S(1)}, bf16[16,8448]{1,0:T(8,128)(2,1)S(1)}, u32[]{:S(2)}, u32[]{:S(2)}) collective-permute-start(bf16[16,8448]{1,0:T(8,128)(2,1)S(1)} %get-tuple-element.54), channel_id=1, source_target_pairs={{0,6},{2,4},{4,2},{6,0},{1,7},{3,5},{5,3},{7,1},{8,14},{10,12},{12... | collective-permute-start | bytes 811016 | tf_op jit(solution)/shard_map/ppermute | solution.py:403
  32.7 8.5 %collective-permute-start.4 = (bf16[16,8448]{1,0:T(8,128)(2,1)S(1)}, bf16[16,8448]{1,0:T(8,128)(2,1)S(1)}, u32[]{:S(2)}, u32[]{:S(2)}) collective-permute-start(bf16[16,8448]{1,0:T(8,128)(2,1)S(1)} %get-tuple-element.60), channel_id=1, source_target_pairs={{0,2},{2,0},{4,6},{6,4},{1,3},{3,1},{5,7},{7,5},{8,10},{10,8},{12,... | collective-permute-start | bytes 811016 | tf_op jit(solution)/shard_map/ppermute | solution.py:403
  34.2 9.4 %collective-permute-start.5 = (bf16[16,8448]{1,0:T(8,128)(2,1)S(1)}, bf16[16,8448]{1,0:T(8,128)(2,1)S(1)}, u32[]{:S(2)}, u32[]{:S(2)}) collective-permute-start(bf16[16,8448]{1,0:T(8,128)(2,1)S(1)} %get-tuple-element.61), channel_id=1, source_target_pairs={{0,4},{2,6},{4,0},{6,2},{1,5},{3,7},{5,1},{7,3},{8,12},{10,14},{12... | collective-permute-start | bytes 811016 | tf_op jit(solution)/shard_map/ppermute | solution.py:403
  34.2 13.0 %collective-permute-start.6 = (bf16[16,8448]{1,0:T(8,128)(2,1)S(1)}, bf16[16,8448]{1,0:T(8,128)(2,1)S(1)}, u32[]{:S(2)}, u32[]{:S(2)}) collective-permute-start(bf16[16,8448]{1,0:T(8,128)(2,1)S(1)} %get-tuple-element.62), channel_id=1, source_target_pairs={{0,6},{2,4},{4,2},{6,0},{1,7},{3,5},{5,3},{7,1},{8,14},{10,12},{12... | collective-permute-start | bytes 811016 | tf_op jit(solution)/shard_map/ppermute | solution.py:403
  48.9 1.7 %collective-permute-start.8 = (f32[64,1280]{1,0:T(8,128)S(1)}, f32[64,1280]{1,0:T(8,128)S(1)}, u32[]{:S(2)}, u32[]{:S(2)}) collective-permute-start(f32[64,1280]{1,0:T(8,128)S(1)} %half_scores.2.mine_ref), channel_id=1, source_target_pairs={{0,1},{1,0},{2,3},{3,2},{4,5},{5,4},{6,7},{7,6},{8,9},{9,8},{10,11... | collective-permute-start | bytes 983048 | tf_op jit(solution)/shard_map/ppermute | solution.py:443
  54.3 3.7 %collective-permute-start.9 = (f32[64,1280]{1,0:T(8,128)S(1)}, f32[64,1280]{1,0:T(8,128)S(1)}, u32[]{:S(2)}, u32[]{:S(2)}) collective-permute-start(f32[64,1280]{1,0:T(8,128)S(1)} %half_scores.3.mine_ref), channel_id=1, source_target_pairs={{0,1},{1,0},{2,3},{3,2},{4,5},{5,4},{6,7},{7,6},{8,9},{9,8},{10,11... | collective-permute-start | bytes 983048 | tf_op jit(solution)/shard_map/ppermute | solution.py:443
  54.5 8.7 %collective-permute-start.10 = (bf16[16,8320]{1,0:T(8,128)(2,1)S(1)}, bf16[16,8320]{1,0:T(8,128)(2,1)S(1)}, u32[]{:S(2)}, u32[]{:S(2)}) collective-permute-start(bf16[16,8320]{1,0:T(8,128)(2,1)S(1)} %get-tuple-element.67), channel_id=1, source_target_pairs={{0,2},{2,0},{4,6},{6,4},{1,3},{3,1},{5,7},{7,5},{8,10},{10,8},{12,... | collective-permute-start | bytes 798728 | tf_op jit(solution)/shard_map/ppermute | solution.py:403
  55.9 9.2 %collective-permute-start.11 = (bf16[16,8320]{1,0:T(8,128)(2,1)S(1)}, bf16[16,8320]{1,0:T(8,128)(2,1)S(1)}, u32[]{:S(2)}, u32[]{:S(2)}) collective-permute-start(bf16[16,8320]{1,0:T(8,128)(2,1)S(1)} %get-tuple-element.68), channel_id=1, source_target_pairs={{0,4},{2,6},{4,0},{6,2},{1,5},{3,7},{5,1},{7,3},{8,12},{10,14},{12... | collective-permute-start | bytes 798728 | tf_op jit(solution)/shard_map/ppermute | solution.py:403
  56.2 13.8 %collective-permute-start.12 = (bf16[16,8320]{1,0:T(8,128)(2,1)S(1)}, bf16[16,8320]{1,0:T(8,128)(2,1)S(1)}, u32[]{:S(2)}, u32[]{:S(2)}) collective-permute-start(bf16[16,8320]{1,0:T(8,128)(2,1)S(1)} %get-tuple-element.69), channel_id=1, source_target_pairs={{0,6},{2,4},{4,2},{6,0},{1,7},{3,5},{5,3},{7,1},{8,14},{10,12},{12... | collective-permute-start | bytes 798728 | tf_op jit(solution)/shard_map/ppermute | solution.py:403
  70.9 26.9 %collective-permute-start.16 = (bf16[32,8320]{1,0:T(8,128)(2,1)S(1)}, bf16[32,8320]{1,0:T(8,128)(2,1)S(1)}, u32[]{:S(2)}, u32[]{:S(2)}) collective-permute-start(bf16[32,8320]{1,0:T(8,128)(2,1)S(1)} %mix_half.1), channel_id=1, source_target_pairs={{0,8},{8,0},{1,9},{9,1},{2,10},{10,2},{3,11},{11,3},{4,12},{12,4},... | collective-permute-start | bytes 1597448 | tf_op jit(solution)/shard_map/ppermute | solution.py:456
  72.9 8.4 %collective-permute-start.13 = (bf16[16,8320]{1,0:T(8,128)(2,1)S(1)}, bf16[16,8320]{1,0:T(8,128)(2,1)S(1)}, u32[]{:S(2)}, u32[]{:S(2)}) collective-permute-start(bf16[16,8320]{1,0:T(8,128)(2,1)S(1)} %get-tuple-element.79), channel_id=1, source_target_pairs={{0,2},{2,0},{4,6},{6,4},{1,3},{3,1},{5,7},{7,5},{8,10},{10,8},{12,... | collective-permute-start | bytes 798728 | tf_op jit(solution)/shard_map/ppermute | solution.py:403
  74.4 16.8 %collective-permute-start.14 = (bf16[16,8320]{1,0:T(8,128)(2,1)S(1)}, bf16[16,8320]{1,0:T(8,128)(2,1)S(1)}, u32[]{:S(2)}, u32[]{:S(2)}) collective-permute-start(bf16[16,8320]{1,0:T(8,128)(2,1)S(1)} %get-tuple-element.80), channel_id=1, source_target_pairs={{0,4},{2,6},{4,0},{6,2},{1,5},{3,7},{5,1},{7,3},{8,12},{10,14},{12... | collective-permute-start | bytes 798728 | tf_op jit(solution)/shard_map/ppermute | solution.py:403
  76.1 21.8 %collective-permute-start.15 = (bf16[16,8320]{1,0:T(8,128)(2,1)S(1)}, bf16[16,8320]{1,0:T(8,128)(2,1)S(1)}, u32[]{:S(2)}, u32[]{:S(2)}) collective-permute-start(bf16[16,8320]{1,0:T(8,128)(2,1)S(1)} %get-tuple-element.81), channel_id=1, source_target_pairs={{0,6},{2,4},{4,2},{6,0},{1,7},{3,5},{5,3},{7,1},{8,14},{10,12},{12... | collective-permute-start | bytes 798728 | tf_op jit(solution)/shard_map/ppermute | solution.py:403

commit v3 on v2

v3 whole, which is shorter than its diff:
```python
import functools

import jax
import jax.numpy as jnp
from jax import lax
from jax.experimental import pallas as pl
from jax.experimental.pallas import tpu as pltpu
from jax.sharding import Mesh
from jax.sharding import PartitionSpec as P

BOX = 128
LANES = 128
NEG = -1e30
shift_count = 5
GIVEN_SHARE = 4
VMEM_LIMIT = 24 * 1024 * 1024
IN_HBM = pl.BlockSpec(memory_space=pltpu.HBM)
IN_VMEM = pl.BlockSpec(memory_space=pltpu.VMEM)


def in_hbm(array):
    return pltpu.with_memory_space_constraint(array, pltpu.HBM)


def joined(refs, start, stop):
    if len(refs) == 1:
        return refs[0][:, start:stop]
    return jnp.concatenate([ref[:, start:stop] for ref in refs], axis=0)


def tiles_of(spans):
    tile = 16 * LANES
    for place, start, length in spans:
        for offset in range(0, length, tile):
            yield place + offset, start + offset, min(tile, length - offset)


def cut(pixels, *shares):
    ends = [pixels // 8 * share for share in shares] + [pixels]
    return tuple(zip([0] + ends[:-1], ends))


def piece_count(peers):
    return peers if peers <= 4 else 1


def split3(value):
    high = value.astype(jnp.bfloat16)
    rest = value - high.astype(jnp.float32)
    middle = rest.astype(jnp.bfloat16)
    low = (rest - middle.astype(jnp.float32)).astype(jnp.bfloat16)
    return high, middle, low


def put_log(value, rows):
    high, middle, low = split3(value)
    lane = lax.broadcasted_iota(jnp.int32, (rows, LANES), 1)
    pieces = jnp.where(
        lane == 0,
        high.astype(jnp.float32),
        jnp.where(
            lane == 1,
            middle.astype(jnp.float32),
            jnp.where(lane == 2, low.astype(jnp.float32), 0.0),
        ),
    )
    return pieces.astype(jnp.bfloat16)


def get_log(pieces):
    wide = pieces.astype(jnp.float32)
    return (wide[:, 0:1] + wide[:, 1:2]) + wide[:, 2:3]


def column_to_row(column, count):
    eye = lax.broadcasted_iota(jnp.int32, (count, count), 0) == lax.broadcasted_iota(
        jnp.int32, (count, count), 1
    )
    return jnp.sum(jnp.where(eye, column, 0.0), axis=0, keepdims=True)


def roll_lanes(block, amount):
    pieces = [
        pltpu.roll(block[:, start : start + LANES], amount % LANES, 1)
        for start in range(0, block.shape[1], LANES)
    ]
    return jnp.concatenate(pieces, axis=1)


def payload_kernel(
    core_ref, x_ref, tau_ref, classes_ref, keep_ref, *refs, chunks
):
    out_refs = refs[: len(chunks)]
    tau_scr, classes_scr, keep_scr, sems = refs[len(chunks) :]
    first_ref = out_refs[0]
    rows = first_ref.shape[0]
    count = keep_scr.shape[1]
    pixels = chunks[-1][1]
    copies = [
        pltpu.make_async_copy(tau_ref, tau_scr, sems.at[0]),
        pltpu.make_async_copy(classes_ref, classes_scr, sems.at[1]),
        pltpu.make_async_copy(keep_ref, keep_scr, sems.at[2]),
    ]
    for out_ref, (start, stop) in zip(out_refs, chunks):
        source = pl.multiple_of(core_ref[0] * pixels + start, LANES)
        copies.append(
            pltpu.make_async_copy(
                x_ref.at[:, pl.ds(source, stop - start)],
                out_ref.at[:, pl.ds(0, stop - start)],
                sems.at[len(copies)],
            )
        )
    for copy in copies:
        copy.start()
    for copy in copies[:3]:
        copy.wait()
    end = chunks[0][1]
    keep = keep_scr[...].astype(jnp.float32).astype(jnp.bfloat16)
    first_ref[:, end : end + count] = keep
    eye = lax.broadcasted_iota(jnp.int32, (rows, rows), 0) == lax.broadcasted_iota(
        jnp.int32, (rows, rows), 1
    )
    tau = jnp.sum(
        jnp.where(eye, tau_scr[...].astype(jnp.float32), 0.0), axis=1, keepdims=True
    )
    lane = lax.broadcasted_iota(jnp.int32, (rows, LANES), 1)
    meta = jnp.where(lane == 0, tau, 0.0)
    for j in range(classes_scr.shape[0]):
        named = classes_scr[j : j + 1, :].astype(jnp.float32)
        named = jnp.sum(jnp.where(eye, named, 0.0), axis=1, keepdims=True)
        meta = jnp.where(lane == 1 + j, named, meta)
    first_ref[:, end + count :] = meta.astype(jnp.bfloat16)
    for copy in copies[3:]:
        copy.wait()


def make_payload(core, particles, tau, candidates, prune, chunks):
    rows, choose = candidates.shape
    count = prune.shape[1]
    widths = [stop - start for start, stop in chunks]
    widths[0] += count + LANES
    return pl.pallas_call(
        functools.partial(payload_kernel, chunks=chunks),
        in_specs=[pl.BlockSpec(memory_space=pltpu.SMEM)] + [IN_HBM] * 4,
        out_specs=[IN_VMEM] * len(chunks),
        out_shape=[jax.ShapeDtypeStruct((rows, width), jnp.bfloat16) for width in widths],
        scratch_shapes=[
            pltpu.VMEM((1, rows), jnp.bfloat16),
            pltpu.VMEM((choose, rows), jnp.int32),
            pltpu.VMEM((rows, count), jnp.int32),
            pltpu.SemaphoreType.DMA((3 + len(chunks),)),
        ],
        compiler_params=pltpu.CompilerParams(vmem_limit_bytes=VMEM_LIMIT),
        name="make_payload",
    )(core, *(in_hbm(x) for x in (particles, tau.reshape(1, rows), candidates.T, prune)))


def choose_slots(meta, base, flip, classes, cap, choose):
    rows = meta.shape[0]
    slots = classes * cap
    ids = base + (lax.broadcasted_iota(jnp.int32, (rows, classes), 1) ^ flip)
    ids = ids.astype(jnp.float32)
    named = jnp.zeros((rows, classes), jnp.float32)
    for j in range(choose):
        named = jnp.where(meta[:, 1 + j : 2 + j] == ids, 1.0, named)
    earlier = (
        lax.broadcasted_iota(jnp.int32, (rows, rows), 0)
        > lax.broadcasted_iota(jnp.int32, (rows, rows), 1)
    ).astype(jnp.float32)
    rank = jnp.dot(earlier, named, preferred_element_type=jnp.float32)
    slot = lax.broadcasted_iota(jnp.int32, (classes, slots), 1)
    first = lax.broadcasted_iota(jnp.int32, (classes, slots), 0) * cap
    spread = ((slot >= first) & (slot < first + cap)).astype(jnp.float32)
    rank_at = jnp.dot(rank, spread, preferred_element_type=jnp.float32)
    named_at = jnp.dot(named, spread, preferred_element_type=jnp.float32)
    place = (lax.broadcasted_iota(jnp.int32, (rows, slots), 1) % cap).astype(jnp.float32)
    return jnp.where((named_at > 0.5) & (rank_at == place), 1.0, 0.0)


def pack_kernel(place_ref, *refs, sources, classes, cap, choose, known):
    x_refs = refs[:sources]
    if known:
        choice_ref = refs[sources]
        piece_refs = refs[sources + 1 :]
        choice = choice_ref[...]
    else:
        *piece_refs, choice_ref = refs[sources:]
        width = x_refs[0].shape[1]
        meta = x_refs[0][:, width - LANES :].astype(jnp.float32)
        choice = choose_slots(meta, place_ref[0], place_ref[1], classes, cap, choose)
        choice_ref[...] = choice
    picks = choice.astype(jnp.bfloat16)
    length = classes * cap // len(piece_refs)
    place = 0
    tile = 16 * LANES
    for x_ref in reversed(x_refs):
        width = x_ref.shape[1]
        for start in range(0, width, tile):
            stop = min(start + tile, width)
            packed = lax.dot_general(
                picks,
                x_ref[:, start:stop],
                (((0,), (0,)), ((), ())),
                preferred_element_type=jnp.float32,
            ).astype(jnp.bfloat16)
            for index, piece_ref in enumerate(piece_refs):
                piece_ref[:, place + start : place + stop] = packed[
                    index * length : (index + 1) * length
                ]
        place += width


def pack(place, chunks, pieces, classes, cap, choose, choice=None):
    rows = chunks[0].shape[0]
    width = sum(chunk.shape[1] for chunk in chunks)
    slots = classes * cap
    known = choice is not None
    outs = [jax.ShapeDtypeStruct((slots // pieces, width), jnp.bfloat16)] * pieces
    if not known:
        outs.append(jax.ShapeDtypeStruct((rows, slots), jnp.float32))
    args = [*chunks, choice] if known else chunks
    packed = pl.pallas_call(
        functools.partial(
            pack_kernel,
            sources=len(chunks),
            classes=classes,
            cap=cap,
            choose=choose,
            known=known,
        ),
        in_specs=[pl.BlockSpec(memory_space=pltpu.SMEM)] + [IN_VMEM] * len(args),
        out_specs=[IN_VMEM] * len(outs),
        out_shape=outs,
        compiler_params=pltpu.CompilerParams(vmem_limit_bytes=VMEM_LIMIT),
        name="pack_rest" if known else "pack",
    )(place, *args)
    return packed if known else (packed[:-1], packed[-1])


def views_kernel(core_ref, mine_ref, theirs_ref, own_ref, other_ref, norm_ref, rest, sems):
    core = core_ref[0]
    _, count, total = mine_ref.shape
    half = total // 2
    images = total // BOX
    before = (core * (images // 2) + images - 1) % images * BOX
    after = (core + 1) * (images // 2) % images * BOX
    copies = []

    def fetch(source_ref, source, target, length):
        source = pl.multiple_of(source, BOX)
        copy = pltpu.make_async_copy(
            source_ref.at[0, :, pl.ds(source, length)], target, sems.at[len(copies)]
        )
        copy.start()
        copies.append(copy)

    for source_ref, out_ref in ((mine_ref, own_ref), (theirs_ref, other_ref)):
        fetch(source_ref, core * half, out_ref.at[:, pl.ds(BOX, half)], half)
        fetch(source_ref, before, out_ref.at[:, pl.ds(0, BOX)], BOX)
        fetch(source_ref, after, out_ref.at[:, pl.ds(BOX + half, BOX)], BOX)
        if source_ref is mine_ref:
            fetch(source_ref, (1 - core) * half, rest, half)
    for copy in copies[:4]:
        copy.wait()
    sums = jnp.zeros((count, LANES), jnp.float32)
    for start in range(0, half, LANES):
        for piece in (own_ref[:, BOX + start : BOX + start + LANES], rest[:, start : start + LANES]):
            piece = piece.astype(jnp.float32)
            sums = sums + piece * piece
    norm_ref[...] = column_to_row(jnp.sum(sums, axis=1, keepdims=True), count)
    for copy in copies[4:]:
        copy.wait()


def make_views(core, mine, theirs):
    _, count, total = mine.shape
    ext = jax.ShapeDtypeStruct((count, total // 2 + 2 * BOX), jnp.bfloat16)
    return pl.pallas_call(
        views_kernel,
        in_specs=[pl.BlockSpec(memory_space=pltpu.SMEM), IN_HBM, IN_HBM],
        out_specs=[IN_VMEM, IN_VMEM, IN_VMEM],
        out_shape=[ext, ext, jax.ShapeDtypeStruct((1, count), jnp.float32)],
        scratch_shapes=[
            pltpu.VMEM((count, total // 2), jnp.bfloat16),
            pltpu.SemaphoreType.DMA((7,)),
        ],
        compiler_params=pltpu.CompilerParams(vmem_limit_bytes=VMEM_LIMIT),
        name="make_views",
    )(core, in_hbm(mine), in_hbm(theirs))


def score_kernel(*refs, pieces, spans, masked, added):
    x_refs = refs[:pieces]
    own_ref, other_ref, norm_ref = refs[pieces : pieces + 3]
    out_ref = refs[-1]
    rows = sum(ref.shape[0] for ref in x_refs)
    count = own_ref.shape[0]
    span = 2 * count
    one = jnp.zeros((rows, LANES), jnp.bfloat16)
    two = jnp.zeros((rows, 2 * LANES), jnp.bfloat16)
    total = None
    for place, start, tile in tiles_of(spans):
        image = joined(x_refs, place, place + tile)
        stack = [
            [one, image, one],
            [image, two],
            [two, image],
            [one, roll_lanes(image, -1), one],
            [one, roll_lanes(image, 1), one],
        ]
        stack = jnp.concatenate([jnp.concatenate(line, axis=1) for line in stack], axis=0)
        stop = start + tile + 2 * LANES
        both = jnp.concatenate([own_ref[:, start:stop], other_ref[:, start:stop]], axis=0)
        part = lax.dot_general(
            stack, both, (((1,), (1,)), ((), ())), preferred_element_type=jnp.float32
        )
        total = part if total is None else total + part
    if masked:
        width = x_refs[0].shape[1]
        keep = joined(x_refs, width - LANES - count, width - LANES).astype(jnp.float32)
        offset = jnp.where(keep > 0.5, 0.0, NEG) - 0.5 * norm_ref[...]
        offset = jnp.concatenate([offset, jnp.zeros_like(offset)], axis=1)
    for index in range(shift_count):
        block = slice(index * span, (index + 1) * span)
        value = total[index * rows : (index + 1) * rows]
        if masked:
            value = value + offset
        if added:
            value = value + refs[pieces + 3][:, block]
        out_ref[:, block] = value


def half_scores(records, own, other, norms, spans, masked, earlier=None):
    rows = sum(piece.shape[0] for piece in records)
    count = own.shape[0]
    args = [*records, own, other, norms]
    if earlier is not None:
        args.append(earlier)
    return pl.pallas_call(
        functools.partial(
            score_kernel,
            pieces=len(records),
            spans=spans,
            masked=masked,
            added=earlier is not None,
        ),
        in_specs=[IN_VMEM] * len(args),
        out_specs=IN_VMEM,
        out_shape=jax.ShapeDtypeStruct((rows, 2 * shift_count * count), jnp.float32),
        compiler_params=pltpu.CompilerParams(vmem_limit_bytes=VMEM_LIMIT),
        name="half_scores",
    )(*args)


def weigh(mine_ref, theirs_ref, tau, count, weight_ref):
    rows = tau.shape[0]
    span = 2 * count
    scores = []
    peak = jnp.full((rows, 1), NEG, jnp.float32)
    for index in range(shift_count):
        mine = mine_ref[:, index * span : (index + 1) * span]
        theirs = theirs_ref[:, index * span : (index + 1) * span]
        swapped = jnp.concatenate([theirs[:, count:], theirs[:, :count]], axis=1)
        full = mine + swapped
        score = jnp.where(full > -1e29, tau * full, NEG)
        scores.append(score)
        peak = jnp.maximum(peak, jnp.max(score, axis=1, keepdims=True))
    total = jnp.zeros((rows, 1), jnp.float32)
    for index, score in enumerate(scores):
        weight = jnp.where(score > -1e28, jnp.exp(score - peak), 0.0).astype(jnp.bfloat16)
        total = total + jnp.sum(weight.astype(jnp.float32), axis=1, keepdims=True)
        weight_ref[index * rows : (index + 1) * rows, :] = weight
    filled = total > 0
    safe = jnp.where(filled, total, 1.0)
    return 1.0 / safe, put_log(jnp.where(filled, peak + jnp.log(safe), NEG), rows)


def write_means(weight_ref, inverse, own_ref, other_ref, out_refs, start, stop):
    length = out_refs[0].shape[0]
    rows = length * len(out_refs)
    weights = weight_ref[...]
    for place, first, tile in tiles_of([(0, start, stop - start)]):
        end = first + tile + 2 * LANES
        both = jnp.concatenate([own_ref[:, first:end], other_ref[:, first:end]], axis=0)
        sums = jnp.dot(weights, both, preferred_element_type=jnp.float32)
        inner = slice(LANES, LANES + tile)
        mean = sums[0:rows, inner] + sums[rows : 2 * rows, 0:tile]
        mean = mean + sums[2 * rows : 3 * rows, 2 * LANES : 2 * LANES + tile]
        mean = mean + roll_lanes(sums[3 * rows : 4 * rows, inner], 1)
        mean = mean + roll_lanes(sums[4 * rows : 5 * rows, inner], -1)
        mean = (mean * inverse).astype(jnp.bfloat16)
        for index, out_ref in enumerate(out_refs):
            out_ref[:, place : place + tile] = mean[index * length : (index + 1) * length]


def mean_kernel(mine_ref, theirs_ref, *refs, chunk, pieces):
    x_refs = refs[:pieces]
    own_ref, other_ref = refs[pieces : pieces + 2]
    out_refs = refs[pieces + 2 : 2 * pieces + 2]
    weight_ref, inverse_ref = refs[2 * pieces + 2 :]
    length, width = x_refs[0].shape
    tau = joined(x_refs, width - LANES, width)[:, 0:1].astype(jnp.float32)
    inverse, logs = weigh(mine_ref, theirs_ref, tau, own_ref.shape[0], weight_ref)
    inverse_ref[...] = jnp.broadcast_to(inverse, inverse_ref.shape)
    start, stop = chunk
    for index, out_ref in enumerate(out_refs):
        out_ref[:, stop - start :] = logs[index * length : (index + 1) * length]
    write_means(weight_ref, inverse, own_ref, other_ref, out_refs, start, stop)


def weighted_means(mine, theirs, records, own, other, chunk):
    length = records[0].shape[0]
    pieces = len(records)
    count = own.shape[0]
    outs = [jax.ShapeDtypeStruct((length, chunk[1] - chunk[0] + LANES), jnp.bfloat16)] * pieces
    outs += [
        jax.ShapeDtypeStruct((shift_count * pieces * length, 2 * count), jnp.bfloat16),
        jax.ShapeDtypeStruct((pieces * length, LANES), jnp.float32),
    ]
    *means, weights, inverse = pl.pallas_call(
        functools.partial(mean_kernel, chunk=chunk, pieces=pieces),
        in_specs=[IN_VMEM] * (pieces + 4),
        out_specs=[IN_VMEM] * len(outs),
        out_shape=outs,
        compiler_params=pltpu.CompilerParams(vmem_limit_bytes=VMEM_LIMIT),
        name="weighted_means",
    )(mine, theirs, *records, own, other)
    return means, weights, inverse


def rest_kernel(weight_ref, inverse_ref, own_ref, other_ref, *out_refs, chunk):
    write_means(weight_ref, inverse_ref[:, 0:1], own_ref, other_ref, out_refs, *chunk)


def rest_of_means(weights, inverse, own, other, chunk, pieces):
    length = inverse.shape[0] // pieces
    return pl.pallas_call(
        functools.partial(rest_kernel, chunk=chunk),
        in_specs=[IN_VMEM] * 4,
        out_specs=[IN_VMEM] * pieces,
        out_shape=[jax.ShapeDtypeStruct((length, chunk[1] - chunk[0]), jnp.bfloat16)] * pieces,
        compiler_params=pltpu.CompilerParams(vmem_limit_bytes=VMEM_LIMIT),
        name="rest_of_means",
    )(weights, inverse, own, other)


def half_mix_kernel(choice_ref, *refs, pieces):
    back_refs = refs[:pieces]
    out_ref, mixer_ref = refs[pieces:]
    rows, slots = choice_ref.shape
    width = out_ref.shape[1] - LANES
    chosen = choice_ref[...] > 0.5
    row = column_to_row(get_log(joined(back_refs, width, width + LANES)), slots)
    value = jnp.where(chosen, row, NEG)
    best = jnp.max(value, axis=1, keepdims=True)
    factor = jnp.where(chosen, jnp.exp(value - best), 0.0)
    total = jnp.sum(factor, axis=1, keepdims=True)
    filled = total > 0
    safe = jnp.where(filled, total, 1.0)
    mixer = jnp.concatenate(split3(factor / safe), axis=0)
    mixer_ref[...] = mixer
    out_ref[:, width:] = put_log(jnp.where(filled, best + jnp.log(safe), NEG), rows)
    write_mix(mixer, back_refs, out_ref, width)


def write_mix(mixer, back_refs, out_ref, width):
    rows = out_ref.shape[0]
    for place, _, tile in tiles_of([(0, 0, width)]):
        images = joined(back_refs, place, place + tile)
        mixed = jnp.dot(mixer, images, preferred_element_type=jnp.float32)
        mixed = mixed[0:rows] + (mixed[rows : 2 * rows] + mixed[2 * rows : 3 * rows])
        out_ref[:, place : place + tile] = mixed.astype(jnp.bfloat16)


def rest_mix_kernel(mixer_ref, *refs):
    *back_refs, out_ref = refs
    write_mix(mixer_ref[...], back_refs, out_ref, out_ref.shape[1])


def half_mix(choice, back):
    rows, slots = choice.shape
    return pl.pallas_call(
        functools.partial(half_mix_kernel, pieces=len(back)),
        in_specs=[IN_VMEM] * (1 + len(back)),
        out_specs=[IN_VMEM] * 2,
        out_shape=[
            jax.ShapeDtypeStruct((rows, back[0].shape[1]), jnp.bfloat16),
            jax.ShapeDtypeStruct((3 * rows, slots), jnp.bfloat16),
        ],
        compiler_params=pltpu.CompilerParams(vmem_limit_bytes=VMEM_LIMIT),
        name="half_mix",
    )(choice, *back)


def rest_of_mix(mixer, back):
    rows = mixer.shape[0] // 3
    return pl.pallas_call(
        rest_mix_kernel,
        in_specs=[IN_VMEM] * (1 + len(back)),
        out_specs=IN_VMEM,
        out_shape=jax.ShapeDtypeStruct((rows, back[0].shape[1]), jnp.bfloat16),
        compiler_params=pltpu.CompilerParams(vmem_limit_bytes=VMEM_LIMIT),
        name="rest_of_mix",
    )(mixer, *back)


def final_kernel(choice_ref, *refs, pieces, chunks):
    back_refs = refs[:pieces]
    part_refs = refs[pieces:-1]
    out_ref = refs[-1]
    rows, slots = choice_ref.shape
    pixels = chunks[-1][1]
    end = chunks[0][1]
    chosen = choice_ref[...] > 0.5
    row = column_to_row(get_log(joined(back_refs, pixels, pixels + LANES)), slots)
    value = jnp.where(chosen, row, NEG)
    part = get_log(part_refs[0][:, end:])
    best = jnp.maximum(jnp.max(value, axis=1, keepdims=True), part)
    factor = jnp.where(chosen, jnp.exp(value - best), 0.0)
    part_factor = jnp.where(part > -1e29, jnp.exp(part - best), 0.0)
    total = jnp.sum(factor, axis=1, keepdims=True) + part_factor
    safe = jnp.where(total > 0, total, 1.0)
    part_factor = part_factor / safe
    mixer = jnp.concatenate(split3(factor / safe), axis=0)
    for (first, last), part_ref in zip(chunks, part_refs):
        for place, start, tile in tiles_of([(0, first, last - first)]):
            images = joined(back_refs, start, start + tile)
            mixed = jnp.dot(mixer, images, preferred_element_type=jnp.float32)
            mixed = mixed[0:rows] + (mixed[rows : 2 * rows] + mixed[2 * rows : 3 * rows])
            mixed = mixed + part_factor * part_ref[:, place : place + tile].astype(jnp.float32)
            out_ref[:, start : start + tile] = mixed.astype(jnp.bfloat16)


def final_mix(choice, back, parts, chunks):
    rows = choice.shape[0]
    args = [choice, *back, *parts]
    return pl.pallas_call(
        functools.partial(final_kernel, pieces=len(back), chunks=chunks),
        in_specs=[IN_VMEM] * len(args),
        out_specs=IN_VMEM,
        out_shape=jax.ShapeDtypeStruct((rows, chunks[-1][1]), jnp.bfloat16),
        compiler_params=pltpu.CompilerParams(vmem_limit_bytes=VMEM_LIMIT),
        name="final_mix",
    )(*args)


def trade(pieces, peers):
    if len(pieces) == peers:
        return [pieces[0]] + [
            lax.ppermute(pieces[flip], "lo", [(i, i ^ flip) for i in range(peers)])
            for flip in range(1, peers)
        ]
    whole = pieces[0]
    parts = whole.reshape(peers, whole.shape[0] // peers, whole.shape[1])
    parts = lax.all_to_all(parts, "lo", split_axis=0, concat_axis=0, tiled=True)
    return [parts.reshape(whole.shape)]


def on_device(particles, tau, candidates, prune, projections):
    halves = lax.axis_size("hi")
    peers = lax.axis_size("lo")
    cores = lax.axis_size("ori")
    core = lax.axis_index("ori")
    part_rows, choose = candidates.shape
    pixels = particles.shape[1] // cores
    count = prune.shape[1]
    cap = 2 * part_rows * choose // (halves * peers)
    lo = lax.axis_index("lo").astype(jnp.int32)
    base = lax.axis_index("hi").astype(jnp.int32) * peers
    pieces = piece_count(peers)
    natural = jnp.stack([base, jnp.zeros_like(lo)])
    place = jnp.stack([base, lo if pieces == peers else jnp.zeros_like(lo)])
    across = [(i, (i + 1) % halves) for i in range(halves)]
    swap = [(i, (i + 1) % cores) for i in range(cores)]

    core_id = core.astype(jnp.int32).reshape(1)
    whole = ((0, pixels),)
    given = cut(pixels, GIVEN_SHARE)
    payload = make_payload(core_id, particles, tau, candidates, prune, whole)
    far_payload = [lax.ppermute(chunk, "hi", across) for chunk in payload]

    sent_near, choice_near = pack(place, payload, pieces, peers, cap, choose)
    records_near = trade(sent_near, peers)

    other = lax.ppermute(projections, "ori", swap)
    own_views, other_views, norms = make_views(core_id, projections, other)
    far_payload, own_views = lax.optimization_barrier((far_payload, own_views))
    views = (own_views, other_views)

    sent_far, choice_far = pack(place, far_payload, pieces, peers, cap, choose)
    sent_far, records_near = lax.optimization_barrier((sent_far, records_near))
    records_far = trade(sent_far, peers)

    spans = ((0, 0, pixels),)
    mine = half_scores(records_far, *views, norms, spans, True)
    theirs = lax.ppermute(mine, "ori", swap)
    far_means, weights, inverse = weighted_means(mine, theirs, records_far, *views, given[0])
    back_far = trade(far_means, peers)
    rest_means = rest_of_means(weights, inverse, *views, given[1], len(far_means))
    back_rest = trade(rest_means, peers)

    records_near, rest_means = lax.optimization_barrier((records_near, rest_means))
    mine = half_scores(records_near, *views, norms, spans, True)
    theirs = lax.ppermute(mine, "ori", swap)
    near_means, _, _ = weighted_means(mine, theirs, records_near, *views, (0, pixels))
    far_mix, mixer = half_mix(choice_far, back_far)
    part_mix = lax.ppermute(far_mix, "hi", across)
    rest_mix = rest_of_mix(mixer, back_rest)
    rest_part = lax.ppermute(rest_mix, "hi", across)
    back_near = trade(near_means, peers)
    return final_mix(choice_near, back_near, (part_mix, rest_part), given)


def solution(mesh):
    grp, cls, ori = (mesh.shape[name] for name in ("grp", "cls", "ori"))
    inner = Mesh(mesh.devices.reshape(grp, 2, cls // 2, ori), ("grp", "hi", "lo", "ori"))
    rows = ("grp", "hi", "lo")
    placed = (
        P(rows, None),
        P(rows),
        P(rows, None),
        P(rows, "ori"),
        P(("hi", "lo"), "ori", None),
    )
    return jax.shard_map(
        on_device, mesh=inner, in_specs=placed, out_specs=P(rows, "ori"), check_vma=False
    )
```

time: 99.9 us -> 95.2 us (0.953)
  waiting for transfers between devices: 62.1 us -> 52.5 us
  starting transfers between devices: 20.3 us -> 24.3 us
  Pallas kernels: 17.1 us -> 18.1 us
    ppermute x12 -> x15, waiting for transfers between devices: 40.8 us -> 19.2 us  [trade(): lax.ppermute(pieces[flip], 'lo', [(i, i ^ flip) for i in range(peers)])]
    ppermute x3 -> x4, waiting for transfers between devices: 21.3 us -> 33.3 us  [the longest x1 16.4 us: on_device(): far_payload = [lax.ppermute(chunk, 'hi', across) for chunk in payload]]
    ppermute x12 -> x15, starting transfers between devices: 14 us -> 16.9 us  [trade(): lax.ppermute(pieces[flip], 'lo', [(i, i ^ flip) for i in range(peers)])]
    ppermute x3 -> x4, starting transfers between devices: 3.92 us -> 5.29 us  [the longest x1 3.65 us: on_device(): far_payload = [lax.ppermute(chunk, 'hi', across) for chunk in payload]]
    pallas_call x9 -> x11, Pallas kernels: 13.9 us -> 14.8 us  [the longest x2 3.7 us: weighted_means(): pl.pallas_call(functools.partial(mean_kernel, chunk=chunk, pieces=pieces)...]
  transfers between devices with their start and end apart: 17 -> 21, of which waited for: 12 -> 11; matrix products, arithmetic and copies ran while one was open for 0% -> 0% of each run, Pallas kernels for 9% -> 11%
where the time goes in v3:
time: 95.2 us; the launch traced here: 95.1 us
  waiting for transfers between devices  52.5 us (55%)
  starting transfers between devices  24.3 us (26%)
  Pallas kernels  18.1 us (19%)
    ppermute x15, waiting for transfers between devices, trade(): lax.ppermute(pieces[flip], 'lo', [(i, i ^ flip) for i in range(peers)])  19.2 us
    ppermute x15, starting transfers between devices, trade(): lax.ppermute(pieces[flip], 'lo', [(i, i ^ flip) for i in range(peers)])  16.9 us
    ppermute x1, waiting for transfers between devices, on_device(): far_payload = [lax.ppermute(chunk, 'hi', across) for chunk in payload]  16.4 us
    ppermute x1, waiting for transfers between devices, on_device(): rest_part = lax.ppermute(rest_mix, 'hi', across)  15.3 us
    pallas_call x2, Pallas kernels, weighted_means(): pl.pallas_call(functools.partial(mean_kernel, chunk=chunk, pieces=pieces)...  3.7 us
    ppermute x1, starting transfers between devices, on_device(): far_payload = [lax.ppermute(chunk, 'hi', across) for chunk in payload]  3.65 us
    pallas_call x2, Pallas kernels, half_scores(): pl.pallas_call(functools.partial(score_kernel, pieces=len(records), spans...  3.46 us
    pallas_call x1, Pallas kernels, make_views(): pl.pallas_call(views_kernel, in_specs=[pl.BlockSpec(memory_space=pltpu.SM...  3.27 us
  transfers between devices with their start and end apart: 21, of which 11 were waited for; matrix products, arithmetic and copies ran while one was open for 0% of the time, Pallas kernels for 11%

profile of v3, /device:TPU:0, one launch (start us, length us, event | category | flops | bytes accessed | tf_op | source)
XLA Modules:
  0.0 95.1 jit_solution(15906332736621517374)
XLA Ops:
  0.5 1.1 %make_payload.1.refs_0_ = bf16[32,8448]{1,0:T(8,128)(2,1)S(1)} custom-call(s32[1]{0:T(128)} %bitcast.2.core_ref, bf16[32,16384]{1,0:T(8,128)(2,1)} %x_ref.1, bf16[1,32]{1,0:T(2,128)(2,1)} %bitcast.6, s32[2,32]{1,0:T(2,128)} %bitcast.5, s32[32,128]{1,0:T(8,128)} %keep_ref.1), custom_call_target="tpu_custom_call" | custom-call | tf_op jit(solution)/shard_map/make_payload/pallas_call | solution.py:142
  1.6 3.7 %collective-permute-start = (bf16[32,8448]{1,0:T(8,128)(2,1)S(1)}, bf16[32,8448]{1,0:T(8,128)(2,1)S(1)}, u32[]{:S(2)}, u32[]{:S(2)}) collective-permute-start(bf16[32,8448]{1,0:T(8,128)(2,1)S(1)} %make_payload.1.refs_0_), channel_id=1, source_target_pairs={{0,8},{8,0},{1,9},{9,1},{2,10},{10,2},{3,11},{11,3},{4,12},{12,4},... | collective-permute-start | bytes 1622024 | tf_op jit(solution)/shard_map/ppermute | solution.py:580
  5.3 1.3 %pack.2 = (bf16[16,8448]{1,0:T(8,128)(2,1)S(1)}, bf16[16,8448]{1,0:T(8,128)(2,1)S(1)}, bf16[16,8448]{1,0:T(8,128)(2,1)S(1)}, bf16[16,8448]{1,0:T(8,128)(2,1)S(1)}, f32[32,64]{1,0:T(8,128)S(1)}) custom-call(s32[2]{0:T(128)S(1)} %pad_add_fusion.place_ref, bf16[32,8448]{1,0:T(8,128)(2,1)S(1)} %make_payload.1.refs_0_), custom_call_target="tpu_custom_call" | custom-call | tf_op jit(solution)/shard_map/pack/pallas_call | solution.py:222
  6.6 1.6 %collective-permute-start.2 = (bf16[16,8448]{1,0:T(8,128)(2,1)S(1)}, bf16[16,8448]{1,0:T(8,128)(2,1)S(1)}, u32[]{:S(2)}, u32[]{:S(2)}) collective-permute-start(bf16[16,8448]{1,0:T(8,128)(2,1)S(1)} %get-tuple-element.56), channel_id=1, source_target_pairs={{0,2},{2,0},{4,6},{6,4},{1,3},{3,1},{5,7},{7,5},{8,10},{10,8},{12,... | collective-permute-start | bytes 811016 | tf_op jit(solution)/shard_map/ppermute | solution.py:550
  8.2 1.6 %collective-permute-start.3 = (bf16[16,8448]{1,0:T(8,128)(2,1)S(1)}, bf16[16,8448]{1,0:T(8,128)(2,1)S(1)}, u32[]{:S(2)}, u32[]{:S(2)}) collective-permute-start(bf16[16,8448]{1,0:T(8,128)(2,1)S(1)} %get-tuple-element.57), channel_id=1, source_target_pairs={{0,4},{2,6},{4,0},{6,2},{1,5},{3,7},{5,1},{7,3},{8,12},{10,14},{12... | collective-permute-start | bytes 811016 | tf_op jit(solution)/shard_map/ppermute | solution.py:550
  10.2 3.3 %make_views.1 = (bf16[128,8448]{1,0:T(8,128)(2,1)S(1)}, bf16[128,8448]{1,0:T(8,128)(2,1)S(1)}, f32[1,128]{1,0:T(1,128)S(1)}) custom-call(s32[1]{0:T(128)} %bitcast.2.core_ref, bf16[1,128,16384]{2,1,0:T(8,128)(2,1)} %mine_ref.1, bf16[1,128,16384]{2,1,0:T(8,128)(2,1)} %collective-permute-done.1.theirs_ref), custom_call_target="tpu_custom_call" | custom-call | tf_op jit(solution)/shard_map/make_views/pallas_call | solution.py:278
  13.5 16.4 %collective-permute-done.refs_0_ = bf16[32,8448]{1,0:T(8,128)(2,1)S(1)} collective-permute-done((bf16[32,8448]{1,0:T(8,128)(2,1)S(1)}, bf16[32,8448]{1,0:T(8,128)(2,1)S(1)}, u32[]{:S(2)}, u32[]{:S(2)}) %collective-permute-start) | collective-permute-done | bytes 540704 | tf_op jit(solution)/shard_map/ppermute | solution.py:580
  29.9 1.3 %pack.3 = (bf16[16,8448]{1,0:T(8,128)(2,1)S(1)}, bf16[16,8448]{1,0:T(8,128)(2,1)S(1)}, bf16[16,8448]{1,0:T(8,128)(2,1)S(1)}, bf16[16,8448]{1,0:T(8,128)(2,1)S(1)}, f32[32,64]{1,0:T(8,128)S(1)}) custom-call(s32[2]{0:T(128)S(1)} %pad_add_fusion.place_ref, bf16[32,8448]{1,0:T(8,128)(2,1)S(1)} %collective-permute-done.refs_0_), custom_call_target="tpu_custom_call" | custom-call | tf_op jit(solution)/shard_map/pack/pallas_call | solution.py:222
  31.2 1.5 %collective-permute-done.4.refs_3_ = bf16[16,8448]{1,0:T(8,128)(2,1)S(1)} collective-permute-done((bf16[16,8448]{1,0:T(8,128)(2,1)S(1)}, bf16[16,8448]{1,0:T(8,128)(2,1)S(1)}, u32[]{:S(2)}, u32[]{:S(2)}) %collective-permute-start.4) | collective-permute-done | bytes 270368 | tf_op jit(solution)/shard_map/ppermute | solution.py:550
  32.8 1.4 %collective-permute-start.5 = (bf16[16,8448]{1,0:T(8,128)(2,1)S(1)}, bf16[16,8448]{1,0:T(8,128)(2,1)S(1)}, u32[]{:S(2)}, u32[]{:S(2)}) collective-permute-start(bf16[16,8448]{1,0:T(8,128)(2,1)S(1)} %get-tuple-element.64), channel_id=1, source_target_pairs={{0,2},{2,0},{4,6},{6,4},{1,3},{3,1},{5,7},{7,5},{8,10},{10,8},{12,... | collective-permute-start | bytes 811016 | tf_op jit(solution)/shard_map/ppermute | solution.py:550
  34.2 2.0 %collective-permute-start.7 = (bf16[16,8448]{1,0:T(8,128)(2,1)S(1)}, bf16[16,8448]{1,0:T(8,128)(2,1)S(1)}, u32[]{:S(2)}, u32[]{:S(2)}) collective-permute-start(bf16[16,8448]{1,0:T(8,128)(2,1)S(1)} %get-tuple-element.66), channel_id=1, source_target_pairs={{0,6},{2,4},{4,2},{6,0},{1,7},{3,5},{5,3},{7,1},{8,14},{10,12},{12... | collective-permute-start | bytes 811016 | tf_op jit(solution)/shard_map/ppermute | solution.py:550
  36.3 5.0 %collective-permute-done.5.refs_1_ = bf16[16,8448]{1,0:T(8,128)(2,1)S(1)} collective-permute-done((bf16[16,8448]{1,0:T(8,128)(2,1)S(1)}, bf16[16,8448]{1,0:T(8,128)(2,1)S(1)}, u32[]{:S(2)}, u32[]{:S(2)}) %collective-permute-start.5) | collective-permute-done | bytes 270368 | tf_op jit(solution)/shard_map/ppermute | solution.py:550
  41.3 2.3 %collective-permute-done.6.refs_2_ = bf16[16,8448]{1,0:T(8,128)(2,1)S(1)} collective-permute-done((bf16[16,8448]{1,0:T(8,128)(2,1)S(1)}, bf16[16,8448]{1,0:T(8,128)(2,1)S(1)}, u32[]{:S(2)}, u32[]{:S(2)}) %collective-permute-start.6) | collective-permute-done | bytes 270368 | tf_op jit(solution)/shard_map/ppermute | solution.py:550
  43.6 3.6 %collective-permute-done.7.refs_3_ = bf16[16,8448]{1,0:T(8,128)(2,1)S(1)} collective-permute-done((bf16[16,8448]{1,0:T(8,128)(2,1)S(1)}, bf16[16,8448]{1,0:T(8,128)(2,1)S(1)}, u32[]{:S(2)}, u32[]{:S(2)}) %collective-permute-start.7) | collective-permute-done | bytes 270368 | tf_op jit(solution)/shard_map/ppermute | solution.py:550
  47.2 1.7 %half_scores.2.mine_ref = f32[64,1280]{1,0:T(8,128)S(1)} custom-call(bf16[16,8448]{1,0:T(8,128)(2,1)S(1)} %get-tuple-element.63.refs_0_, bf16[16,8448]{1,0:T(8,128)(2,1)S(1)} %collective-permute-done.5.refs_1_, bf16[16,8448]{1,0:T(8,128)(2,1)S(1)} %collective-permute-done.6.refs_2_, bf16[16,8448]{1,0:T(8,128)(2,1)S(1)} %collective-permute-done.7.refs_3_, ...), custom_call_target="tpu_custom_call" | custom-call | tf_op jit(solution)/shard_map/half_scores/pallas_call | solution.py:339
  49.0 1.6 %collective-permute-done.8.theirs_ref = f32[64,1280]{1,0:T(8,128)S(1)} collective-permute-done((f32[64,1280]{1,0:T(8,128)S(1)}, f32[64,1280]{1,0:T(8,128)S(1)}, u32[]{:S(2)}, u32[]{:S(2)}) %collective-permute-start.8) | collective-permute-done | bytes 327712 | tf_op jit(solution)/shard_map/ppermute | solution.py:596
  50.6 1.2 %weighted_means.2 = (bf16[16,4224]{1,0:T(8,128)(2,1)S(1)}, bf16[16,4224]{1,0:T(8,128)(2,1)S(1)}, bf16[16,4224]{1,0:T(8,128)(2,1)S(1)}, bf16[16,4224]{1,0:T(8,128...) custom-call(f32[64,1280]{1,0:T(8,128)S(1)} %half_scores.2.mine_ref, ...), custom_call_target="tpu_custom_call" | custom-call | tf_op jit(solution)/shard_map/weighted_means/pallas_call | solution.py:420
  52.9 1.7 %half_scores.3.mine_ref = f32[64,1280]{1,0:T(8,128)S(1)} custom-call(bf16[16,8448]{1,0:T(8,128)(2,1)S(1)} %get-tuple-element.76.refs_0_, bf16[16,8448]{1,0:T(8,128)(2,1)S(1)} %collective-permute-done.2.refs_1_, bf16[16,8448]{1,0:T(8,128)(2,1)S(1)} %collective-permute-done.3.refs_2_, bf16[16,8448]{1,0:T(8,128)(2,1)S(1)} %collective-permute-done.4.refs_3_, ...), custom_call_target="tpu_custom_call" | custom-call | tf_op jit(solution)/shard_map/half_scores/pallas_call | solution.py:339
  54.8 1.5 %collective-permute-start.13 = (bf16[16,4224]{1,0:T(8,128)(2,1)S(1)}, bf16[16,4224]{1,0:T(8,128)(2,1)S(1)}, u32[]{:S(2)}, u32[]{:S(2)}) collective-permute-start(bf16[16,4224]{1,0:T(8,128)(2,1)S(1)} %get-tuple-element.86), channel_id=1, source_target_pairs={{0,2},{2,0},{4,6},{6,4},{1,3},{3,1},{5,7},{7,5},{8,10},{10,8},{12,... | collective-permute-start | bytes 405512 | tf_op jit(solution)/shard_map/ppermute | solution.py:550
  56.6 1.8 %collective-permute-start.15 = (bf16[16,4224]{1,0:T(8,128)(2,1)S(1)}, bf16[16,4224]{1,0:T(8,128)(2,1)S(1)}, u32[]{:S(2)}, u32[]{:S(2)}) collective-permute-start(bf16[16,4224]{1,0:T(8,128)(2,1)S(1)} %get-tuple-element.88), channel_id=1, source_target_pairs={{0,6},{2,4},{4,2},{6,0},{1,7},{3,5},{5,3},{7,1},{8,14},{10,12},{12... | collective-permute-start | bytes 405512 | tf_op jit(solution)/shard_map/ppermute | solution.py:550
  58.3 1.4 %collective-permute-start.17 = (bf16[16,4096]{1,0:T(8,128)(2,1)S(1)}, bf16[16,4096]{1,0:T(8,128)(2,1)S(1)}, u32[]{:S(2)}, u32[]{:S(2)}) collective-permute-start(bf16[16,4096]{1,0:T(8,128)(2,1)S(1)} %get-tuple-element.73), channel_id=1, source_target_pairs={{0,2},{2,0},{4,6},{6,4},{1,3},{3,1},{5,7},{7,5},{8,10},{10,8},{12,... | collective-permute-start | bytes 393224 | tf_op jit(solution)/shard_map/ppermute | solution.py:550
  59.8 1.1 %collective-permute-done.13.refs_1_ = bf16[16,4224]{1,0:T(8,128)(2,1)S(1)} collective-permute-done((bf16[16,4224]{1,0:T(8,128)(2,1)S(1)}, bf16[16,4224]{1,0:T(8,128)(2,1)S(1)}, u32[]{:S(2)}, u32[]{:S(2)}) %collective-permute-start.13) | collective-permute-done | bytes 135200 | tf_op jit(solution)/shard_map/ppermute | solution.py:550
  61.2 1.5 %collective-permute-done.14.refs_2_ = bf16[16,4224]{1,0:T(8,128)(2,1)S(1)} collective-permute-done((bf16[16,4224]{1,0:T(8,128)(2,1)S(1)}, bf16[16,4224]{1,0:T(8,128)(2,1)S(1)}, u32[]{:S(2)}, u32[]{:S(2)}) %collective-permute-start.14) | collective-permute-done | bytes 135200 | tf_op jit(solution)/shard_map/ppermute | solution.py:550
  63.8 1.9 %collective-permute-done.15.refs_3_ = bf16[16,4224]{1,0:T(8,128)(2,1)S(1)} collective-permute-done((bf16[16,4224]{1,0:T(8,128)(2,1)S(1)}, bf16[16,4224]{1,0:T(8,128)(2,1)S(1)}, u32[]{:S(2)}, u32[]{:S(2)}) %collective-permute-start.15) | collective-permute-done | bytes 135200 | tf_op jit(solution)/shard_map/ppermute | solution.py:550
  66.4 1.7 %collective-permute-start.16 = (bf16[32,4224]{1,0:T(8,128)(2,1)S(1)}, bf16[32,4224]{1,0:T(8,128)(2,1)S(1)}, u32[]{:S(2)}, u32[]{:S(2)}) collective-permute-start(bf16[32,4224]{1,0:T(8,128)(2,1)S(1)} %get-tuple-element.89), channel_id=1, source_target_pairs={{0,8},{8,0},{1,9},{9,1},{2,10},{10,2},{3,11},{11,3},{4,12},{12,4},... | collective-permute-start | bytes 811016 | tf_op jit(solution)/shard_map/ppermute | solution.py:607
  68.1 2.5 %weighted_means.3 = (bf16[16,8320]{1,0:T(8,128)(2,1)S(1)}, bf16[16,8320]{1,0:T(8,128)(2,1)S(1)}, bf16[16,8320]{1,0:T(8,128)(2,1)S(1)}, bf16[16,8320]{1,0:T(8,128...) custom-call(f32[64,1280]{1,0:T(8,128)S(1)} %half_scores.3.mine_ref, ...), custom_call_target="tpu_custom_call" | custom-call | tf_op jit(solution)/shard_map/weighted_means/pallas_call | solution.py:420
  70.6 1.7 %collective-permute-start.10 = (bf16[16,8320]{1,0:T(8,128)(2,1)S(1)}, bf16[16,8320]{1,0:T(8,128)(2,1)S(1)}, u32[]{:S(2)}, u32[]{:S(2)}) collective-permute-start(bf16[16,8320]{1,0:T(8,128)(2,1)S(1)} %get-tuple-element.81), channel_id=1, source_target_pairs={{0,2},{2,0},{4,6},{6,4},{1,3},{3,1},{5,7},{7,5},{8,10},{10,8},{12,... | collective-permute-start | bytes 798728 | tf_op jit(solution)/shard_map/ppermute | solution.py:550
  72.3 1.7 %collective-permute-start.11 = (bf16[16,8320]{1,0:T(8,128)(2,1)S(1)}, bf16[16,8320]{1,0:T(8,128)(2,1)S(1)}, u32[]{:S(2)}, u32[]{:S(2)}) collective-permute-start(bf16[16,8320]{1,0:T(8,128)(2,1)S(1)} %get-tuple-element.82), channel_id=1, source_target_pairs={{0,4},{2,6},{4,0},{6,2},{1,5},{3,7},{5,1},{7,3},{8,12},{10,14},{12... | collective-permute-start | bytes 798728 | tf_op jit(solution)/shard_map/ppermute | solution.py:550
  74.4 1.4 %collective-permute-start.20 = (bf16[32,4096]{1,0:T(8,128)(2,1)S(1)}, bf16[32,4096]{1,0:T(8,128)(2,1)S(1)}, u32[]{:S(2)}, u32[]{:S(2)}) collective-permute-start(bf16[32,4096]{1,0:T(8,128)(2,1)S(1)} %rest_of_mix.1), channel_id=1, source_target_pairs={{0,8},{8,0},{1,9},{9,1},{2,10},{10,2},{3,11},{11,3},{4,12},{12,4},... | collective-permute-start | bytes 786440 | tf_op jit(solution)/shard_map/ppermute | solution.py:609
  75.8 15.3 %collective-permute-done.20.refs_5_ = bf16[32,4096]{1,0:T(8,128)(2,1)S(1)} collective-permute-done((bf16[32,4096]{1,0:T(8,128)(2,1)S(1)}, bf16[32,4096]{1,0:T(8,128)(2,1)S(1)}, u32[]{:S(2)}, u32[]{:S(2)}) %collective-permute-start.20) | collective-permute-done | bytes 262176 | tf_op jit(solution)/shard_map/ppermute | solution.py:609
  91.1 2.2 %collective-permute-done.12.refs_3_ = bf16[16,8320]{1,0:T(8,128)(2,1)S(1)} collective-permute-done((bf16[16,8320]{1,0:T(8,128)(2,1)S(1)}, bf16[16,8320]{1,0:T(8,128)(2,1)S(1)}, u32[]{:S(2)}, u32[]{:S(2)}) %collective-permute-start.12) | collective-permute-done | bytes 266272 | tf_op jit(solution)/shard_map/ppermute | solution.py:550
  93.3 1.8 %final_mix.1 = bf16[32,8192]{1,0:T(8,128)(2,1)} custom-call(f32[32,64]{1,0:T(8,128)S(1)} %get-tuple-element.48.choice_ref, bf16[16,8320]{1,0:T(8,128)(2,1)S(1)} %get-tuple-element.80.refs_0_, bf16[16,8320]{1,0:T(8,128)(2,1)S(1)} %collective-permute-done.10.refs_1_, bf16[16,8320]{1,0:T(8,128)(2,1)S(1)} %collective-permute-done.11.refs_2_, ...), custom_call_target="tpu_custom_call" | custom-call | tf_op jit(solution)/shard_map/final_mix/pallas_call | solution.py:537
  (23 shorter events, 5.0 us)
Async XLA Ops:
  0.0 10.2 %collective-permute-start.1 = (bf16[1,128,16384]{2,1,0:T(8,128)(2,1)}, bf16[1,128,16384]{2,1,0:T(8,128)(2,1)}, u32[]{:S(2)}, u32[]{:S(2)}) collective-permute-start(bf16[1,128,16384]{2,1,0:T(8,128)(2,1)} %mine_ref.1), channel_id=1, source_target_pairs={{0,1},{1,0},{2,3},{3,2},{4,5},{5,4},{6,7},{7,6},{8,9},{9,8},{10,11... | collective-permute-start | bytes 12582920 | tf_op jit(solution)/shard_map/ppermute | solution.py:585
  1.6 28.3 %collective-permute-start = (bf16[32,8448]{1,0:T(8,128)(2,1)S(1)}, bf16[32,8448]{1,0:T(8,128)(2,1)S(1)}, u32[]{:S(2)}, u32[]{:S(2)}) collective-permute-start(bf16[32,8448]{1,0:T(8,128)(2,1)S(1)} %make_payload.1.refs_0_), channel_id=1, source_target_pairs={{0,8},{8,0},{1,9},{9,1},{2,10},{10,2},{3,11},{11,3},{4,12},{12,4},... | collective-permute-start | bytes 1622024 | tf_op jit(solution)/shard_map/ppermute | solution.py:580
  6.6 24.6 %collective-permute-start.2 = (bf16[16,8448]{1,0:T(8,128)(2,1)S(1)}, bf16[16,8448]{1,0:T(8,128)(2,1)S(1)}, u32[]{:S(2)}, u32[]{:S(2)}) collective-permute-start(bf16[16,8448]{1,0:T(8,128)(2,1)S(1)} %get-tuple-element.56), channel_id=1, source_target_pairs={{0,2},{2,0},{4,6},{6,4},{1,3},{3,1},{5,7},{7,5},{8,10},{10,8},{12,... | collective-permute-start | bytes 811016 | tf_op jit(solution)/shard_map/ppermute | solution.py:550
  8.2 23.0 %collective-permute-start.3 = (bf16[16,8448]{1,0:T(8,128)(2,1)S(1)}, bf16[16,8448]{1,0:T(8,128)(2,1)S(1)}, u32[]{:S(2)}, u32[]{:S(2)}) collective-permute-start(bf16[16,8448]{1,0:T(8,128)(2,1)S(1)} %get-tuple-element.57), channel_id=1, source_target_pairs={{0,4},{2,6},{4,0},{6,2},{1,5},{3,7},{5,1},{7,3},{8,12},{10,14},{12... | collective-permute-start | bytes 811016 | tf_op jit(solution)/shard_map/ppermute | solution.py:550
  9.8 23.0 %collective-permute-start.4 = (bf16[16,8448]{1,0:T(8,128)(2,1)S(1)}, bf16[16,8448]{1,0:T(8,128)(2,1)S(1)}, u32[]{:S(2)}, u32[]{:S(2)}) collective-permute-start(bf16[16,8448]{1,0:T(8,128)(2,1)S(1)} %get-tuple-element.58), channel_id=1, source_target_pairs={{0,6},{2,4},{4,2},{6,0},{1,7},{3,5},{5,3},{7,1},{8,14},{10,12},{12... | collective-permute-start | bytes 811016 | tf_op jit(solution)/shard_map/ppermute | solution.py:550
  32.8 8.5 %collective-permute-start.5 = (bf16[16,8448]{1,0:T(8,128)(2,1)S(1)}, bf16[16,8448]{1,0:T(8,128)(2,1)S(1)}, u32[]{:S(2)}, u32[]{:S(2)}) collective-permute-start(bf16[16,8448]{1,0:T(8,128)(2,1)S(1)} %get-tuple-element.64), channel_id=1, source_target_pairs={{0,2},{2,0},{4,6},{6,4},{1,3},{3,1},{5,7},{7,5},{8,10},{10,8},{12,... | collective-permute-start | bytes 811016 | tf_op jit(solution)/shard_map/ppermute | solution.py:550
  34.2 9.4 %collective-permute-start.6 = (bf16[16,8448]{1,0:T(8,128)(2,1)S(1)}, bf16[16,8448]{1,0:T(8,128)(2,1)S(1)}, u32[]{:S(2)}, u32[]{:S(2)}) collective-permute-start(bf16[16,8448]{1,0:T(8,128)(2,1)S(1)} %get-tuple-element.65), channel_id=1, source_target_pairs={{0,4},{2,6},{4,0},{6,2},{1,5},{3,7},{5,1},{7,3},{8,12},{10,14},{12... | collective-permute-start | bytes 811016 | tf_op jit(solution)/shard_map/ppermute | solution.py:550
  34.2 13.0 %collective-permute-start.7 = (bf16[16,8448]{1,0:T(8,128)(2,1)S(1)}, bf16[16,8448]{1,0:T(8,128)(2,1)S(1)}, u32[]{:S(2)}, u32[]{:S(2)}) collective-permute-start(bf16[16,8448]{1,0:T(8,128)(2,1)S(1)} %get-tuple-element.66), channel_id=1, source_target_pairs={{0,6},{2,4},{4,2},{6,0},{1,7},{3,5},{5,3},{7,1},{8,14},{10,12},{12... | collective-permute-start | bytes 811016 | tf_op jit(solution)/shard_map/ppermute | solution.py:550
  48.9 1.7 %collective-permute-start.8 = (f32[64,1280]{1,0:T(8,128)S(1)}, f32[64,1280]{1,0:T(8,128)S(1)}, u32[]{:S(2)}, u32[]{:S(2)}) collective-permute-start(f32[64,1280]{1,0:T(8,128)S(1)} %half_scores.2.mine_ref), channel_id=1, source_target_pairs={{0,1},{1,0},{2,3},{3,2},{4,5},{5,4},{6,7},{7,6},{8,9},{9,8},{10,11... | collective-permute-start | bytes 983048 | tf_op jit(solution)/shard_map/ppermute | solution.py:596
  54.6 13.4 %collective-permute-start.9 = (f32[64,1280]{1,0:T(8,128)S(1)}, f32[64,1280]{1,0:T(8,128)S(1)}, u32[]{:S(2)}, u32[]{:S(2)}) collective-permute-start(f32[64,1280]{1,0:T(8,128)S(1)} %half_scores.3.mine_ref), channel_id=1, source_target_pairs={{0,1},{1,0},{2,3},{3,2},{4,5},{5,4},{6,7},{7,6},{8,9},{9,8},{10,11... | collective-permute-start | bytes 983048 | tf_op jit(solution)/shard_map/ppermute | solution.py:604
  54.8 6.0 %collective-permute-start.13 = (bf16[16,4224]{1,0:T(8,128)(2,1)S(1)}, bf16[16,4224]{1,0:T(8,128)(2,1)S(1)}, u32[]{:S(2)}, u32[]{:S(2)}) collective-permute-start(bf16[16,4224]{1,0:T(8,128)(2,1)S(1)} %get-tuple-element.86), channel_id=1, source_target_pairs={{0,2},{2,0},{4,6},{6,4},{1,3},{3,1},{5,7},{7,5},{8,10},{10,8},{12,... | collective-permute-start | bytes 405512 | tf_op jit(solution)/shard_map/ppermute | solution.py:550
  56.3 6.4 %collective-permute-start.14 = (bf16[16,4224]{1,0:T(8,128)(2,1)S(1)}, bf16[16,4224]{1,0:T(8,128)(2,1)S(1)}, u32[]{:S(2)}, u32[]{:S(2)}) collective-permute-start(bf16[16,4224]{1,0:T(8,128)(2,1)S(1)} %get-tuple-element.87), channel_id=1, source_target_pairs={{0,4},{2,6},{4,0},{6,2},{1,5},{3,7},{5,1},{7,3},{8,12},{10,14},{12... | collective-permute-start | bytes 405512 | tf_op jit(solution)/shard_map/ppermute | solution.py:550
  56.6 9.1 %collective-permute-start.15 = (bf16[16,4224]{1,0:T(8,128)(2,1)S(1)}, bf16[16,4224]{1,0:T(8,128)(2,1)S(1)}, u32[]{:S(2)}, u32[]{:S(2)}) collective-permute-start(bf16[16,4224]{1,0:T(8,128)(2,1)S(1)} %get-tuple-element.88), channel_id=1, source_target_pairs={{0,6},{2,4},{4,2},{6,0},{1,7},{3,5},{5,3},{7,1},{8,14},{10,12},{12... | collective-permute-start | bytes 405512 | tf_op jit(solution)/shard_map/ppermute | solution.py:550
  58.3 13.9 %collective-permute-start.17 = (bf16[16,4096]{1,0:T(8,128)(2,1)S(1)}, bf16[16,4096]{1,0:T(8,128)(2,1)S(1)}, u32[]{:S(2)}, u32[]{:S(2)}) collective-permute-start(bf16[16,4096]{1,0:T(8,128)(2,1)S(1)} %get-tuple-element.73), channel_id=1, source_target_pairs={{0,2},{2,0},{4,6},{6,4},{1,3},{3,1},{5,7},{7,5},{8,10},{10,8},{12,... | collective-permute-start | bytes 393224 | tf_op jit(solution)/shard_map/ppermute | solution.py:550
  60.9 13.1 %collective-permute-start.18 = (bf16[16,4096]{1,0:T(8,128)(2,1)S(1)}, bf16[16,4096]{1,0:T(8,128)(2,1)S(1)}, u32[]{:S(2)}, u32[]{:S(2)}) collective-permute-start(bf16[16,4096]{1,0:T(8,128)(2,1)S(1)} %get-tuple-element.74), channel_id=1, source_target_pairs={{0,4},{2,6},{4,0},{6,2},{1,5},{3,7},{5,1},{7,3},{8,12},{10,14},{12... | collective-permute-start | bytes 393224 | tf_op jit(solution)/shard_map/ppermute | solution.py:550
  62.7 11.3 %collective-permute-start.19 = (bf16[16,4096]{1,0:T(8,128)(2,1)S(1)}, bf16[16,4096]{1,0:T(8,128)(2,1)S(1)}, u32[]{:S(2)}, u32[]{:S(2)}) collective-permute-start(bf16[16,4096]{1,0:T(8,128)(2,1)S(1)} %get-tuple-element.75), channel_id=1, source_target_pairs={{0,6},{2,4},{4,2},{6,0},{1,7},{3,5},{5,3},{7,1},{8,14},{10,12},{12... | collective-permute-start | bytes 393224 | tf_op jit(solution)/shard_map/ppermute | solution.py:550
  66.4 24.7 %collective-permute-start.16 = (bf16[32,4224]{1,0:T(8,128)(2,1)S(1)}, bf16[32,4224]{1,0:T(8,128)(2,1)S(1)}, u32[]{:S(2)}, u32[]{:S(2)}) collective-permute-start(bf16[32,4224]{1,0:T(8,128)(2,1)S(1)} %get-tuple-element.89), channel_id=1, source_target_pairs={{0,8},{8,0},{1,9},{9,1},{2,10},{10,2},{3,11},{11,3},{4,12},{12,4},... | collective-permute-start | bytes 811016 | tf_op jit(solution)/shard_map/ppermute | solution.py:607
  70.6 20.5 %collective-permute-start.10 = (bf16[16,8320]{1,0:T(8,128)(2,1)S(1)}, bf16[16,8320]{1,0:T(8,128)(2,1)S(1)}, u32[]{:S(2)}, u32[]{:S(2)}) collective-permute-start(bf16[16,8320]{1,0:T(8,128)(2,1)S(1)} %get-tuple-element.81), channel_id=1, source_target_pairs={{0,2},{2,0},{4,6},{6,4},{1,3},{3,1},{5,7},{7,5},{8,10},{10,8},{12,... | collective-permute-start | bytes 798728 | tf_op jit(solution)/shard_map/ppermute | solution.py:550
  72.3 18.8 %collective-permute-start.11 = (bf16[16,8320]{1,0:T(8,128)(2,1)S(1)}, bf16[16,8320]{1,0:T(8,128)(2,1)S(1)}, u32[]{:S(2)}, u32[]{:S(2)}) collective-permute-start(bf16[16,8320]{1,0:T(8,128)(2,1)S(1)} %get-tuple-element.82), channel_id=1, source_target_pairs={{0,4},{2,6},{4,0},{6,2},{1,5},{3,7},{5,1},{7,3},{8,12},{10,14},{12... | collective-permute-start | bytes 798728 | tf_op jit(solution)/shard_map/ppermute | solution.py:550
  74.0 19.3 %collective-permute-start.12 = (bf16[16,8320]{1,0:T(8,128)(2,1)S(1)}, bf16[16,8320]{1,0:T(8,128)(2,1)S(1)}, u32[]{:S(2)}, u32[]{:S(2)}) collective-permute-start(bf16[16,8320]{1,0:T(8,128)(2,1)S(1)} %get-tuple-element.83), channel_id=1, source_target_pairs={{0,6},{2,4},{4,2},{6,0},{1,7},{3,5},{5,3},{7,1},{8,14},{10,12},{12... | collective-permute-start | bytes 798728 | tf_op jit(solution)/shard_map/ppermute | solution.py:550
  74.4 16.7 %collective-permute-start.20 = (bf16[32,4096]{1,0:T(8,128)(2,1)S(1)}, bf16[32,4096]{1,0:T(8,128)(2,1)S(1)}, u32[]{:S(2)}, u32[]{:S(2)}) collective-permute-start(bf16[32,4096]{1,0:T(8,128)(2,1)S(1)} %rest_of_mix.1), channel_id=1, source_target_pairs={{0,8},{8,0},{1,9},{9,1},{2,10},{10,2},{3,11},{11,3},{4,12},{12,4},... | collective-permute-start | bytes 786440 | tf_op jit(solution)/shard_map/ppermute | solution.py:609

commit v4 on v3

--- a/solution.py
+++ b/solution.py
@@ -13,6 +13,7 @@
 NEG = -1e30
 shift_count = 5
 GIVEN_SHARE = 4
+SENT_SHARE = 4
 VMEM_LIMIT = 24 * 1024 * 1024
 IN_HBM = pl.BlockSpec(memory_space=pltpu.HBM)
 IN_VMEM = pl.BlockSpec(memory_space=pltpu.VMEM)
@@ -574,9 +575,10 @@
     swap = [(i, (i + 1) % cores) for i in range(cores)]
 
     core_id = core.astype(jnp.int32).reshape(1)
-    whole = ((0, pixels),)
+    sent = cut(pixels, SENT_SHARE)
+    first, last = sent[0][1], pixels - sent[0][1]
     given = cut(pixels, GIVEN_SHARE)
-    payload = make_payload(core_id, particles, tau, candidates, prune, whole)
+    payload = make_payload(core_id, particles, tau, candidates, prune, sent)
     far_payload = [lax.ppermute(chunk, "hi", across) for chunk in payload]
 
     sent_near, choice_near = pack(place, payload, pieces, peers, cap, choose)
@@ -584,25 +586,34 @@
 
     other = lax.ppermute(projections, "ori", swap)
     own_views, other_views, norms = make_views(core_id, projections, other)
-    far_payload, own_views = lax.optimization_barrier((far_payload, own_views))
+    far_payload[0], own_views = lax.optimization_barrier((far_payload[0], own_views))
     views = (own_views, other_views)
 
-    sent_far, choice_far = pack(place, far_payload, pieces, peers, cap, choose)
-    sent_far, records_near = lax.optimization_barrier((sent_far, records_near))
+    sent_far, choice_far = pack(place, far_payload[:1], pieces, peers, cap, choose)
+    sent_far, records_near[1:3] = lax.optimization_barrier((sent_far, records_near[1:3]))
     records_far = trade(sent_far, peers)
-
-    spans = ((0, 0, pixels),)
-    mine = half_scores(records_far, *views, norms, spans, True)
+    choice_far, records_far[1 % len(records_far)] = lax.optimization_barrier(
+        (choice_far, records_far[1 % len(records_far)])
+    )
+    rest_far = pack(place, far_payload[1:], pieces, peers, cap, choose, choice_far)
+    rest_far, records_near = lax.optimization_barrier((rest_far, records_near))
+    records_rest = trade(rest_far, peers)
+
+    spans = ((last, 0, first), (0, first, last))
+    near_mine = half_scores(records_near, *views, norms, spans, True)
+    near_mine, records_rest = lax.optimization_barrier((near_mine, records_rest))
+
+    mine = half_scores(records_far, *views, norms, ((0, 0, first),), True)
+    mine = half_scores(records_rest, *views, norms, ((0, first, last),), False, mine)
     theirs = lax.ppermute(mine, "ori", swap)
     far_means, weights, inverse = weighted_means(mine, theirs, records_far, *views, given[0])
+    near_theirs = lax.ppermute(near_mine, "ori", swap)
+    near_theirs, far_means = lax.optimization_barrier((near_theirs, far_means))
     back_far = trade(far_means, peers)
     rest_means = rest_of_means(weights, inverse, *views, given[1], len(far_means))
     back_rest = trade(rest_means, peers)
-
-    records_near, rest_means = lax.optimization_barrier((records_near, rest_means))
-    mine = half_scores(records_near, *views, norms, spans, True)
-    theirs = lax.ppermute(mine, "ori", swap)
-    near_means, _, _ = weighted_means(mine, theirs, records_near, *views, (0, pixels))
+    near_means, _, _ = weighted_means(near_mine, near_theirs, records_near, *views, (0, pixels))
+    near_means, back_far = lax.optimization_barrier((near_means, back_far))
     far_mix, mixer = half_mix(choice_far, back_far)
     part_mix = lax.ppermute(far_mix, "hi", across)
     rest_mix = rest_of_mix(mixer, back_rest)

time: 95.2 us -> 91.1 us (0.957)
  waiting for transfers between devices: 52.5 us -> 43.2 us
  starting transfers between devices: 24.3 us -> 28.5 us
    ppermute x1 -> x2, waiting for transfers between devices: 16.4 us -> 4 us  [on_device(): far_payload = [lax.ppermute(chunk, 'hi', across) for chunk in payload]]
    ppermute x15 -> x18, starting transfers between devices: 16.9 us -> 21.2 us  [trade(): lax.ppermute(pieces[flip], 'lo', [(i, i ^ flip) for i in range(peers)])]
    ppermute x15 -> x18, waiting for transfers between devices: 19.2 us -> 21.6 us  [trade(): lax.ppermute(pieces[flip], 'lo', [(i, i ^ flip) for i in range(peers)])]
    ppermute x1 -> x2, starting transfers between devices: 3.65 us -> 5 us  [on_device(): far_payload = [lax.ppermute(chunk, 'hi', across) for chunk in payload]]
    ppermute x1, starting transfers between devices: 1.36 us -> 0.07 us  [on_device(): rest_part = lax.ppermute(rest_mix, 'hi', across)]
    ppermute x1, waiting for transfers between devices: 15.3 us -> 16.4 us  [on_device(): rest_part = lax.ppermute(rest_mix, 'hi', across)]
    pallas_call x2 -> x3, Pallas kernels: 2.64 us -> 3.36 us  [pack(): pl.pallas_call(functools.partial(pack_kernel, sources=len(chunks), classe...]
    pallas_call x2 -> x3, Pallas kernels: 3.46 us -> 3.66 us  [half_scores(): pl.pallas_call(functools.partial(score_kernel, pieces=len(records), spans...]
  transfers between devices with their start and end apart: 21 -> 25, of which waited for: 11 -> 10; matrix products, arithmetic and copies ran while one was open for 0% -> 0% of each run, Pallas kernels for 11% -> 18%
where the time goes in v4:
time: 91.1 us; the launch traced here: 90.9 us
  waiting for transfers between devices  43.2 us (47%)
  starting transfers between devices  28.5 us (31%)
  Pallas kernels  19 us (21%)
    ppermute x18, waiting for transfers between devices, trade(): lax.ppermute(pieces[flip], 'lo', [(i, i ^ flip) for i in range(peers)])  21.6 us
    ppermute x18, starting transfers between devices, trade(): lax.ppermute(pieces[flip], 'lo', [(i, i ^ flip) for i in range(peers)])  21.2 us
    ppermute x1, waiting for transfers between devices, on_device(): rest_part = lax.ppermute(rest_mix, 'hi', across)  16.4 us
    ppermute x2, starting transfers between devices, on_device(): far_payload = [lax.ppermute(chunk, 'hi', across) for chunk in payload]  5 us
    ppermute x2, waiting for transfers between devices, on_device(): far_payload = [lax.ppermute(chunk, 'hi', across) for chunk in payload]  4 us
    pallas_call x2, Pallas kernels, weighted_means(): pl.pallas_call(functools.partial(mean_kernel, chunk=chunk, pieces=pieces)...  3.7 us
    pallas_call x3, Pallas kernels, half_scores(): pl.pallas_call(functools.partial(score_kernel, pieces=len(records), spans...  3.66 us
    pallas_call x3, Pallas kernels, pack(): pl.pallas_call(functools.partial(pack_kernel, sources=len(chunks), classe...  3.36 us
  transfers between devices with their start and end apart: 25, of which 10 were waited for; matrix products, arithmetic and copies ran while one was open for 0% of the time, Pallas kernels for 18%

profile of v4, /device:TPU:0, one launch (start us, length us, event | category | flops | bytes accessed | tf_op | source)
XLA Modules:
  0.0 90.9 jit_solution(13367372027327034232)
XLA Ops:
  0.5 1.1 %make_payload.1 = (bf16[32,4352]{1,0:T(8,128)(2,1)S(1)}, bf16[32,4096]{1,0:T(8,128)(2,1)S(1)}) custom-call(s32[1]{0:T(128)} %bitcast.2.core_ref, bf16[32,16384]{1,0:T(8,128)(2,1)} %x_ref.1, bf16[1,32]{1,0:T(2,128)(2,1)} %bitcast.6, s32[2,32]{1,0:T(2,128)} %bitcast.5, s32[32,128]{1,0:T(8,128)} %keep_ref.1), custom_call_target="tpu_custom_call" | custom-call | tf_op jit(solution)/shard_map/make_payload/pallas_call | solution.py:143
  1.6 3.7 %collective-permute-start.1 = (bf16[32,4352]{1,0:T(8,128)(2,1)S(1)}, bf16[32,4352]{1,0:T(8,128)(2,1)S(1)}, u32[]{:S(2)}, u32[]{:S(2)}) collective-permute-start(bf16[32,4352]{1,0:T(8,128)(2,1)S(1)} %get-tuple-element.76.refs_0_), channel_id=1, source_target_pairs={{0,8},{8,0},{1,9},{9,1},{2,10},{10,2},{3,11},{11,3},{4,12},{12,4},... | collective-permute-start | bytes 835592 | tf_op jit(solution)/shard_map/ppermute | solution.py:582
  5.3 1.3 %pack.2 = (bf16[16,8448]{1,0:T(8,128)(2,1)S(1)}, bf16[16,8448]{1,0:T(8,128)(2,1)S(1)}, bf16[16,8448]{1,0:T(8,128)(2,1)S(1)}, bf16[16,8448]{1,0:T(8,128)(2,1)S(1)}, f32[32,64]{1,0:T(8,128)S(1)}) custom-call(s32[2]{0:T(128)S(1)} %pad_add_fusion.place_ref, bf16[32,4352]{1,0:T(8,128)(2,1)S(1)} %get-tuple-element.76.refs_0_, ...), custom_call_target="tpu_custom_call" | custom-call | tf_op jit(solution)/shard_map/pack/pallas_call | solution.py:223
  6.6 1.6 %collective-permute-start.3 = (bf16[16,8448]{1,0:T(8,128)(2,1)S(1)}, bf16[16,8448]{1,0:T(8,128)(2,1)S(1)}, u32[]{:S(2)}, u32[]{:S(2)}) collective-permute-start(bf16[16,8448]{1,0:T(8,128)(2,1)S(1)} %get-tuple-element.86), channel_id=1, source_target_pairs={{0,2},{2,0},{4,6},{6,4},{1,3},{3,1},{5,7},{7,5},{8,10},{10,8},{12,... | collective-permute-start | bytes 811016 | tf_op jit(solution)/shard_map/ppermute | solution.py:551
  8.2 1.6 %collective-permute-start.4 = (bf16[16,8448]{1,0:T(8,128)(2,1)S(1)}, bf16[16,8448]{1,0:T(8,128)(2,1)S(1)}, u32[]{:S(2)}, u32[]{:S(2)}) collective-permute-start(bf16[16,8448]{1,0:T(8,128)(2,1)S(1)} %get-tuple-element.87), channel_id=1, source_target_pairs={{0,4},{2,6},{4,0},{6,2},{1,5},{3,7},{5,1},{7,3},{8,12},{10,14},{12... | collective-permute-start | bytes 811016 | tf_op jit(solution)/shard_map/ppermute | solution.py:551
  10.2 1.3 %collective-permute-start = (bf16[32,4096]{1,0:T(8,128)(2,1)S(1)}, bf16[32,4096]{1,0:T(8,128)(2,1)S(1)}, u32[]{:S(2)}, u32[]{:S(2)}) collective-permute-start(bf16[32,4096]{1,0:T(8,128)(2,1)S(1)} %get-tuple-element.77.refs_1_), channel_id=1, source_target_pairs={{0,8},{8,0},{1,9},{9,1},{2,10},{10,2},{3,11},{11,3},{4,12},{12,4},... | collective-permute-start | bytes 786440 | tf_op jit(solution)/shard_map/ppermute | solution.py:582
  11.5 3.3 %make_views.1 = (bf16[128,8448]{1,0:T(8,128)(2,1)S(1)}, bf16[128,8448]{1,0:T(8,128)(2,1)S(1)}, f32[1,128]{1,0:T(1,128)S(1)}) custom-call(s32[1]{0:T(128)} %bitcast.2.core_ref, bf16[1,128,16384]{2,1,0:T(8,128)(2,1)} %mine_ref.1, bf16[1,128,16384]{2,1,0:T(8,128)(2,1)} %collective-permute-done.2.theirs_ref), custom_call_target="tpu_custom_call" | custom-call | tf_op jit(solution)/shard_map/make_views/pallas_call | solution.py:279
  14.8 4.0 %collective-permute-done.1.refs_0_ = bf16[32,4352]{1,0:T(8,128)(2,1)S(1)} collective-permute-done((bf16[32,4352]{1,0:T(8,128)(2,1)S(1)}, bf16[32,4352]{1,0:T(8,128)(2,1)S(1)}, u32[]{:S(2)}, u32[]{:S(2)}) %collective-permute-start.1) | collective-permute-done | bytes 278560 | tf_op jit(solution)/shard_map/ppermute | solution.py:582
  18.8 1.2 %pack.3 = (bf16[16,4352]{1,0:T(8,128)(2,1)S(1)}, bf16[16,4352]{1,0:T(8,128)(2,1)S(1)}, bf16[16,4352]{1,0:T(8,128)(2,1)S(1)}, bf16[16,4352]{1,0:T(8,128)(2,1)S(1)}, f32[32,64]{1,0:T(8,128)S(1)}) custom-call(s32[2]{0:T(128)S(1)} %pad_add_fusion.place_ref, bf16[32,4352]{1,0:T(8,128)(2,1)S(1)} %collective-permute-done.1.refs_0_), custom_call_target="tpu_custom_call" | custom-call | tf_op jit(solution)/shard_map/pack/pallas_call | solution.py:223
  20.0 8.0 %collective-permute-done.4.refs_2_ = bf16[16,8448]{1,0:T(8,128)(2,1)S(1)} collective-permute-done((bf16[16,8448]{1,0:T(8,128)(2,1)S(1)}, bf16[16,8448]{1,0:T(8,128)(2,1)S(1)}, u32[]{:S(2)}, u32[]{:S(2)}) %collective-permute-start.4) | collective-permute-done | bytes 270368 | tf_op jit(solution)/shard_map/ppermute | solution.py:551
  28.6 2.9 %collective-permute-start.12 = (bf16[16,4352]{1,0:T(8,128)(2,1)S(1)}, bf16[16,4352]{1,0:T(8,128)(2,1)S(1)}, u32[]{:S(2)}, u32[]{:S(2)}) collective-permute-start(bf16[16,4352]{1,0:T(8,128)(2,1)S(1)} %get-tuple-element.117), channel_id=1, source_target_pairs={{0,6},{2,4},{4,2},{6,0},{1,7},{3,5},{5,3},{7,1},{8,14},{10,12},{12... | collective-permute-start | bytes 417800 | tf_op jit(solution)/shard_map/ppermute | solution.py:551
  31.5 5.3 %collective-permute-done.5.refs_1_ = bf16[16,4352]{1,0:T(8,128)(2,1)S(1)} collective-permute-done((bf16[16,4352]{1,0:T(8,128)(2,1)S(1)}, bf16[16,4352]{1,0:T(8,128)(2,1)S(1)}, u32[]{:S(2)}, u32[]{:S(2)}) %collective-permute-start.5) | collective-permute-done | bytes 139296 | tf_op jit(solution)/shard_map/ppermute | solution.py:551
  37.6 1.3 %collective-permute-start.7 = (bf16[16,4096]{1,0:T(8,128)(2,1)S(1)}, bf16[16,4096]{1,0:T(8,128)(2,1)S(1)}, u32[]{:S(2)}, u32[]{:S(2)}) collective-permute-start(bf16[16,4096]{1,0:T(8,128)(2,1)S(1)} %get-tuple-element.106), channel_id=1, source_target_pairs={{0,2},{2,0},{4,6},{6,4},{1,3},{3,1},{5,7},{7,5},{8,10},{10,8},{12,... | collective-permute-start | bytes 393224 | tf_op jit(solution)/shard_map/ppermute | solution.py:551
  38.9 2.3 %collective-permute-start.9 = (bf16[16,4096]{1,0:T(8,128)(2,1)S(1)}, bf16[16,4096]{1,0:T(8,128)(2,1)S(1)}, u32[]{:S(2)}, u32[]{:S(2)}) collective-permute-start(bf16[16,4096]{1,0:T(8,128)(2,1)S(1)} %get-tuple-element.108), channel_id=1, source_target_pairs={{0,6},{2,4},{4,2},{6,0},{1,7},{3,5},{5,3},{7,1},{8,14},{10,12},{12... | collective-permute-start | bytes 393224 | tf_op jit(solution)/shard_map/ppermute | solution.py:551
  41.2 1.7 %half_scores.3.mine_ref = f32[64,1280]{1,0:T(8,128)S(1)} custom-call(bf16[16,8448]{1,0:T(8,128)(2,1)S(1)} %get-tuple-element.98.refs_0_, bf16[16,8448]{1,0:T(8,128)(2,1)S(1)} %collective-permute-done.3.refs_1_, bf16[16,8448]{1,0:T(8,128)(2,1)S(1)} %collective-permute-done.4.refs_2_, bf16[16,8448]{1,0:T(8,128)(2,1)S(1)} %collective-permute-done.6.refs_3_, ...), custom_call_target="tpu_custom_call" | custom-call | tf_op jit(solution)/shard_map/half_scores/pallas_call | solution.py:340
  43.9 1.2 %collective-permute-done.8.refs_2_ = bf16[16,4096]{1,0:T(8,128)(2,1)S(1)} collective-permute-done((bf16[16,4096]{1,0:T(8,128)(2,1)S(1)}, bf16[16,4096]{1,0:T(8,128)(2,1)S(1)}, u32[]{:S(2)}, u32[]{:S(2)}) %collective-permute-start.8) | collective-permute-done | bytes 131104 | tf_op jit(solution)/shard_map/ppermute | solution.py:551
  45.1 1.8 %collective-permute-done.9.refs_3_ = bf16[16,4096]{1,0:T(8,128)(2,1)S(1)} collective-permute-done((bf16[16,4096]{1,0:T(8,128)(2,1)S(1)}, bf16[16,4096]{1,0:T(8,128)(2,1)S(1)}, u32[]{:S(2)}, u32[]{:S(2)}) %collective-permute-start.9) | collective-permute-done | bytes 131104 | tf_op jit(solution)/shard_map/ppermute | solution.py:551
  48.5 1.1 %collective-permute-done.13.theirs_ref = f32[64,1280]{1,0:T(8,128)S(1)} collective-permute-done((f32[64,1280]{1,0:T(8,128)S(1)}, f32[64,1280]{1,0:T(8,128)S(1)}, u32[]{:S(2)}, u32[]{:S(2)}) %collective-permute-start.13) | collective-permute-done | bytes 327712 | tf_op jit(solution)/shard_map/ppermute | solution.py:608
  49.6 1.2 %weighted_means.2 = (bf16[16,4224]{1,0:T(8,128)(2,1)S(1)}, bf16[16,4224]{1,0:T(8,128)(2,1)S(1)}, bf16[16,4224]{1,0:T(8,128)(2,1)S(1)}, bf16[16,4224]{1,0:T(8,128...) custom-call(f32[64,1280]{1,0:T(8,128)S(1)} %half_scores.5.mine_ref, ...), custom_call_target="tpu_custom_call" | custom-call | tf_op jit(solution)/shard_map/weighted_means/pallas_call | solution.py:421
  50.9 1.1 %collective-permute-start.14 = (bf16[16,4224]{1,0:T(8,128)(2,1)S(1)}, bf16[16,4224]{1,0:T(8,128)(2,1)S(1)}, u32[]{:S(2)}, u32[]{:S(2)}) collective-permute-start(bf16[16,4224]{1,0:T(8,128)(2,1)S(1)} %get-tuple-element.128), channel_id=1, source_target_pairs={{0,2},{2,0},{4,6},{6,4},{1,3},{3,1},{5,7},{7,5},{8,10},{10,8},{12,... | collective-permute-start | bytes 405512 | tf_op jit(solution)/shard_map/ppermute | solution.py:551
  52.2 2.2 %collective-permute-start.16 = (bf16[16,4224]{1,0:T(8,128)(2,1)S(1)}, bf16[16,4224]{1,0:T(8,128)(2,1)S(1)}, u32[]{:S(2)}, u32[]{:S(2)}) collective-permute-start(bf16[16,4224]{1,0:T(8,128)(2,1)S(1)} %get-tuple-element.130), channel_id=1, source_target_pairs={{0,6},{2,4},{4,2},{6,0},{1,7},{3,5},{5,3},{7,1},{8,14},{10,12},{12... | collective-permute-start | bytes 405512 | tf_op jit(solution)/shard_map/ppermute | solution.py:551
  54.4 1.0 %rest_of_means.1 = (bf16[16,4096]{1,0:T(8,128)(2,1)S(1)}, bf16[16,4096]{1,0:T(8,128)(2,1)S(1)}, bf16[16,4096]{1,0:T(8,128)(2,1)S(1)}, bf16[16,4096]{1,0:T(8,128)(2,1)S(1)}) custom-call(bf16[320,256]{1,0:T(8,128)(2,1)S(1)} %get-tuple-element.141.weight_ref, f32[64,128]{1,0:T(8,128)S(1)} %get-tuple-element.142.inverse_ref, ...), custom_call_target="tpu_custom_call" | custom-call | tf_op jit(solution)/shard_map/rest_of_means/pallas_call | solution.py:438
  55.4 1.1 %collective-permute-start.21 = (bf16[16,4096]{1,0:T(8,128)(2,1)S(1)}, bf16[16,4096]{1,0:T(8,128)(2,1)S(1)}, u32[]{:S(2)}, u32[]{:S(2)}) collective-permute-start(bf16[16,4096]{1,0:T(8,128)(2,1)S(1)} %get-tuple-element.144), channel_id=1, source_target_pairs={{0,2},{2,0},{4,6},{6,4},{1,3},{3,1},{5,7},{7,5},{8,10},{10,8},{12,... | collective-permute-start | bytes 393224 | tf_op jit(solution)/shard_map/ppermute | solution.py:551
  56.8 2.2 %collective-permute-start.23 = (bf16[16,4096]{1,0:T(8,128)(2,1)S(1)}, bf16[16,4096]{1,0:T(8,128)(2,1)S(1)}, u32[]{:S(2)}, u32[]{:S(2)}) collective-permute-start(bf16[16,4096]{1,0:T(8,128)(2,1)S(1)} %get-tuple-element.146), channel_id=1, source_target_pairs={{0,6},{2,4},{4,2},{6,0},{1,7},{3,5},{5,3},{7,1},{8,14},{10,12},{12... | collective-permute-start | bytes 393224 | tf_op jit(solution)/shard_map/ppermute | solution.py:551
  59.0 2.5 %weighted_means.3 = (bf16[16,8320]{1,0:T(8,128)(2,1)S(1)}, bf16[16,8320]{1,0:T(8,128)(2,1)S(1)}, bf16[16,8320]{1,0:T(8,128)(2,1)S(1)}, bf16[16,8320]{1,0:T(8,128...) custom-call(f32[64,1280]{1,0:T(8,128)S(1)} %half_scores.3.mine_ref, ...), custom_call_target="tpu_custom_call" | custom-call | tf_op jit(solution)/shard_map/weighted_means/pallas_call | solution.py:421
  62.4 1.2 %collective-permute-start.20 = (bf16[32,4224]{1,0:T(8,128)(2,1)S(1)}, bf16[32,4224]{1,0:T(8,128)(2,1)S(1)}, u32[]{:S(2)}, u32[]{:S(2)}) collective-permute-start(bf16[32,4224]{1,0:T(8,128)(2,1)S(1)} %get-tuple-element.139), channel_id=1, source_target_pairs={{0,8},{8,0},{1,9},{9,1},{2,10},{10,2},{3,11},{11,3},{4,12},{12,4},... | collective-permute-start | bytes 811016 | tf_op jit(solution)/shard_map/ppermute | solution.py:618
  64.2 1.6 %collective-permute-start.18 = (bf16[16,8320]{1,0:T(8,128)(2,1)S(1)}, bf16[16,8320]{1,0:T(8,128)(2,1)S(1)}, u32[]{:S(2)}, u32[]{:S(2)}) collective-permute-start(bf16[16,8320]{1,0:T(8,128)(2,1)S(1)} %get-tuple-element.133), channel_id=1, source_target_pairs={{0,4},{2,6},{4,0},{6,2},{1,5},{3,7},{5,1},{7,3},{8,12},{10,14},{12... | collective-permute-start | bytes 798728 | tf_op jit(solution)/shard_map/ppermute | solution.py:551
  65.8 1.4 %collective-permute-start.19 = (bf16[16,8320]{1,0:T(8,128)(2,1)S(1)}, bf16[16,8320]{1,0:T(8,128)(2,1)S(1)}, u32[]{:S(2)}, u32[]{:S(2)}) collective-permute-start(bf16[16,8320]{1,0:T(8,128)(2,1)S(1)} %get-tuple-element.134), channel_id=1, source_target_pairs={{0,6},{2,4},{4,2},{6,0},{1,7},{3,5},{5,3},{7,1},{8,14},{10,12},{12... | collective-permute-start | bytes 798728 | tf_op jit(solution)/shard_map/ppermute | solution.py:551
  67.2 2.4 %collective-permute-done.23.refs_3_ = bf16[16,4096]{1,0:T(8,128)(2,1)S(1)} collective-permute-done((bf16[16,4096]{1,0:T(8,128)(2,1)S(1)}, bf16[16,4096]{1,0:T(8,128)(2,1)S(1)}, u32[]{:S(2)}, u32[]{:S(2)}) %collective-permute-start.23) | collective-permute-done | bytes 131104 | tf_op jit(solution)/shard_map/ppermute | solution.py:551
  70.0 16.4 %collective-permute-done.24.refs_5_ = bf16[32,4096]{1,0:T(8,128)(2,1)S(1)} collective-permute-done((bf16[32,4096]{1,0:T(8,128)(2,1)S(1)}, bf16[32,4096]{1,0:T(8,128)(2,1)S(1)}, u32[]{:S(2)}, u32[]{:S(2)}) %collective-permute-start.24) | collective-permute-done | bytes 262176 | tf_op jit(solution)/shard_map/ppermute | solution.py:620
  86.5 2.6 %collective-permute-done.19.refs_3_ = bf16[16,8320]{1,0:T(8,128)(2,1)S(1)} collective-permute-done((bf16[16,8320]{1,0:T(8,128)(2,1)S(1)}, bf16[16,8320]{1,0:T(8,128)(2,1)S(1)}, u32[]{:S(2)}, u32[]{:S(2)}) %collective-permute-start.19) | collective-permute-done | bytes 266272 | tf_op jit(solution)/shard_map/ppermute | solution.py:551
  89.1 1.8 %final_mix.1 = bf16[32,8192]{1,0:T(8,128)(2,1)} custom-call(f32[32,64]{1,0:T(8,128)S(1)} %get-tuple-element.78.choice_ref, bf16[16,8320]{1,0:T(8,128)(2,1)S(1)} %get-tuple-element.131.refs_0_, bf16[16,8320]{1,0:T(8,128)(2,1)S(1)} %collective-permute-done.17.refs_1_, bf16[16,8320]{1,0:T(8,128)(2,1)S(1)} %collective-permute-done.18.refs_2_, ...), custom_call_target="tpu_custom_call" | custom-call | tf_op jit(solution)/shard_map/final_mix/pallas_call | solution.py:538
  (33 shorter events, 7.3 us)
Async XLA Ops:
  0.0 10.2 %collective-permute-start.2 = (bf16[1,128,16384]{2,1,0:T(8,128)(2,1)}, bf16[1,128,16384]{2,1,0:T(8,128)(2,1)}, u32[]{:S(2)}, u32[]{:S(2)}) collective-permute-start(bf16[1,128,16384]{2,1,0:T(8,128)(2,1)} %mine_ref.1), channel_id=1, source_target_pairs={{0,1},{1,0},{2,3},{3,2},{4,5},{5,4},{6,7},{7,6},{8,9},{9,8},{10,11... | collective-permute-start | bytes 12582920 | tf_op jit(solution)/shard_map/ppermute | solution.py:587
  1.6 17.2 %collective-permute-start.1 = (bf16[32,4352]{1,0:T(8,128)(2,1)S(1)}, bf16[32,4352]{1,0:T(8,128)(2,1)S(1)}, u32[]{:S(2)}, u32[]{:S(2)}) collective-permute-start(bf16[32,4352]{1,0:T(8,128)(2,1)S(1)} %get-tuple-element.76.refs_0_), channel_id=1, source_target_pairs={{0,8},{8,0},{1,9},{9,1},{2,10},{10,2},{3,11},{11,3},{4,12},{12,4},... | collective-permute-start | bytes 835592 | tf_op jit(solution)/shard_map/ppermute | solution.py:582
  6.6 13.4 %collective-permute-start.3 = (bf16[16,8448]{1,0:T(8,128)(2,1)S(1)}, bf16[16,8448]{1,0:T(8,128)(2,1)S(1)}, u32[]{:S(2)}, u32[]{:S(2)}) collective-permute-start(bf16[16,8448]{1,0:T(8,128)(2,1)S(1)} %get-tuple-element.86), channel_id=1, source_target_pairs={{0,2},{2,0},{4,6},{6,4},{1,3},{3,1},{5,7},{7,5},{8,10},{10,8},{12,... | collective-permute-start | bytes 811016 | tf_op jit(solution)/shard_map/ppermute | solution.py:551
  8.2 19.8 %collective-permute-start.4 = (bf16[16,8448]{1,0:T(8,128)(2,1)S(1)}, bf16[16,8448]{1,0:T(8,128)(2,1)S(1)}, u32[]{:S(2)}, u32[]{:S(2)}) collective-permute-start(bf16[16,8448]{1,0:T(8,128)(2,1)S(1)} %get-tuple-element.87), channel_id=1, source_target_pairs={{0,4},{2,6},{4,0},{6,2},{1,5},{3,7},{5,1},{7,3},{8,12},{10,14},{12... | collective-permute-start | bytes 811016 | tf_op jit(solution)/shard_map/ppermute | solution.py:551
  9.8 27.8 %collective-permute-start.6 = (bf16[16,8448]{1,0:T(8,128)(2,1)S(1)}, bf16[16,8448]{1,0:T(8,128)(2,1)S(1)}, u32[]{:S(2)}, u32[]{:S(2)}) collective-permute-start(bf16[16,8448]{1,0:T(8,128)(2,1)S(1)} %get-tuple-element.97), channel_id=1, source_target_pairs={{0,6},{2,4},{4,2},{6,0},{1,7},{3,5},{5,3},{7,1},{8,14},{10,12},{12... | collective-permute-start | bytes 811016 | tf_op jit(solution)/shard_map/ppermute | solution.py:551
  10.2 26.5 %collective-permute-start = (bf16[32,4096]{1,0:T(8,128)(2,1)S(1)}, bf16[32,4096]{1,0:T(8,128)(2,1)S(1)}, u32[]{:S(2)}, u32[]{:S(2)}) collective-permute-start(bf16[32,4096]{1,0:T(8,128)(2,1)S(1)} %get-tuple-element.77.refs_1_), channel_id=1, source_target_pairs={{0,8},{8,0},{1,9},{9,1},{2,10},{10,2},{3,11},{11,3},{4,12},{12,4},... | collective-permute-start | bytes 786440 | tf_op jit(solution)/shard_map/ppermute | solution.py:582
  28.0 8.8 %collective-permute-start.5 = (bf16[16,4352]{1,0:T(8,128)(2,1)S(1)}, bf16[16,4352]{1,0:T(8,128)(2,1)S(1)}, u32[]{:S(2)}, u32[]{:S(2)}) collective-permute-start(bf16[16,4352]{1,0:T(8,128)(2,1)S(1)} %get-tuple-element.88), channel_id=1, source_target_pairs={{0,2},{2,0},{4,6},{6,4},{1,3},{3,1},{5,7},{7,5},{8,10},{10,8},{12,... | collective-permute-start | bytes 417800 | tf_op jit(solution)/shard_map/ppermute | solution.py:551
  28.6 14.3 %collective-permute-start.11 = (bf16[16,4352]{1,0:T(8,128)(2,1)S(1)}, bf16[16,4352]{1,0:T(8,128)(2,1)S(1)}, u32[]{:S(2)}, u32[]{:S(2)}) collective-permute-start(bf16[16,4352]{1,0:T(8,128)(2,1)S(1)} %get-tuple-element.116), channel_id=1, source_target_pairs={{0,4},{2,6},{4,0},{6,2},{1,5},{3,7},{5,1},{7,3},{8,12},{10,14},{12... | collective-permute-start | bytes 417800 | tf_op jit(solution)/shard_map/ppermute | solution.py:551
  28.6 14.3 %collective-permute-start.12 = (bf16[16,4352]{1,0:T(8,128)(2,1)S(1)}, bf16[16,4352]{1,0:T(8,128)(2,1)S(1)}, u32[]{:S(2)}, u32[]{:S(2)}) collective-permute-start(bf16[16,4352]{1,0:T(8,128)(2,1)S(1)} %get-tuple-element.117), channel_id=1, source_target_pairs={{0,6},{2,4},{4,2},{6,0},{1,7},{3,5},{5,3},{7,1},{8,14},{10,12},{12... | collective-permute-start | bytes 417800 | tf_op jit(solution)/shard_map/ppermute | solution.py:551
  37.6 6.3 %collective-permute-start.7 = (bf16[16,4096]{1,0:T(8,128)(2,1)S(1)}, bf16[16,4096]{1,0:T(8,128)(2,1)S(1)}, u32[]{:S(2)}, u32[]{:S(2)}) collective-permute-start(bf16[16,4096]{1,0:T(8,128)(2,1)S(1)} %get-tuple-element.106), channel_id=1, source_target_pairs={{0,2},{2,0},{4,6},{6,4},{1,3},{3,1},{5,7},{7,5},{8,10},{10,8},{12,... | collective-permute-start | bytes 393224 | tf_op jit(solution)/shard_map/ppermute | solution.py:551
  38.9 6.2 %collective-permute-start.8 = (bf16[16,4096]{1,0:T(8,128)(2,1)S(1)}, bf16[16,4096]{1,0:T(8,128)(2,1)S(1)}, u32[]{:S(2)}, u32[]{:S(2)}) collective-permute-start(bf16[16,4096]{1,0:T(8,128)(2,1)S(1)} %get-tuple-element.107), channel_id=1, source_target_pairs={{0,4},{2,6},{4,0},{6,2},{1,5},{3,7},{5,1},{7,3},{8,12},{10,14},{12... | collective-permute-start | bytes 393224 | tf_op jit(solution)/shard_map/ppermute | solution.py:551
  38.9 8.1 %collective-permute-start.9 = (bf16[16,4096]{1,0:T(8,128)(2,1)S(1)}, bf16[16,4096]{1,0:T(8,128)(2,1)S(1)}, u32[]{:S(2)}, u32[]{:S(2)}) collective-permute-start(bf16[16,4096]{1,0:T(8,128)(2,1)S(1)} %get-tuple-element.108), channel_id=1, source_target_pairs={{0,6},{2,4},{4,2},{6,0},{1,7},{3,5},{5,3},{7,1},{8,14},{10,12},{12... | collective-permute-start | bytes 393224 | tf_op jit(solution)/shard_map/ppermute | solution.py:551
  48.0 1.7 %collective-permute-start.13 = (f32[64,1280]{1,0:T(8,128)S(1)}, f32[64,1280]{1,0:T(8,128)S(1)}, u32[]{:S(2)}, u32[]{:S(2)}) collective-permute-start(f32[64,1280]{1,0:T(8,128)S(1)} %half_scores.5.mine_ref), channel_id=1, source_target_pairs={{0,1},{1,0},{2,3},{3,2},{4,5},{5,4},{6,7},{7,6},{8,9},{9,8},{10,11... | collective-permute-start | bytes 983048 | tf_op jit(solution)/shard_map/ppermute | solution.py:608
  48.0 2.8 %collective-permute-start.10 = (f32[64,1280]{1,0:T(8,128)S(1)}, f32[64,1280]{1,0:T(8,128)S(1)}, u32[]{:S(2)}, u32[]{:S(2)}) collective-permute-start(f32[64,1280]{1,0:T(8,128)S(1)} %half_scores.3.mine_ref), channel_id=1, source_target_pairs={{0,1},{1,0},{2,3},{3,2},{4,5},{5,4},{6,7},{7,6},{8,9},{9,8},{10,11... | collective-permute-start | bytes 983048 | tf_op jit(solution)/shard_map/ppermute | solution.py:610
  50.9 6.0 %collective-permute-start.14 = (bf16[16,4224]{1,0:T(8,128)(2,1)S(1)}, bf16[16,4224]{1,0:T(8,128)(2,1)S(1)}, u32[]{:S(2)}, u32[]{:S(2)}) collective-permute-start(bf16[16,4224]{1,0:T(8,128)(2,1)S(1)} %get-tuple-element.128), channel_id=1, source_target_pairs={{0,2},{2,0},{4,6},{6,4},{1,3},{3,1},{5,7},{7,5},{8,10},{10,8},{12,... | collective-permute-start | bytes 405512 | tf_op jit(solution)/shard_map/ppermute | solution.py:551
  51.9 9.6 %collective-permute-start.15 = (bf16[16,4224]{1,0:T(8,128)(2,1)S(1)}, bf16[16,4224]{1,0:T(8,128)(2,1)S(1)}, u32[]{:S(2)}, u32[]{:S(2)}) collective-permute-start(bf16[16,4224]{1,0:T(8,128)(2,1)S(1)} %get-tuple-element.129), channel_id=1, source_target_pairs={{0,4},{2,6},{4,0},{6,2},{1,5},{3,7},{5,1},{7,3},{8,12},{10,14},{12... | collective-permute-start | bytes 405512 | tf_op jit(solution)/shard_map/ppermute | solution.py:551
  52.2 9.5 %collective-permute-start.16 = (bf16[16,4224]{1,0:T(8,128)(2,1)S(1)}, bf16[16,4224]{1,0:T(8,128)(2,1)S(1)}, u32[]{:S(2)}, u32[]{:S(2)}) collective-permute-start(bf16[16,4224]{1,0:T(8,128)(2,1)S(1)} %get-tuple-element.130), channel_id=1, source_target_pairs={{0,6},{2,4},{4,2},{6,0},{1,7},{3,5},{5,3},{7,1},{8,14},{10,12},{12... | collective-permute-start | bytes 405512 | tf_op jit(solution)/shard_map/ppermute | solution.py:551
  55.4 8.7 %collective-permute-start.21 = (bf16[16,4096]{1,0:T(8,128)(2,1)S(1)}, bf16[16,4096]{1,0:T(8,128)(2,1)S(1)}, u32[]{:S(2)}, u32[]{:S(2)}) collective-permute-start(bf16[16,4096]{1,0:T(8,128)(2,1)S(1)} %get-tuple-element.144), channel_id=1, source_target_pairs={{0,2},{2,0},{4,6},{6,4},{1,3},{3,1},{5,7},{7,5},{8,10},{10,8},{12,... | collective-permute-start | bytes 393224 | tf_op jit(solution)/shard_map/ppermute | solution.py:551
  56.5 9.2 %collective-permute-start.22 = (bf16[16,4096]{1,0:T(8,128)(2,1)S(1)}, bf16[16,4096]{1,0:T(8,128)(2,1)S(1)}, u32[]{:S(2)}, u32[]{:S(2)}) collective-permute-start(bf16[16,4096]{1,0:T(8,128)(2,1)S(1)} %get-tuple-element.145), channel_id=1, source_target_pairs={{0,4},{2,6},{4,0},{6,2},{1,5},{3,7},{5,1},{7,3},{8,12},{10,14},{12... | collective-permute-start | bytes 393224 | tf_op jit(solution)/shard_map/ppermute | solution.py:551
  56.8 12.8 %collective-permute-start.23 = (bf16[16,4096]{1,0:T(8,128)(2,1)S(1)}, bf16[16,4096]{1,0:T(8,128)(2,1)S(1)}, u32[]{:S(2)}, u32[]{:S(2)}) collective-permute-start(bf16[16,4096]{1,0:T(8,128)(2,1)S(1)} %get-tuple-element.146), channel_id=1, source_target_pairs={{0,6},{2,4},{4,2},{6,0},{1,7},{3,5},{5,3},{7,1},{8,14},{10,12},{12... | collective-permute-start | bytes 393224 | tf_op jit(solution)/shard_map/ppermute | solution.py:551
  62.4 26.6 %collective-permute-start.20 = (bf16[32,4224]{1,0:T(8,128)(2,1)S(1)}, bf16[32,4224]{1,0:T(8,128)(2,1)S(1)}, u32[]{:S(2)}, u32[]{:S(2)}) collective-permute-start(bf16[32,4224]{1,0:T(8,128)(2,1)S(1)} %get-tuple-element.139), channel_id=1, source_target_pairs={{0,8},{8,0},{1,9},{9,1},{2,10},{10,2},{3,11},{11,3},{4,12},{12,4},... | collective-permute-start | bytes 811016 | tf_op jit(solution)/shard_map/ppermute | solution.py:618
  63.7 22.8 %collective-permute-start.17 = (bf16[16,8320]{1,0:T(8,128)(2,1)S(1)}, bf16[16,8320]{1,0:T(8,128)(2,1)S(1)}, u32[]{:S(2)}, u32[]{:S(2)}) collective-permute-start(bf16[16,8320]{1,0:T(8,128)(2,1)S(1)} %get-tuple-element.132), channel_id=1, source_target_pairs={{0,2},{2,0},{4,6},{6,4},{1,3},{3,1},{5,7},{7,5},{8,10},{10,8},{12,... | collective-permute-start | bytes 798728 | tf_op jit(solution)/shard_map/ppermute | solution.py:551
  64.2 22.3 %collective-permute-start.18 = (bf16[16,8320]{1,0:T(8,128)(2,1)S(1)}, bf16[16,8320]{1,0:T(8,128)(2,1)S(1)}, u32[]{:S(2)}, u32[]{:S(2)}) collective-permute-start(bf16[16,8320]{1,0:T(8,128)(2,1)S(1)} %get-tuple-element.133), channel_id=1, source_target_pairs={{0,4},{2,6},{4,0},{6,2},{1,5},{3,7},{5,1},{7,3},{8,12},{10,14},{12... | collective-permute-start | bytes 798728 | tf_op jit(solution)/shard_map/ppermute | solution.py:551
  65.8 23.3 %collective-permute-start.19 = (bf16[16,8320]{1,0:T(8,128)(2,1)S(1)}, bf16[16,8320]{1,0:T(8,128)(2,1)S(1)}, u32[]{:S(2)}, u32[]{:S(2)}) collective-permute-start(bf16[16,8320]{1,0:T(8,128)(2,1)S(1)} %get-tuple-element.134), channel_id=1, source_target_pairs={{0,6},{2,4},{4,2},{6,0},{1,7},{3,5},{5,3},{7,1},{8,14},{10,12},{12... | collective-permute-start | bytes 798728 | tf_op jit(solution)/shard_map/ppermute | solution.py:551
  70.0 16.5 %collective-permute-start.24 = (bf16[32,4096]{1,0:T(8,128)(2,1)S(1)}, bf16[32,4096]{1,0:T(8,128)(2,1)S(1)}, u32[]{:S(2)}, u32[]{:S(2)}) collective-permute-start(bf16[32,4096]{1,0:T(8,128)(2,1)S(1)} %rest_of_mix.1), channel_id=1, source_target_pairs={{0,8},{8,0},{1,9},{9,1},{2,10},{10,2},{3,11},{11,3},{4,12},{12,4},... | collective-permute-start | bytes 786440 | tf_op jit(solution)/shard_map/ppermute | solution.py:620

commit v5 on v4

--- a/solution.py
+++ b/solution.py
@@ -557,6 +557,13 @@
     return [parts.reshape(whole.shape)]
 
 
+def hold_back(early, late, part):
+    held, late = lax.optimization_barrier((early[part], late))
+    early = list(early)
+    early[part] = held
+    return early, late
+
+
 def on_device(particles, tau, candidates, prune, projections):
     halves = lax.axis_size("hi")
     peers = lax.axis_size("lo")
@@ -590,7 +597,7 @@
     views = (own_views, other_views)
 
     sent_far, choice_far = pack(place, far_payload[:1], pieces, peers, cap, choose)
-    sent_far, records_near[1:3] = lax.optimization_barrier((sent_far, records_near[1:3]))
+    records_near, sent_far = hold_back(records_near, sent_far, slice(1, 2))
     records_far = trade(sent_far, peers)
     choice_far, records_far[1 % len(records_far)] = lax.optimization_barrier(
         (choice_far, records_far[1 % len(records_far)])

time: 91.1 us -> 88.5 us (0.971)
  waiting for transfers between devices: 43.2 us -> 37.1 us
  starting transfers between devices: 28.5 us -> 32 us
    ppermute x18, waiting for transfers between devices: 21.6 us -> 15.1 us  [trade(): lax.ppermute(pieces[flip], 'lo', [(i, i ^ flip) for i in range(peers)])]
    ppermute x18, starting transfers between devices: 21.2 us -> 24.2 us  [trade(): lax.ppermute(pieces[flip], 'lo', [(i, i ^ flip) for i in range(peers)])]
  transfers between devices with their start and end apart: 25 -> 25, of which waited for: 10 -> 11; matrix products, arithmetic and copies ran while one was open for 0% -> 0% of each run, Pallas kernels for 18% -> 18%
where the time goes in v5:
time: 88.5 us; the launch traced here: 88.3 us
  waiting for transfers between devices  37.1 us (42%)
  starting transfers between devices  32 us (36%)
  Pallas kernels  19 us (21%)
    ppermute x18, starting transfers between devices, trade(): lax.ppermute(pieces[flip], 'lo', [(i, i ^ flip) for i in range(peers)])  24.2 us
    ppermute x1, waiting for transfers between devices, on_device(): rest_part = lax.ppermute(rest_mix, 'hi', across)  16.9 us
    ppermute x18, waiting for transfers between devices, trade(): lax.ppermute(pieces[flip], 'lo', [(i, i ^ flip) for i in range(peers)])  15.1 us
    ppermute x2, starting transfers between devices, on_device(): far_payload = [lax.ppermute(chunk, 'hi', across) for chunk in payload]  5 us
    ppermute x2, waiting for transfers between devices, on_device(): far_payload = [lax.ppermute(chunk, 'hi', across) for chunk in payload]  4 us
    pallas_call x2, Pallas kernels, weighted_means(): pl.pallas_call(functools.partial(mean_kernel, chunk=chunk, pieces=pieces)...  3.7 us
    pallas_call x3, Pallas kernels, half_scores(): pl.pallas_call(functools.partial(score_kernel, pieces=len(records), spans...  3.66 us
    pallas_call x3, Pallas kernels, pack(): pl.pallas_call(functools.partial(pack_kernel, sources=len(chunks), classe...  3.35 us
  transfers between devices with their start and end apart: 25, of which 11 were waited for; matrix products, arithmetic and copies ran while one was open for 0% of the time, Pallas kernels for 18%

profile of v5, /device:TPU:0, one launch (start us, length us, event | category | flops | bytes accessed | tf_op | source)
XLA Modules:
  0.0 88.3 jit_solution(4994845913199623824)
XLA Ops:
  0.5 1.1 %make_payload.1 = (bf16[32,4352]{1,0:T(8,128)(2,1)S(1)}, bf16[32,4096]{1,0:T(8,128)(2,1)S(1)}) custom-call(s32[1]{0:T(128)} %bitcast.2.core_ref, bf16[32,16384]{1,0:T(8,128)(2,1)} %x_ref.1, bf16[1,32]{1,0:T(2,128)(2,1)} %bitcast.6, s32[2,32]{1,0:T(2,128)} %bitcast.5, s32[32,128]{1,0:T(8,128)} %keep_ref.1), custom_call_target="tpu_custom_call" | custom-call | tf_op jit(solution)/shard_map/make_payload/pallas_call | solution.py:143
  1.6 3.7 %collective-permute-start.1 = (bf16[32,4352]{1,0:T(8,128)(2,1)S(1)}, bf16[32,4352]{1,0:T(8,128)(2,1)S(1)}, u32[]{:S(2)}, u32[]{:S(2)}) collective-permute-start(bf16[32,4352]{1,0:T(8,128)(2,1)S(1)} %get-tuple-element.75.refs_0_), channel_id=1, source_target_pairs={{0,8},{8,0},{1,9},{9,1},{2,10},{10,2},{3,11},{11,3},{4,12},{12,4},... | collective-permute-start | bytes 835592 | tf_op jit(solution)/shard_map/ppermute | solution.py:589
  5.3 1.3 %pack.2 = (bf16[16,8448]{1,0:T(8,128)(2,1)S(1)}, bf16[16,8448]{1,0:T(8,128)(2,1)S(1)}, bf16[16,8448]{1,0:T(8,128)(2,1)S(1)}, bf16[16,8448]{1,0:T(8,128)(2,1)S(1)}, f32[32,64]{1,0:T(8,128)S(1)}) custom-call(s32[2]{0:T(128)S(1)} %pad_add_fusion.place_ref, bf16[32,4352]{1,0:T(8,128)(2,1)S(1)} %get-tuple-element.75.refs_0_, ...), custom_call_target="tpu_custom_call" | custom-call | tf_op jit(solution)/shard_map/pack/pallas_call | solution.py:223
  6.6 1.6 %collective-permute-start.3 = (bf16[16,8448]{1,0:T(8,128)(2,1)S(1)}, bf16[16,8448]{1,0:T(8,128)(2,1)S(1)}, u32[]{:S(2)}, u32[]{:S(2)}) collective-permute-start(bf16[16,8448]{1,0:T(8,128)(2,1)S(1)} %get-tuple-element.81), channel_id=1, source_target_pairs={{0,2},{2,0},{4,6},{6,4},{1,3},{3,1},{5,7},{7,5},{8,10},{10,8},{12,... | collective-permute-start | bytes 811016 | tf_op jit(solution)/shard_map/ppermute | solution.py:551
  8.2 1.6 %collective-permute-start.5 = (bf16[16,8448]{1,0:T(8,128)(2,1)S(1)}, bf16[16,8448]{1,0:T(8,128)(2,1)S(1)}, u32[]{:S(2)}, u32[]{:S(2)}) collective-permute-start(bf16[16,8448]{1,0:T(8,128)(2,1)S(1)} %get-tuple-element.94), channel_id=1, source_target_pairs={{0,4},{2,6},{4,0},{6,2},{1,5},{3,7},{5,1},{7,3},{8,12},{10,14},{12... | collective-permute-start | bytes 811016 | tf_op jit(solution)/shard_map/ppermute | solution.py:551
  10.2 1.3 %collective-permute-start = (bf16[32,4096]{1,0:T(8,128)(2,1)S(1)}, bf16[32,4096]{1,0:T(8,128)(2,1)S(1)}, u32[]{:S(2)}, u32[]{:S(2)}) collective-permute-start(bf16[32,4096]{1,0:T(8,128)(2,1)S(1)} %get-tuple-element.76.refs_1_), channel_id=1, source_target_pairs={{0,8},{8,0},{1,9},{9,1},{2,10},{10,2},{3,11},{11,3},{4,12},{12,4},... | collective-permute-start | bytes 786440 | tf_op jit(solution)/shard_map/ppermute | solution.py:589
  11.5 3.3 %make_views.1 = (bf16[128,8448]{1,0:T(8,128)(2,1)S(1)}, bf16[128,8448]{1,0:T(8,128)(2,1)S(1)}, f32[1,128]{1,0:T(1,128)S(1)}) custom-call(s32[1]{0:T(128)} %bitcast.2.core_ref, bf16[1,128,16384]{2,1,0:T(8,128)(2,1)} %mine_ref.1, bf16[1,128,16384]{2,1,0:T(8,128)(2,1)} %collective-permute-done.2.theirs_ref), custom_call_target="tpu_custom_call" | custom-call | tf_op jit(solution)/shard_map/make_views/pallas_call | solution.py:279
  14.8 4.0 %collective-permute-done.1.refs_0_ = bf16[32,4352]{1,0:T(8,128)(2,1)S(1)} collective-permute-done((bf16[32,4352]{1,0:T(8,128)(2,1)S(1)}, bf16[32,4352]{1,0:T(8,128)(2,1)S(1)}, u32[]{:S(2)}, u32[]{:S(2)}) %collective-permute-start.1) | collective-permute-done | bytes 278560 | tf_op jit(solution)/shard_map/ppermute | solution.py:589
  18.8 1.2 %pack.3 = (bf16[16,4352]{1,0:T(8,128)(2,1)S(1)}, bf16[16,4352]{1,0:T(8,128)(2,1)S(1)}, bf16[16,4352]{1,0:T(8,128)(2,1)S(1)}, bf16[16,4352]{1,0:T(8,128)(2,1)S(1)}, f32[32,64]{1,0:T(8,128)S(1)}) custom-call(s32[2]{0:T(128)S(1)} %pad_add_fusion.place_ref, bf16[32,4352]{1,0:T(8,128)(2,1)S(1)} %collective-permute-done.1.refs_0_), custom_call_target="tpu_custom_call" | custom-call | tf_op jit(solution)/shard_map/pack/pallas_call | solution.py:223
  20.0 1.8 %collective-permute-start.4 = (bf16[16,4352]{1,0:T(8,128)(2,1)S(1)}, bf16[16,4352]{1,0:T(8,128)(2,1)S(1)}, u32[]{:S(2)}, u32[]{:S(2)}) collective-permute-start(bf16[16,4352]{1,0:T(8,128)(2,1)S(1)} %get-tuple-element.86), channel_id=1, source_target_pairs={{0,2},{2,0},{4,6},{6,4},{1,3},{3,1},{5,7},{7,5},{8,10},{10,8},{12,... | collective-permute-start | bytes 417800 | tf_op jit(solution)/shard_map/ppermute | solution.py:551
  22.1 3.3 %collective-permute-done.4.refs_1_ = bf16[16,4352]{1,0:T(8,128)(2,1)S(1)} collective-permute-done((bf16[16,4352]{1,0:T(8,128)(2,1)S(1)}, bf16[16,4352]{1,0:T(8,128)(2,1)S(1)}, u32[]{:S(2)}, u32[]{:S(2)}) %collective-permute-start.4) | collective-permute-done | bytes 139296 | tf_op jit(solution)/shard_map/ppermute | solution.py:551
  25.4 4.5 %collective-permute-start.12 = (bf16[16,4352]{1,0:T(8,128)(2,1)S(1)}, bf16[16,4352]{1,0:T(8,128)(2,1)S(1)}, u32[]{:S(2)}, u32[]{:S(2)}) collective-permute-start(bf16[16,4352]{1,0:T(8,128)(2,1)S(1)} %get-tuple-element.115), channel_id=1, source_target_pairs={{0,6},{2,4},{4,2},{6,0},{1,7},{3,5},{5,3},{7,1},{8,14},{10,12},{12... | collective-permute-start | bytes 417800 | tf_op jit(solution)/shard_map/ppermute | solution.py:551
  30.7 3.1 %collective-permute-done.6.refs_3_ = bf16[16,8448]{1,0:T(8,128)(2,1)S(1)} collective-permute-done((bf16[16,8448]{1,0:T(8,128)(2,1)S(1)}, bf16[16,8448]{1,0:T(8,128)(2,1)S(1)}, u32[]{:S(2)}, u32[]{:S(2)}) %collective-permute-start.6) | collective-permute-done | bytes 270368 | tf_op jit(solution)/shard_map/ppermute | solution.py:551
  33.8 1.4 %collective-permute-start.7 = (bf16[16,4096]{1,0:T(8,128)(2,1)S(1)}, bf16[16,4096]{1,0:T(8,128)(2,1)S(1)}, u32[]{:S(2)}, u32[]{:S(2)}) collective-permute-start(bf16[16,4096]{1,0:T(8,128)(2,1)S(1)} %get-tuple-element.104), channel_id=1, source_target_pairs={{0,2},{2,0},{4,6},{6,4},{1,3},{3,1},{5,7},{7,5},{8,10},{10,8},{12,... | collective-permute-start | bytes 393224 | tf_op jit(solution)/shard_map/ppermute | solution.py:551
  35.2 2.0 %collective-permute-start.9 = (bf16[16,4096]{1,0:T(8,128)(2,1)S(1)}, bf16[16,4096]{1,0:T(8,128)(2,1)S(1)}, u32[]{:S(2)}, u32[]{:S(2)}) collective-permute-start(bf16[16,4096]{1,0:T(8,128)(2,1)S(1)} %get-tuple-element.106), channel_id=1, source_target_pairs={{0,6},{2,4},{4,2},{6,0},{1,7},{3,5},{5,3},{7,1},{8,14},{10,12},{12... | collective-permute-start | bytes 393224 | tf_op jit(solution)/shard_map/ppermute | solution.py:551
  37.3 1.7 %half_scores.3.mine_ref = f32[64,1280]{1,0:T(8,128)S(1)} custom-call(bf16[16,8448]{1,0:T(8,128)(2,1)S(1)} %get-tuple-element.96.refs_0_, bf16[16,8448]{1,0:T(8,128)(2,1)S(1)} %collective-permute-done.3.refs_1_, bf16[16,8448]{1,0:T(8,128)(2,1)S(1)} %collective-permute-done.5.refs_2_, bf16[16,8448]{1,0:T(8,128)(2,1)S(1)} %collective-permute-done.6.refs_3_, ...), custom_call_target="tpu_custom_call" | custom-call | tf_op jit(solution)/shard_map/half_scores/pallas_call | solution.py:340
  40.8 1.8 %collective-permute-done.8.refs_2_ = bf16[16,4096]{1,0:T(8,128)(2,1)S(1)} collective-permute-done((bf16[16,4096]{1,0:T(8,128)(2,1)S(1)}, bf16[16,4096]{1,0:T(8,128)(2,1)S(1)}, u32[]{:S(2)}, u32[]{:S(2)}) %collective-permute-start.8) | collective-permute-done | bytes 131104 | tf_op jit(solution)/shard_map/ppermute | solution.py:551
  42.6 1.8 %collective-permute-done.9.refs_3_ = bf16[16,4096]{1,0:T(8,128)(2,1)S(1)} collective-permute-done((bf16[16,4096]{1,0:T(8,128)(2,1)S(1)}, bf16[16,4096]{1,0:T(8,128)(2,1)S(1)}, u32[]{:S(2)}, u32[]{:S(2)}) %collective-permute-start.9) | collective-permute-done | bytes 131104 | tf_op jit(solution)/shard_map/ppermute | solution.py:551
  45.9 1.1 %collective-permute-done.13.theirs_ref = f32[64,1280]{1,0:T(8,128)S(1)} collective-permute-done((f32[64,1280]{1,0:T(8,128)S(1)}, f32[64,1280]{1,0:T(8,128)S(1)}, u32[]{:S(2)}, u32[]{:S(2)}) %collective-permute-start.13) | collective-permute-done | bytes 327712 | tf_op jit(solution)/shard_map/ppermute | solution.py:615
  47.1 1.2 %weighted_means.2 = (bf16[16,4224]{1,0:T(8,128)(2,1)S(1)}, bf16[16,4224]{1,0:T(8,128)(2,1)S(1)}, bf16[16,4224]{1,0:T(8,128)(2,1)S(1)}, bf16[16,4224]{1,0:T(8,128...) custom-call(f32[64,1280]{1,0:T(8,128)S(1)} %half_scores.5.mine_ref, ...), custom_call_target="tpu_custom_call" | custom-call | tf_op jit(solution)/shard_map/weighted_means/pallas_call | solution.py:421
  48.3 1.5 %collective-permute-start.14 = (bf16[16,4224]{1,0:T(8,128)(2,1)S(1)}, bf16[16,4224]{1,0:T(8,128)(2,1)S(1)}, u32[]{:S(2)}, u32[]{:S(2)}) collective-permute-start(bf16[16,4224]{1,0:T(8,128)(2,1)S(1)} %get-tuple-element.126), channel_id=1, source_target_pairs={{0,2},{2,0},{4,6},{6,4},{1,3},{3,1},{5,7},{7,5},{8,10},{10,8},{12,... | collective-permute-start | bytes 405512 | tf_op jit(solution)/shard_map/ppermute | solution.py:551
  49.8 2.0 %collective-permute-start.16 = (bf16[16,4224]{1,0:T(8,128)(2,1)S(1)}, bf16[16,4224]{1,0:T(8,128)(2,1)S(1)}, u32[]{:S(2)}, u32[]{:S(2)}) collective-permute-start(bf16[16,4224]{1,0:T(8,128)(2,1)S(1)} %get-tuple-element.128), channel_id=1, source_target_pairs={{0,6},{2,4},{4,2},{6,0},{1,7},{3,5},{5,3},{7,1},{8,14},{10,12},{12... | collective-permute-start | bytes 405512 | tf_op jit(solution)/shard_map/ppermute | solution.py:551
  52.8 1.5 %collective-permute-start.21 = (bf16[16,4096]{1,0:T(8,128)(2,1)S(1)}, bf16[16,4096]{1,0:T(8,128)(2,1)S(1)}, u32[]{:S(2)}, u32[]{:S(2)}) collective-permute-start(bf16[16,4096]{1,0:T(8,128)(2,1)S(1)} %get-tuple-element.142), channel_id=1, source_target_pairs={{0,2},{2,0},{4,6},{6,4},{1,3},{3,1},{5,7},{7,5},{8,10},{10,8},{12,... | collective-permute-start | bytes 393224 | tf_op jit(solution)/shard_map/ppermute | solution.py:551
  54.4 2.0 %collective-permute-start.23 = (bf16[16,4096]{1,0:T(8,128)(2,1)S(1)}, bf16[16,4096]{1,0:T(8,128)(2,1)S(1)}, u32[]{:S(2)}, u32[]{:S(2)}) collective-permute-start(bf16[16,4096]{1,0:T(8,128)(2,1)S(1)} %get-tuple-element.144), channel_id=1, source_target_pairs={{0,6},{2,4},{4,2},{6,0},{1,7},{3,5},{5,3},{7,1},{8,14},{10,12},{12... | collective-permute-start | bytes 393224 | tf_op jit(solution)/shard_map/ppermute | solution.py:551
  56.4 2.5 %weighted_means.3 = (bf16[16,8320]{1,0:T(8,128)(2,1)S(1)}, bf16[16,8320]{1,0:T(8,128)(2,1)S(1)}, bf16[16,8320]{1,0:T(8,128)(2,1)S(1)}, bf16[16,8320]{1,0:T(8,128...) custom-call(f32[64,1280]{1,0:T(8,128)S(1)} %half_scores.3.mine_ref, ...), custom_call_target="tpu_custom_call" | custom-call | tf_op jit(solution)/shard_map/weighted_means/pallas_call | solution.py:421
  59.8 1.2 %collective-permute-start.20 = (bf16[32,4224]{1,0:T(8,128)(2,1)S(1)}, bf16[32,4224]{1,0:T(8,128)(2,1)S(1)}, u32[]{:S(2)}, u32[]{:S(2)}) collective-permute-start(bf16[32,4224]{1,0:T(8,128)(2,1)S(1)} %get-tuple-element.137), channel_id=1, source_target_pairs={{0,8},{8,0},{1,9},{9,1},{2,10},{10,2},{3,11},{11,3},{4,12},{12,4},... | collective-permute-start | bytes 811016 | tf_op jit(solution)/shard_map/ppermute | solution.py:625
  61.1 1.2 %collective-permute-start.17 = (bf16[16,8320]{1,0:T(8,128)(2,1)S(1)}, bf16[16,8320]{1,0:T(8,128)(2,1)S(1)}, u32[]{:S(2)}, u32[]{:S(2)}) collective-permute-start(bf16[16,8320]{1,0:T(8,128)(2,1)S(1)} %get-tuple-element.130), channel_id=1, source_target_pairs={{0,2},{2,0},{4,6},{6,4},{1,3},{3,1},{5,7},{7,5},{8,10},{10,8},{12,... | collective-permute-start | bytes 798728 | tf_op jit(solution)/shard_map/ppermute | solution.py:551
  62.3 2.0 %collective-permute-start.18 = (bf16[16,8320]{1,0:T(8,128)(2,1)S(1)}, bf16[16,8320]{1,0:T(8,128)(2,1)S(1)}, u32[]{:S(2)}, u32[]{:S(2)}) collective-permute-start(bf16[16,8320]{1,0:T(8,128)(2,1)S(1)} %get-tuple-element.131), channel_id=1, source_target_pairs={{0,4},{2,6},{4,0},{6,2},{1,5},{3,7},{5,1},{7,3},{8,12},{10,14},{12... | collective-permute-start | bytes 798728 | tf_op jit(solution)/shard_map/ppermute | solution.py:551
  64.6 1.9 %collective-permute-done.23.refs_3_ = bf16[16,4096]{1,0:T(8,128)(2,1)S(1)} collective-permute-done((bf16[16,4096]{1,0:T(8,128)(2,1)S(1)}, bf16[16,4096]{1,0:T(8,128)(2,1)S(1)}, u32[]{:S(2)}, u32[]{:S(2)}) %collective-permute-start.23) | collective-permute-done | bytes 131104 | tf_op jit(solution)/shard_map/ppermute | solution.py:551
  67.4 16.9 %collective-permute-done.24.refs_5_ = bf16[32,4096]{1,0:T(8,128)(2,1)S(1)} collective-permute-done((bf16[32,4096]{1,0:T(8,128)(2,1)S(1)}, bf16[32,4096]{1,0:T(8,128)(2,1)S(1)}, u32[]{:S(2)}, u32[]{:S(2)}) %collective-permute-start.24) | collective-permute-done | bytes 262176 | tf_op jit(solution)/shard_map/ppermute | solution.py:627
  84.3 2.2 %collective-permute-done.19.refs_3_ = bf16[16,8320]{1,0:T(8,128)(2,1)S(1)} collective-permute-done((bf16[16,8320]{1,0:T(8,128)(2,1)S(1)}, bf16[16,8320]{1,0:T(8,128)(2,1)S(1)}, u32[]{:S(2)}, u32[]{:S(2)}) %collective-permute-start.19) | collective-permute-done | bytes 266272 | tf_op jit(solution)/shard_map/ppermute | solution.py:551
  86.5 1.8 %final_mix.1 = bf16[32,8192]{1,0:T(8,128)(2,1)} custom-call(f32[32,64]{1,0:T(8,128)S(1)} %get-tuple-element.77.choice_ref, bf16[16,8320]{1,0:T(8,128)(2,1)S(1)} %get-tuple-element.129.refs_0_, bf16[16,8320]{1,0:T(8,128)(2,1)S(1)} %collective-permute-done.17.refs_1_, bf16[16,8320]{1,0:T(8,128)(2,1)S(1)} %collective-permute-done.18.refs_2_, ...), custom_call_target="tpu_custom_call" | custom-call | tf_op jit(solution)/shard_map/final_mix/pallas_call | solution.py:538
  (33 shorter events, 8.5 us)
Async XLA Ops:
  0.0 10.2 %collective-permute-start.2 = (bf16[1,128,16384]{2,1,0:T(8,128)(2,1)}, bf16[1,128,16384]{2,1,0:T(8,128)(2,1)}, u32[]{:S(2)}, u32[]{:S(2)}) collective-permute-start(bf16[1,128,16384]{2,1,0:T(8,128)(2,1)} %mine_ref.1), channel_id=1, source_target_pairs={{0,1},{1,0},{2,3},{3,2},{4,5},{5,4},{6,7},{7,6},{8,9},{9,8},{10,11... | collective-permute-start | bytes 12582920 | tf_op jit(solution)/shard_map/ppermute | solution.py:594
  1.6 17.2 %collective-permute-start.1 = (bf16[32,4352]{1,0:T(8,128)(2,1)S(1)}, bf16[32,4352]{1,0:T(8,128)(2,1)S(1)}, u32[]{:S(2)}, u32[]{:S(2)}) collective-permute-start(bf16[32,4352]{1,0:T(8,128)(2,1)S(1)} %get-tuple-element.75.refs_0_), channel_id=1, source_target_pairs={{0,8},{8,0},{1,9},{9,1},{2,10},{10,2},{3,11},{11,3},{4,12},{12,4},... | collective-permute-start | bytes 835592 | tf_op jit(solution)/shard_map/ppermute | solution.py:589
  6.6 13.4 %collective-permute-start.3 = (bf16[16,8448]{1,0:T(8,128)(2,1)S(1)}, bf16[16,8448]{1,0:T(8,128)(2,1)S(1)}, u32[]{:S(2)}, u32[]{:S(2)}) collective-permute-start(bf16[16,8448]{1,0:T(8,128)(2,1)S(1)} %get-tuple-element.81), channel_id=1, source_target_pairs={{0,2},{2,0},{4,6},{6,4},{1,3},{3,1},{5,7},{7,5},{8,10},{10,8},{12,... | collective-permute-start | bytes 811016 | tf_op jit(solution)/shard_map/ppermute | solution.py:551
  8.2 22.5 %collective-permute-start.5 = (bf16[16,8448]{1,0:T(8,128)(2,1)S(1)}, bf16[16,8448]{1,0:T(8,128)(2,1)S(1)}, u32[]{:S(2)}, u32[]{:S(2)}) collective-permute-start(bf16[16,8448]{1,0:T(8,128)(2,1)S(1)} %get-tuple-element.94), channel_id=1, source_target_pairs={{0,4},{2,6},{4,0},{6,2},{1,5},{3,7},{5,1},{7,3},{8,12},{10,14},{12... | collective-permute-start | bytes 811016 | tf_op jit(solution)/shard_map/ppermute | solution.py:551
  9.8 24.0 %collective-permute-start.6 = (bf16[16,8448]{1,0:T(8,128)(2,1)S(1)}, bf16[16,8448]{1,0:T(8,128)(2,1)S(1)}, u32[]{:S(2)}, u32[]{:S(2)}) collective-permute-start(bf16[16,8448]{1,0:T(8,128)(2,1)S(1)} %get-tuple-element.95), channel_id=1, source_target_pairs={{0,6},{2,4},{4,2},{6,0},{1,7},{3,5},{5,3},{7,1},{8,14},{10,12},{12... | collective-permute-start | bytes 811016 | tf_op jit(solution)/shard_map/ppermute | solution.py:551
  10.2 19.6 %collective-permute-start = (bf16[32,4096]{1,0:T(8,128)(2,1)S(1)}, bf16[32,4096]{1,0:T(8,128)(2,1)S(1)}, u32[]{:S(2)}, u32[]{:S(2)}) collective-permute-start(bf16[32,4096]{1,0:T(8,128)(2,1)S(1)} %get-tuple-element.76.refs_1_), channel_id=1, source_target_pairs={{0,8},{8,0},{1,9},{9,1},{2,10},{10,2},{3,11},{11,3},{4,12},{12,4},... | collective-permute-start | bytes 786440 | tf_op jit(solution)/shard_map/ppermute | solution.py:589
  20.0 5.3 %collective-permute-start.4 = (bf16[16,4352]{1,0:T(8,128)(2,1)S(1)}, bf16[16,4352]{1,0:T(8,128)(2,1)S(1)}, u32[]{:S(2)}, u32[]{:S(2)}) collective-permute-start(bf16[16,4352]{1,0:T(8,128)(2,1)S(1)} %get-tuple-element.86), channel_id=1, source_target_pairs={{0,2},{2,0},{4,6},{6,4},{1,3},{3,1},{5,7},{7,5},{8,10},{10,8},{12,... | collective-permute-start | bytes 417800 | tf_op jit(solution)/shard_map/ppermute | solution.py:551
  21.8 17.2 %collective-permute-start.11 = (bf16[16,4352]{1,0:T(8,128)(2,1)S(1)}, bf16[16,4352]{1,0:T(8,128)(2,1)S(1)}, u32[]{:S(2)}, u32[]{:S(2)}) collective-permute-start(bf16[16,4352]{1,0:T(8,128)(2,1)S(1)} %get-tuple-element.114), channel_id=1, source_target_pairs={{0,4},{2,6},{4,0},{6,2},{1,5},{3,7},{5,1},{7,3},{8,12},{10,14},{12... | collective-permute-start | bytes 417800 | tf_op jit(solution)/shard_map/ppermute | solution.py:551
  25.4 14.4 %collective-permute-start.12 = (bf16[16,4352]{1,0:T(8,128)(2,1)S(1)}, bf16[16,4352]{1,0:T(8,128)(2,1)S(1)}, u32[]{:S(2)}, u32[]{:S(2)}) collective-permute-start(bf16[16,4352]{1,0:T(8,128)(2,1)S(1)} %get-tuple-element.115), channel_id=1, source_target_pairs={{0,6},{2,4},{4,2},{6,0},{1,7},{3,5},{5,3},{7,1},{8,14},{10,12},{12... | collective-permute-start | bytes 417800 | tf_op jit(solution)/shard_map/ppermute | solution.py:551
  33.8 7.0 %collective-permute-start.7 = (bf16[16,4096]{1,0:T(8,128)(2,1)S(1)}, bf16[16,4096]{1,0:T(8,128)(2,1)S(1)}, u32[]{:S(2)}, u32[]{:S(2)}) collective-permute-start(bf16[16,4096]{1,0:T(8,128)(2,1)S(1)} %get-tuple-element.104), channel_id=1, source_target_pairs={{0,2},{2,0},{4,6},{6,4},{1,3},{3,1},{5,7},{7,5},{8,10},{10,8},{12,... | collective-permute-start | bytes 393224 | tf_op jit(solution)/shard_map/ppermute | solution.py:551
  35.2 7.3 %collective-permute-start.8 = (bf16[16,4096]{1,0:T(8,128)(2,1)S(1)}, bf16[16,4096]{1,0:T(8,128)(2,1)S(1)}, u32[]{:S(2)}, u32[]{:S(2)}) collective-permute-start(bf16[16,4096]{1,0:T(8,128)(2,1)S(1)} %get-tuple-element.105), channel_id=1, source_target_pairs={{0,4},{2,6},{4,0},{6,2},{1,5},{3,7},{5,1},{7,3},{8,12},{10,14},{12... | collective-permute-start | bytes 393224 | tf_op jit(solution)/shard_map/ppermute | solution.py:551
  35.2 9.2 %collective-permute-start.9 = (bf16[16,4096]{1,0:T(8,128)(2,1)S(1)}, bf16[16,4096]{1,0:T(8,128)(2,1)S(1)}, u32[]{:S(2)}, u32[]{:S(2)}) collective-permute-start(bf16[16,4096]{1,0:T(8,128)(2,1)S(1)} %get-tuple-element.106), channel_id=1, source_target_pairs={{0,6},{2,4},{4,2},{6,0},{1,7},{3,5},{5,3},{7,1},{8,14},{10,12},{12... | collective-permute-start | bytes 393224 | tf_op jit(solution)/shard_map/ppermute | solution.py:551
  45.4 1.7 %collective-permute-start.13 = (f32[64,1280]{1,0:T(8,128)S(1)}, f32[64,1280]{1,0:T(8,128)S(1)}, u32[]{:S(2)}, u32[]{:S(2)}) collective-permute-start(f32[64,1280]{1,0:T(8,128)S(1)} %half_scores.5.mine_ref), channel_id=1, source_target_pairs={{0,1},{1,0},{2,3},{3,2},{4,5},{5,4},{6,7},{7,6},{8,9},{9,8},{10,11... | collective-permute-start | bytes 983048 | tf_op jit(solution)/shard_map/ppermute | solution.py:615
  45.4 2.8 %collective-permute-start.10 = (f32[64,1280]{1,0:T(8,128)S(1)}, f32[64,1280]{1,0:T(8,128)S(1)}, u32[]{:S(2)}, u32[]{:S(2)}) collective-permute-start(f32[64,1280]{1,0:T(8,128)S(1)} %half_scores.3.mine_ref), channel_id=1, source_target_pairs={{0,1},{1,0},{2,3},{3,2},{4,5},{5,4},{6,7},{7,6},{8,9},{9,8},{10,11... | collective-permute-start | bytes 983048 | tf_op jit(solution)/shard_map/ppermute | solution.py:617
  48.3 6.1 %collective-permute-start.14 = (bf16[16,4224]{1,0:T(8,128)(2,1)S(1)}, bf16[16,4224]{1,0:T(8,128)(2,1)S(1)}, u32[]{:S(2)}, u32[]{:S(2)}) collective-permute-start(bf16[16,4224]{1,0:T(8,128)(2,1)S(1)} %get-tuple-element.126), channel_id=1, source_target_pairs={{0,2},{2,0},{4,6},{6,4},{1,3},{3,1},{5,7},{7,5},{8,10},{10,8},{12,... | collective-permute-start | bytes 405512 | tf_op jit(solution)/shard_map/ppermute | solution.py:551
  49.8 9.1 %collective-permute-start.15 = (bf16[16,4224]{1,0:T(8,128)(2,1)S(1)}, bf16[16,4224]{1,0:T(8,128)(2,1)S(1)}, u32[]{:S(2)}, u32[]{:S(2)}) collective-permute-start(bf16[16,4224]{1,0:T(8,128)(2,1)S(1)} %get-tuple-element.127), channel_id=1, source_target_pairs={{0,4},{2,6},{4,0},{6,2},{1,5},{3,7},{5,1},{7,3},{8,12},{10,14},{12... | collective-permute-start | bytes 405512 | tf_op jit(solution)/shard_map/ppermute | solution.py:551
  49.8 9.4 %collective-permute-start.16 = (bf16[16,4224]{1,0:T(8,128)(2,1)S(1)}, bf16[16,4224]{1,0:T(8,128)(2,1)S(1)}, u32[]{:S(2)}, u32[]{:S(2)}) collective-permute-start(bf16[16,4224]{1,0:T(8,128)(2,1)S(1)} %get-tuple-element.128), channel_id=1, source_target_pairs={{0,6},{2,4},{4,2},{6,0},{1,7},{3,5},{5,3},{7,1},{8,14},{10,12},{12... | collective-permute-start | bytes 405512 | tf_op jit(solution)/shard_map/ppermute | solution.py:551
  52.8 9.4 %collective-permute-start.21 = (bf16[16,4096]{1,0:T(8,128)(2,1)S(1)}, bf16[16,4096]{1,0:T(8,128)(2,1)S(1)}, u32[]{:S(2)}, u32[]{:S(2)}) collective-permute-start(bf16[16,4096]{1,0:T(8,128)(2,1)S(1)} %get-tuple-element.142), channel_id=1, source_target_pairs={{0,2},{2,0},{4,6},{6,4},{1,3},{3,1},{5,7},{7,5},{8,10},{10,8},{12,... | collective-permute-start | bytes 393224 | tf_op jit(solution)/shard_map/ppermute | solution.py:551
  54.4 10.0 %collective-permute-start.22 = (bf16[16,4096]{1,0:T(8,128)(2,1)S(1)}, bf16[16,4096]{1,0:T(8,128)(2,1)S(1)}, u32[]{:S(2)}, u32[]{:S(2)}) collective-permute-start(bf16[16,4096]{1,0:T(8,128)(2,1)S(1)} %get-tuple-element.143), channel_id=1, source_target_pairs={{0,4},{2,6},{4,0},{6,2},{1,5},{3,7},{5,1},{7,3},{8,12},{10,14},{12... | collective-permute-start | bytes 393224 | tf_op jit(solution)/shard_map/ppermute | solution.py:551
  54.4 12.1 %collective-permute-start.23 = (bf16[16,4096]{1,0:T(8,128)(2,1)S(1)}, bf16[16,4096]{1,0:T(8,128)(2,1)S(1)}, u32[]{:S(2)}, u32[]{:S(2)}) collective-permute-start(bf16[16,4096]{1,0:T(8,128)(2,1)S(1)} %get-tuple-element.144), channel_id=1, source_target_pairs={{0,6},{2,4},{4,2},{6,0},{1,7},{3,5},{5,3},{7,1},{8,14},{10,12},{12... | collective-permute-start | bytes 393224 | tf_op jit(solution)/shard_map/ppermute | solution.py:551
  59.8 26.6 %collective-permute-start.20 = (bf16[32,4224]{1,0:T(8,128)(2,1)S(1)}, bf16[32,4224]{1,0:T(8,128)(2,1)S(1)}, u32[]{:S(2)}, u32[]{:S(2)}) collective-permute-start(bf16[32,4224]{1,0:T(8,128)(2,1)S(1)} %get-tuple-element.137), channel_id=1, source_target_pairs={{0,8},{8,0},{1,9},{9,1},{2,10},{10,2},{3,11},{11,3},{4,12},{12,4},... | collective-permute-start | bytes 811016 | tf_op jit(solution)/shard_map/ppermute | solution.py:625
  61.1 23.2 %collective-permute-start.17 = (bf16[16,8320]{1,0:T(8,128)(2,1)S(1)}, bf16[16,8320]{1,0:T(8,128)(2,1)S(1)}, u32[]{:S(2)}, u32[]{:S(2)}) collective-permute-start(bf16[16,8320]{1,0:T(8,128)(2,1)S(1)} %get-tuple-element.130), channel_id=1, source_target_pairs={{0,2},{2,0},{4,6},{6,4},{1,3},{3,1},{5,7},{7,5},{8,10},{10,8},{12,... | collective-permute-start | bytes 798728 | tf_op jit(solution)/shard_map/ppermute | solution.py:551
  62.3 22.0 %collective-permute-start.18 = (bf16[16,8320]{1,0:T(8,128)(2,1)S(1)}, bf16[16,8320]{1,0:T(8,128)(2,1)S(1)}, u32[]{:S(2)}, u32[]{:S(2)}) collective-permute-start(bf16[16,8320]{1,0:T(8,128)(2,1)S(1)} %get-tuple-element.131), channel_id=1, source_target_pairs={{0,4},{2,6},{4,0},{6,2},{1,5},{3,7},{5,1},{7,3},{8,12},{10,14},{12... | collective-permute-start | bytes 798728 | tf_op jit(solution)/shard_map/ppermute | solution.py:551
  64.3 22.2 %collective-permute-start.19 = (bf16[16,8320]{1,0:T(8,128)(2,1)S(1)}, bf16[16,8320]{1,0:T(8,128)(2,1)S(1)}, u32[]{:S(2)}, u32[]{:S(2)}) collective-permute-start(bf16[16,8320]{1,0:T(8,128)(2,1)S(1)} %get-tuple-element.132), channel_id=1, source_target_pairs={{0,6},{2,4},{4,2},{6,0},{1,7},{3,5},{5,3},{7,1},{8,14},{10,12},{12... | collective-permute-start | bytes 798728 | tf_op jit(solution)/shard_map/ppermute | solution.py:551
  66.8 17.5 %collective-permute-start.24 = (bf16[32,4096]{1,0:T(8,128)(2,1)S(1)}, bf16[32,4096]{1,0:T(8,128)(2,1)S(1)}, u32[]{:S(2)}, u32[]{:S(2)}) collective-permute-start(bf16[32,4096]{1,0:T(8,128)(2,1)S(1)} %rest_of_mix.1), channel_id=1, source_target_pairs={{0,8},{8,0},{1,9},{9,1},{2,10},{10,2},{3,11},{11,3},{4,12},{12,4},... | collective-permute-start | bytes 786440 | tf_op jit(solution)/shard_map/ppermute | solution.py:627

commit v6 on v5

--- a/solution.py
+++ b/solution.py
@@ -13,7 +13,7 @@
 NEG = -1e30
 shift_count = 5
 GIVEN_SHARE = 4
-SENT_SHARE = 4
+SENT_SHARE = 5
 VMEM_LIMIT = 24 * 1024 * 1024
 IN_HBM = pl.BlockSpec(memory_space=pltpu.HBM)
 IN_VMEM = pl.BlockSpec(memory_space=pltpu.VMEM)
@@ -30,7 +30,7 @@
 
 
 def tiles_of(spans):
-    tile = 16 * LANES
+    tile = 32 * LANES
     for place, start, length in spans:
         for offset in range(0, length, tile):
             yield place + offset, start + offset, min(tile, length - offset)
@@ -507,8 +507,8 @@
 
 def final_kernel(choice_ref, *refs, pieces, chunks):
     back_refs = refs[:pieces]
-    part_refs = refs[pieces:-1]
-    out_ref = refs[-1]
+    *part_refs, out_ref, mixed_ref, sems = refs[pieces:]
+    copies = []
     rows, slots = choice_ref.shape
     pixels = chunks[-1][1]
     end = chunks[0][1]
@@ -529,17 +529,30 @@
             mixed = jnp.dot(mixer, images, preferred_element_type=jnp.float32)
             mixed = mixed[0:rows] + (mixed[rows : 2 * rows] + mixed[2 * rows : 3 * rows])
             mixed = mixed + part_factor * part_ref[:, place : place + tile].astype(jnp.float32)
-            out_ref[:, start : start + tile] = mixed.astype(jnp.bfloat16)
+            span = pl.ds(start, tile)
+            mixed_ref[:, span] = mixed.astype(jnp.bfloat16)
+            copy = pltpu.make_async_copy(
+                mixed_ref.at[:, span], out_ref.at[:, span], sems.at[len(copies)]
+            )
+            copy.start()
+            copies.append(copy)
+    for copy in copies:
+        copy.wait()
 
 
 def final_mix(choice, back, parts, chunks):
     rows = choice.shape[0]
     args = [choice, *back, *parts]
+    count = len(list(tiles_of([(0, first, last - first) for first, last in chunks])))
     return pl.pallas_call(
         functools.partial(final_kernel, pieces=len(back), chunks=chunks),
         in_specs=[IN_VMEM] * len(args),
-        out_specs=IN_VMEM,
+        out_specs=IN_HBM,
         out_shape=jax.ShapeDtypeStruct((rows, chunks[-1][1]), jnp.bfloat16),
+        scratch_shapes=[
+            pltpu.VMEM((rows, chunks[-1][1]), jnp.bfloat16),
+            pltpu.SemaphoreType.DMA((count,)),
+        ],
         compiler_params=pltpu.CompilerParams(vmem_limit_bytes=VMEM_LIMIT),
         name="final_mix",
     )(*args)

time: 88.5 us -> 88.2 us (level)
  starting transfers between devices: 32 us -> 30 us
  waiting for transfers between devices: 37.1 us -> 39.1 us
    ppermute x2, waiting for transfers between devices: 4 us -> 11.5 us  [on_device(): far_payload = [lax.ppermute(chunk, 'hi', across) for chunk in payload]]
    ppermute x18, waiting for transfers between devices: 15.1 us -> 9.77 us  [trade(): lax.ppermute(pieces[flip], 'lo', [(i, i ^ flip) for i in range(peers)])]
    ppermute x2, starting transfers between devices: 5 us -> 3.65 us  [on_device(): far_payload = [lax.ppermute(chunk, 'hi', across) for chunk in payload]]
  transfers between devices with their start and end apart: 25 -> 25, of which waited for: 11 -> 10; matrix products, arithmetic and copies ran while one was open for 0% -> 0% of each run, Pallas kernels for 18% -> 18%
where the time goes in v6:
time: 88.2 us; the launch traced here: 88 us
  waiting for transfers between devices  39.1 us (44%)
  starting transfers between devices  30 us (34%)
  Pallas kernels  18.7 us (21%)
    ppermute x18, starting transfers between devices, trade(): lax.ppermute(pieces[flip], 'lo', [(i, i ^ flip) for i in range(peers)])  23.4 us
    ppermute x1, waiting for transfers between devices, on_device(): rest_part = lax.ppermute(rest_mix, 'hi', across)  16.7 us
    ppermute x2, waiting for transfers between devices, on_device(): far_payload = [lax.ppermute(chunk, 'hi', across) for chunk in payload]  11.5 us
    ppermute x18, waiting for transfers between devices, trade(): lax.ppermute(pieces[flip], 'lo', [(i, i ^ flip) for i in range(peers)])  9.77 us
    ppermute x2, starting transfers between devices, on_device(): far_payload = [lax.ppermute(chunk, 'hi', across) for chunk in payload]  3.65 us
    pallas_call x2, Pallas kernels, weighted_means(): pl.pallas_call(functools.partial(mean_kernel, chunk=chunk, pieces=pieces)...  3.6 us
    pallas_call x3, Pallas kernels, half_scores(): pl.pallas_call(functools.partial(score_kernel, pieces=len(records), spans...  3.58 us
    pallas_call x3, Pallas kernels, pack(): pl.pallas_call(functools.partial(pack_kernel, sources=len(chunks), classe...  3.36 us
  transfers between devices with their start and end apart: 25, of which 10 were waited for; matrix products, arithmetic and copies ran while one was open for 0% of the time, Pallas kernels for 18%

profile of v6, /device:TPU:0, one launch (start us, length us, event | category | flops | bytes accessed | tf_op | source)
XLA Modules:
  0.0 88.0 jit_solution(16074939631412216340)
XLA Ops:
  0.5 1.1 %make_payload.1 = (bf16[32,5376]{1,0:T(8,128)(2,1)S(1)}, bf16[32,3072]{1,0:T(8,128)(2,1)S(1)}) custom-call(s32[1]{0:T(128)} %bitcast.2.core_ref, bf16[32,16384]{1,0:T(8,128)(2,1)} %x_ref.1, bf16[1,32]{1,0:T(2,128)(2,1)} %bitcast.6, s32[2,32]{1,0:T(2,128)} %bitcast.5, s32[32,128]{1,0:T(8,128)} %keep_ref.1), custom_call_target="tpu_custom_call" | custom-call | tf_op jit(solution)/shard_map/make_payload/pallas_call | solution.py:143
  1.6 3.7 %collective-permute-start.1 = (bf16[32,5376]{1,0:T(8,128)(2,1)S(1)}, bf16[32,5376]{1,0:T(8,128)(2,1)S(1)}, u32[]{:S(2)}, u32[]{:S(2)}) collective-permute-start(bf16[32,5376]{1,0:T(8,128)(2,1)S(1)} %get-tuple-element.75.refs_0_), channel_id=1, source_target_pairs={{0,8},{8,0},{1,9},{9,1},{2,10},{10,2},{3,11},{11,3},{4,12},{12,4},... | collective-permute-start | bytes 1032200 | tf_op jit(solution)/shard_map/ppermute | solution.py:602
  5.3 1.3 %pack.2 = (bf16[16,8448]{1,0:T(8,128)(2,1)S(1)}, bf16[16,8448]{1,0:T(8,128)(2,1)S(1)}, bf16[16,8448]{1,0:T(8,128)(2,1)S(1)}, bf16[16,8448]{1,0:T(8,128)(2,1)S(1)}, f32[32,64]{1,0:T(8,128)S(1)}) custom-call(s32[2]{0:T(128)S(1)} %pad_add_fusion.place_ref, bf16[32,5376]{1,0:T(8,128)(2,1)S(1)} %get-tuple-element.75.refs_0_, ...), custom_call_target="tpu_custom_call" | custom-call | tf_op jit(solution)/shard_map/pack/pallas_call | solution.py:223
  6.6 1.6 %collective-permute-start.3 = (bf16[16,8448]{1,0:T(8,128)(2,1)S(1)}, bf16[16,8448]{1,0:T(8,128)(2,1)S(1)}, u32[]{:S(2)}, u32[]{:S(2)}) collective-permute-start(bf16[16,8448]{1,0:T(8,128)(2,1)S(1)} %get-tuple-element.81), channel_id=1, source_target_pairs={{0,2},{2,0},{4,6},{6,4},{1,3},{3,1},{5,7},{7,5},{8,10},{10,8},{12,... | collective-permute-start | bytes 811016 | tf_op jit(solution)/shard_map/ppermute | solution.py:564
  8.2 1.6 %collective-permute-start.5 = (bf16[16,8448]{1,0:T(8,128)(2,1)S(1)}, bf16[16,8448]{1,0:T(8,128)(2,1)S(1)}, u32[]{:S(2)}, u32[]{:S(2)}) collective-permute-start(bf16[16,8448]{1,0:T(8,128)(2,1)S(1)} %get-tuple-element.94), channel_id=1, source_target_pairs={{0,4},{2,6},{4,0},{6,2},{1,5},{3,7},{5,1},{7,3},{8,12},{10,14},{12... | collective-permute-start | bytes 811016 | tf_op jit(solution)/shard_map/ppermute | solution.py:564
  10.2 3.3 %make_views.1 = (bf16[128,8448]{1,0:T(8,128)(2,1)S(1)}, bf16[128,8448]{1,0:T(8,128)(2,1)S(1)}, f32[1,128]{1,0:T(1,128)S(1)}) custom-call(s32[1]{0:T(128)} %bitcast.2.core_ref, bf16[1,128,16384]{2,1,0:T(8,128)(2,1)} %mine_ref.1, bf16[1,128,16384]{2,1,0:T(8,128)(2,1)} %collective-permute-done.2.theirs_ref), custom_call_target="tpu_custom_call" | custom-call | tf_op jit(solution)/shard_map/make_views/pallas_call | solution.py:279
  13.5 8.0 %collective-permute-done.1.refs_0_ = bf16[32,5376]{1,0:T(8,128)(2,1)S(1)} collective-permute-done((bf16[32,5376]{1,0:T(8,128)(2,1)S(1)}, bf16[32,5376]{1,0:T(8,128)(2,1)S(1)}, u32[]{:S(2)}, u32[]{:S(2)}) %collective-permute-start.1) | collective-permute-done | bytes 344096 | tf_op jit(solution)/shard_map/ppermute | solution.py:602
  21.4 1.2 %pack.3 = (bf16[16,5376]{1,0:T(8,128)(2,1)S(1)}, bf16[16,5376]{1,0:T(8,128)(2,1)S(1)}, bf16[16,5376]{1,0:T(8,128)(2,1)S(1)}, bf16[16,5376]{1,0:T(8,128)(2,1)S(1)}, f32[32,64]{1,0:T(8,128)S(1)}) custom-call(s32[2]{0:T(128)S(1)} %pad_add_fusion.place_ref, bf16[32,5376]{1,0:T(8,128)(2,1)S(1)} %collective-permute-done.1.refs_0_), custom_call_target="tpu_custom_call" | custom-call | tf_op jit(solution)/shard_map/pack/pallas_call | solution.py:223
  22.7 1.6 %collective-permute-start.4 = (bf16[16,5376]{1,0:T(8,128)(2,1)S(1)}, bf16[16,5376]{1,0:T(8,128)(2,1)S(1)}, u32[]{:S(2)}, u32[]{:S(2)}) collective-permute-start(bf16[16,5376]{1,0:T(8,128)(2,1)S(1)} %get-tuple-element.86), channel_id=1, source_target_pairs={{0,2},{2,0},{4,6},{6,4},{1,3},{3,1},{5,7},{7,5},{8,10},{10,8},{12,... | collective-permute-start | bytes 516104 | tf_op jit(solution)/shard_map/ppermute | solution.py:564
  24.3 4.0 %collective-permute-start.11 = (bf16[16,5376]{1,0:T(8,128)(2,1)S(1)}, bf16[16,5376]{1,0:T(8,128)(2,1)S(1)}, u32[]{:S(2)}, u32[]{:S(2)}) collective-permute-start(bf16[16,5376]{1,0:T(8,128)(2,1)S(1)} %get-tuple-element.114), channel_id=1, source_target_pairs={{0,4},{2,6},{4,0},{6,2},{1,5},{3,7},{5,1},{7,3},{8,12},{10,14},{12... | collective-permute-start | bytes 516104 | tf_op jit(solution)/shard_map/ppermute | solution.py:564
  28.3 3.9 %collective-permute-done.4.refs_1_ = bf16[16,5376]{1,0:T(8,128)(2,1)S(1)} collective-permute-done((bf16[16,5376]{1,0:T(8,128)(2,1)S(1)}, bf16[16,5376]{1,0:T(8,128)(2,1)S(1)}, u32[]{:S(2)}, u32[]{:S(2)}) %collective-permute-start.4) | collective-permute-done | bytes 172064 | tf_op jit(solution)/shard_map/ppermute | solution.py:564
  32.2 3.5 %collective-permute-done.refs_0_ = bf16[32,3072]{1,0:T(8,128)(2,1)S(1)} collective-permute-done((bf16[32,3072]{1,0:T(8,128)(2,1)S(1)}, bf16[32,3072]{1,0:T(8,128)(2,1)S(1)}, u32[]{:S(2)}, u32[]{:S(2)}) %collective-permute-start) | collective-permute-done | bytes 196640 | tf_op jit(solution)/shard_map/ppermute | solution.py:602
  35.7 0.8 pack_rest.1
  37.3 2.8 %collective-permute-start.9 = (bf16[16,3072]{1,0:T(8,128)(2,1)S(1)}, bf16[16,3072]{1,0:T(8,128)(2,1)S(1)}, u32[]{:S(2)}, u32[]{:S(2)}) collective-permute-start(bf16[16,3072]{1,0:T(8,128)(2,1)S(1)} %get-tuple-element.106), channel_id=1, source_target_pairs={{0,6},{2,4},{4,2},{6,0},{1,7},{3,5},{5,3},{7,1},{8,14},{10,12},{12... | collective-permute-start | bytes 294920 | tf_op jit(solution)/shard_map/ppermute | solution.py:564
  40.1 1.7 %half_scores.3.mine_ref = f32[64,1280]{1,0:T(8,128)S(1)} custom-call(bf16[16,8448]{1,0:T(8,128)(2,1)S(1)} %get-tuple-element.96.refs_0_, bf16[16,8448]{1,0:T(8,128)(2,1)S(1)} %collective-permute-done.3.refs_1_, bf16[16,8448]{1,0:T(8,128)(2,1)S(1)} %collective-permute-done.5.refs_2_, bf16[16,8448]{1,0:T(8,128)(2,1)S(1)} %collective-permute-done.6.refs_3_, ...), custom_call_target="tpu_custom_call" | custom-call | tf_op jit(solution)/shard_map/half_scores/pallas_call | solution.py:340
  41.9 1.1 %half_scores.4.refs_7_ = f32[64,1280]{1,0:T(8,128)S(1)} custom-call(bf16[16,5376]{1,0:T(8,128)(2,1)S(1)} %get-tuple-element.112.refs_0_, bf16[16,5376]{1,0:T(8,128)(2,1)S(1)} %collective-permute-done.4.refs_1_, bf16[16,5376]{1,0:T(8,128)(2,1)S(1)} %collective-permute-done.11.refs_2_, bf16[16,5376]{1,0:T(8,128)(2,1)S(1)} %collective-permute-done.12.refs_3_, ...), custom_call_target="tpu_custom_call" | custom-call | tf_op jit(solution)/shard_map/half_scores/pallas_call | solution.py:340
  43.3 1.1 %collective-permute-done.9.refs_3_ = bf16[16,3072]{1,0:T(8,128)(2,1)S(1)} collective-permute-done((bf16[16,3072]{1,0:T(8,128)(2,1)S(1)}, bf16[16,3072]{1,0:T(8,128)(2,1)S(1)}, u32[]{:S(2)}, u32[]{:S(2)}) %collective-permute-start.9) | collective-permute-done | bytes 98336 | tf_op jit(solution)/shard_map/ppermute | solution.py:564
  45.7 1.1 %collective-permute-done.13.theirs_ref = f32[64,1280]{1,0:T(8,128)S(1)} collective-permute-done((f32[64,1280]{1,0:T(8,128)S(1)}, f32[64,1280]{1,0:T(8,128)S(1)}, u32[]{:S(2)}, u32[]{:S(2)}) %collective-permute-start.13) | collective-permute-done | bytes 327712 | tf_op jit(solution)/shard_map/ppermute | solution.py:628
  46.9 1.2 %weighted_means.2 = (bf16[16,4224]{1,0:T(8,128)(2,1)S(1)}, bf16[16,4224]{1,0:T(8,128)(2,1)S(1)}, bf16[16,4224]{1,0:T(8,128)(2,1)S(1)}, bf16[16,4224]{1,0:T(8,128...) custom-call(f32[64,1280]{1,0:T(8,128)S(1)} %half_scores.5.mine_ref, ...), custom_call_target="tpu_custom_call" | custom-call | tf_op jit(solution)/shard_map/weighted_means/pallas_call | solution.py:421
  48.1 1.6 %collective-permute-start.14 = (bf16[16,4224]{1,0:T(8,128)(2,1)S(1)}, bf16[16,4224]{1,0:T(8,128)(2,1)S(1)}, u32[]{:S(2)}, u32[]{:S(2)}) collective-permute-start(bf16[16,4224]{1,0:T(8,128)(2,1)S(1)} %get-tuple-element.126), channel_id=1, source_target_pairs={{0,2},{2,0},{4,6},{6,4},{1,3},{3,1},{5,7},{7,5},{8,10},{10,8},{12,... | collective-permute-start | bytes 405512 | tf_op jit(solution)/shard_map/ppermute | solution.py:564
  49.9 1.7 %collective-permute-start.16 = (bf16[16,4224]{1,0:T(8,128)(2,1)S(1)}, bf16[16,4224]{1,0:T(8,128)(2,1)S(1)}, u32[]{:S(2)}, u32[]{:S(2)}) collective-permute-start(bf16[16,4224]{1,0:T(8,128)(2,1)S(1)} %get-tuple-element.128), channel_id=1, source_target_pairs={{0,6},{2,4},{4,2},{6,0},{1,7},{3,5},{5,3},{7,1},{8,14},{10,12},{12... | collective-permute-start | bytes 405512 | tf_op jit(solution)/shard_map/ppermute | solution.py:564
  51.6 1.0 %rest_of_means.1 = (bf16[16,4096]{1,0:T(8,128)(2,1)S(1)}, bf16[16,4096]{1,0:T(8,128)(2,1)S(1)}, bf16[16,4096]{1,0:T(8,128)(2,1)S(1)}, bf16[16,4096]{1,0:T(8,128)(2,1)S(1)}) custom-call(bf16[320,256]{1,0:T(8,128)(2,1)S(1)} %get-tuple-element.139.weight_ref, f32[64,128]{1,0:T(8,128)S(1)} %get-tuple-element.140.inverse_ref, ...), custom_call_target="tpu_custom_call" | custom-call | tf_op jit(solution)/shard_map/rest_of_means/pallas_call | solution.py:438
  52.6 1.6 %collective-permute-start.21 = (bf16[16,4096]{1,0:T(8,128)(2,1)S(1)}, bf16[16,4096]{1,0:T(8,128)(2,1)S(1)}, u32[]{:S(2)}, u32[]{:S(2)}) collective-permute-start(bf16[16,4096]{1,0:T(8,128)(2,1)S(1)} %get-tuple-element.142), channel_id=1, source_target_pairs={{0,2},{2,0},{4,6},{6,4},{1,3},{3,1},{5,7},{7,5},{8,10},{10,8},{12,... | collective-permute-start | bytes 393224 | tf_op jit(solution)/shard_map/ppermute | solution.py:564
  54.5 1.7 %collective-permute-start.23 = (bf16[16,4096]{1,0:T(8,128)(2,1)S(1)}, bf16[16,4096]{1,0:T(8,128)(2,1)S(1)}, u32[]{:S(2)}, u32[]{:S(2)}) collective-permute-start(bf16[16,4096]{1,0:T(8,128)(2,1)S(1)} %get-tuple-element.144), channel_id=1, source_target_pairs={{0,6},{2,4},{4,2},{6,0},{1,7},{3,5},{5,3},{7,1},{8,14},{10,12},{12... | collective-permute-start | bytes 393224 | tf_op jit(solution)/shard_map/ppermute | solution.py:564
  56.2 2.4 %weighted_means.3 = (bf16[16,8320]{1,0:T(8,128)(2,1)S(1)}, bf16[16,8320]{1,0:T(8,128)(2,1)S(1)}, bf16[16,8320]{1,0:T(8,128)(2,1)S(1)}, bf16[16,8320]{1,0:T(8,128...) custom-call(f32[64,1280]{1,0:T(8,128)S(1)} %half_scores.3.mine_ref, ...), custom_call_target="tpu_custom_call" | custom-call | tf_op jit(solution)/shard_map/weighted_means/pallas_call | solution.py:421
  59.6 1.8 %collective-permute-start.20 = (bf16[32,4224]{1,0:T(8,128)(2,1)S(1)}, bf16[32,4224]{1,0:T(8,128)(2,1)S(1)}, u32[]{:S(2)}, u32[]{:S(2)}) collective-permute-start(bf16[32,4224]{1,0:T(8,128)(2,1)S(1)} %get-tuple-element.137), channel_id=1, source_target_pairs={{0,8},{8,0},{1,9},{9,1},{2,10},{10,2},{3,11},{11,3},{4,12},{12,4},... | collective-permute-start | bytes 811016 | tf_op jit(solution)/shard_map/ppermute | solution.py:638
  62.2 1.9 %collective-permute-start.18 = (bf16[16,8320]{1,0:T(8,128)(2,1)S(1)}, bf16[16,8320]{1,0:T(8,128)(2,1)S(1)}, u32[]{:S(2)}, u32[]{:S(2)}) collective-permute-start(bf16[16,8320]{1,0:T(8,128)(2,1)S(1)} %get-tuple-element.131), channel_id=1, source_target_pairs={{0,4},{2,6},{4,0},{6,2},{1,5},{3,7},{5,1},{7,3},{8,12},{10,14},{12... | collective-permute-start | bytes 798728 | tf_op jit(solution)/shard_map/ppermute | solution.py:564
  64.1 0.9 %collective-permute-start.19 = (bf16[16,8320]{1,0:T(8,128)(2,1)S(1)}, bf16[16,8320]{1,0:T(8,128)(2,1)S(1)}, u32[]{:S(2)}, u32[]{:S(2)}) collective-permute-start(bf16[16,8320]{1,0:T(8,128)(2,1)S(1)} %get-tuple-element.132), channel_id=1, source_target_pairs={{0,6},{2,4},{4,2},{6,0},{1,7},{3,5},{5,3},{7,1},{8,14},{10,12},{12... | collective-permute-start | bytes 798728 | tf_op jit(solution)/shard_map/ppermute | solution.py:564
  65.0 2.0 %collective-permute-done.23.refs_3_ = bf16[16,4096]{1,0:T(8,128)(2,1)S(1)} collective-permute-done((bf16[16,4096]{1,0:T(8,128)(2,1)S(1)}, bf16[16,4096]{1,0:T(8,128)(2,1)S(1)}, u32[]{:S(2)}, u32[]{:S(2)}) %collective-permute-start.23) | collective-permute-done | bytes 131104 | tf_op jit(solution)/shard_map/ppermute | solution.py:564
  67.5 16.7 %collective-permute-done.24.refs_5_ = bf16[32,4096]{1,0:T(8,128)(2,1)S(1)} collective-permute-done((bf16[32,4096]{1,0:T(8,128)(2,1)S(1)}, bf16[32,4096]{1,0:T(8,128)(2,1)S(1)}, u32[]{:S(2)}, u32[]{:S(2)}) %collective-permute-start.24) | collective-permute-done | bytes 262176 | tf_op jit(solution)/shard_map/ppermute | solution.py:640
  84.2 2.1 %collective-permute-done.19.refs_3_ = bf16[16,8320]{1,0:T(8,128)(2,1)S(1)} collective-permute-done((bf16[16,8320]{1,0:T(8,128)(2,1)S(1)}, bf16[16,8320]{1,0:T(8,128)(2,1)S(1)}, u32[]{:S(2)}, u32[]{:S(2)}) %collective-permute-start.19) | collective-permute-done | bytes 266272 | tf_op jit(solution)/shard_map/ppermute | solution.py:564
  86.3 1.8 %final_mix.1 = bf16[32,8192]{1,0:T(8,128)(2,1)} custom-call(f32[32,64]{1,0:T(8,128)S(1)} %get-tuple-element.77.choice_ref, bf16[16,8320]{1,0:T(8,128)(2,1)S(1)} %get-tuple-element.129.refs_0_, bf16[16,8320]{1,0:T(8,128)(2,1)S(1)} %collective-permute-done.17.refs_1_, bf16[16,8320]{1,0:T(8,128)(2,1)S(1)} %collective-permute-done.18.refs_2_, ...), custom_call_target="tpu_custom_call" | custom-call | tf_op jit(solution)/shard_map/final_mix/pallas_call | solution.py:547
  (33 shorter events, 6.2 us)
Async XLA Ops:
  0.0 10.2 %collective-permute-start.2 = (bf16[1,128,16384]{2,1,0:T(8,128)(2,1)}, bf16[1,128,16384]{2,1,0:T(8,128)(2,1)}, u32[]{:S(2)}, u32[]{:S(2)}) collective-permute-start(bf16[1,128,16384]{2,1,0:T(8,128)(2,1)} %mine_ref.1), channel_id=1, source_target_pairs={{0,1},{1,0},{2,3},{3,2},{4,5},{5,4},{6,7},{7,6},{8,9},{9,8},{10,11... | collective-permute-start | bytes 12582920 | tf_op jit(solution)/shard_map/ppermute | solution.py:607
  1.6 19.9 %collective-permute-start.1 = (bf16[32,5376]{1,0:T(8,128)(2,1)S(1)}, bf16[32,5376]{1,0:T(8,128)(2,1)S(1)}, u32[]{:S(2)}, u32[]{:S(2)}) collective-permute-start(bf16[32,5376]{1,0:T(8,128)(2,1)S(1)} %get-tuple-element.75.refs_0_), channel_id=1, source_target_pairs={{0,8},{8,0},{1,9},{9,1},{2,10},{10,2},{3,11},{11,3},{4,12},{12,4},... | collective-permute-start | bytes 1032200 | tf_op jit(solution)/shard_map/ppermute | solution.py:602
  6.6 16.0 %collective-permute-start.3 = (bf16[16,8448]{1,0:T(8,128)(2,1)S(1)}, bf16[16,8448]{1,0:T(8,128)(2,1)S(1)}, u32[]{:S(2)}, u32[]{:S(2)}) collective-permute-start(bf16[16,8448]{1,0:T(8,128)(2,1)S(1)} %get-tuple-element.81), channel_id=1, source_target_pairs={{0,2},{2,0},{4,6},{6,4},{1,3},{3,1},{5,7},{7,5},{8,10},{10,8},{12,... | collective-permute-start | bytes 811016 | tf_op jit(solution)/shard_map/ppermute | solution.py:564
  8.2 28.4 %collective-permute-start.5 = (bf16[16,8448]{1,0:T(8,128)(2,1)S(1)}, bf16[16,8448]{1,0:T(8,128)(2,1)S(1)}, u32[]{:S(2)}, u32[]{:S(2)}) collective-permute-start(bf16[16,8448]{1,0:T(8,128)(2,1)S(1)} %get-tuple-element.94), channel_id=1, source_target_pairs={{0,4},{2,6},{4,0},{6,2},{1,5},{3,7},{5,1},{7,3},{8,12},{10,14},{12... | collective-permute-start | bytes 811016 | tf_op jit(solution)/shard_map/ppermute | solution.py:564
  9.8 26.8 %collective-permute-start.6 = (bf16[16,8448]{1,0:T(8,128)(2,1)S(1)}, bf16[16,8448]{1,0:T(8,128)(2,1)S(1)}, u32[]{:S(2)}, u32[]{:S(2)}) collective-permute-start(bf16[16,8448]{1,0:T(8,128)(2,1)S(1)} %get-tuple-element.95), channel_id=1, source_target_pairs={{0,6},{2,4},{4,2},{6,0},{1,7},{3,5},{5,3},{7,1},{8,14},{10,12},{12... | collective-permute-start | bytes 811016 | tf_op jit(solution)/shard_map/ppermute | solution.py:564
  22.7 9.6 %collective-permute-start.4 = (bf16[16,5376]{1,0:T(8,128)(2,1)S(1)}, bf16[16,5376]{1,0:T(8,128)(2,1)S(1)}, u32[]{:S(2)}, u32[]{:S(2)}) collective-permute-start(bf16[16,5376]{1,0:T(8,128)(2,1)S(1)} %get-tuple-element.86), channel_id=1, source_target_pairs={{0,2},{2,0},{4,6},{6,4},{1,3},{3,1},{5,7},{7,5},{8,10},{10,8},{12,... | collective-permute-start | bytes 516104 | tf_op jit(solution)/shard_map/ppermute | solution.py:564
  24.3 11.5 %collective-permute-start = (bf16[32,3072]{1,0:T(8,128)(2,1)S(1)}, bf16[32,3072]{1,0:T(8,128)(2,1)S(1)}, u32[]{:S(2)}, u32[]{:S(2)}) collective-permute-start(bf16[32,3072]{1,0:T(8,128)(2,1)S(1)} %get-tuple-element.76.refs_1_), channel_id=1, source_target_pairs={{0,8},{8,0},{1,9},{9,1},{2,10},{10,2},{3,11},{11,3},{4,12},{12,4},... | collective-permute-start | bytes 589832 | tf_op jit(solution)/shard_map/ppermute | solution.py:602
  24.3 17.6 %collective-permute-start.11 = (bf16[16,5376]{1,0:T(8,128)(2,1)S(1)}, bf16[16,5376]{1,0:T(8,128)(2,1)S(1)}, u32[]{:S(2)}, u32[]{:S(2)}) collective-permute-start(bf16[16,5376]{1,0:T(8,128)(2,1)S(1)} %get-tuple-element.114), channel_id=1, source_target_pairs={{0,4},{2,6},{4,0},{6,2},{1,5},{3,7},{5,1},{7,3},{8,12},{10,14},{12... | collective-permute-start | bytes 516104 | tf_op jit(solution)/shard_map/ppermute | solution.py:564
  32.2 9.6 %collective-permute-start.12 = (bf16[16,5376]{1,0:T(8,128)(2,1)S(1)}, bf16[16,5376]{1,0:T(8,128)(2,1)S(1)}, u32[]{:S(2)}, u32[]{:S(2)}) collective-permute-start(bf16[16,5376]{1,0:T(8,128)(2,1)S(1)} %get-tuple-element.115), channel_id=1, source_target_pairs={{0,6},{2,4},{4,2},{6,0},{1,7},{3,5},{5,3},{7,1},{8,14},{10,12},{12... | collective-permute-start | bytes 516104 | tf_op jit(solution)/shard_map/ppermute | solution.py:564
  36.6 6.7 %collective-permute-start.7 = (bf16[16,3072]{1,0:T(8,128)(2,1)S(1)}, bf16[16,3072]{1,0:T(8,128)(2,1)S(1)}, u32[]{:S(2)}, u32[]{:S(2)}) collective-permute-start(bf16[16,3072]{1,0:T(8,128)(2,1)S(1)} %get-tuple-element.104), channel_id=1, source_target_pairs={{0,2},{2,0},{4,6},{6,4},{1,3},{3,1},{5,7},{7,5},{8,10},{10,8},{12,... | collective-permute-start | bytes 294920 | tf_op jit(solution)/shard_map/ppermute | solution.py:564
  37.3 6.0 %collective-permute-start.8 = (bf16[16,3072]{1,0:T(8,128)(2,1)S(1)}, bf16[16,3072]{1,0:T(8,128)(2,1)S(1)}, u32[]{:S(2)}, u32[]{:S(2)}) collective-permute-start(bf16[16,3072]{1,0:T(8,128)(2,1)S(1)} %get-tuple-element.105), channel_id=1, source_target_pairs={{0,4},{2,6},{4,0},{6,2},{1,5},{3,7},{5,1},{7,3},{8,12},{10,14},{12... | collective-permute-start | bytes 294920 | tf_op jit(solution)/shard_map/ppermute | solution.py:564
  37.3 7.1 %collective-permute-start.9 = (bf16[16,3072]{1,0:T(8,128)(2,1)S(1)}, bf16[16,3072]{1,0:T(8,128)(2,1)S(1)}, u32[]{:S(2)}, u32[]{:S(2)}) collective-permute-start(bf16[16,3072]{1,0:T(8,128)(2,1)S(1)} %get-tuple-element.106), channel_id=1, source_target_pairs={{0,6},{2,4},{4,2},{6,0},{1,7},{3,5},{5,3},{7,1},{8,14},{10,12},{12... | collective-permute-start | bytes 294920 | tf_op jit(solution)/shard_map/ppermute | solution.py:564
  45.2 1.7 %collective-permute-start.13 = (f32[64,1280]{1,0:T(8,128)S(1)}, f32[64,1280]{1,0:T(8,128)S(1)}, u32[]{:S(2)}, u32[]{:S(2)}) collective-permute-start(f32[64,1280]{1,0:T(8,128)S(1)} %half_scores.5.mine_ref), channel_id=1, source_target_pairs={{0,1},{1,0},{2,3},{3,2},{4,5},{5,4},{6,7},{7,6},{8,9},{9,8},{10,11... | collective-permute-start | bytes 983048 | tf_op jit(solution)/shard_map/ppermute | solution.py:628
  45.2 2.8 %collective-permute-start.10 = (f32[64,1280]{1,0:T(8,128)S(1)}, f32[64,1280]{1,0:T(8,128)S(1)}, u32[]{:S(2)}, u32[]{:S(2)}) collective-permute-start(f32[64,1280]{1,0:T(8,128)S(1)} %half_scores.3.mine_ref), channel_id=1, source_target_pairs={{0,1},{1,0},{2,3},{3,2},{4,5},{5,4},{6,7},{7,6},{8,9},{9,8},{10,11... | collective-permute-start | bytes 983048 | tf_op jit(solution)/shard_map/ppermute | solution.py:630
  48.1 6.4 %collective-permute-start.14 = (bf16[16,4224]{1,0:T(8,128)(2,1)S(1)}, bf16[16,4224]{1,0:T(8,128)(2,1)S(1)}, u32[]{:S(2)}, u32[]{:S(2)}) collective-permute-start(bf16[16,4224]{1,0:T(8,128)(2,1)S(1)} %get-tuple-element.126), channel_id=1, source_target_pairs={{0,2},{2,0},{4,6},{6,4},{1,3},{3,1},{5,7},{7,5},{8,10},{10,8},{12,... | collective-permute-start | bytes 405512 | tf_op jit(solution)/shard_map/ppermute | solution.py:564
  49.6 9.0 %collective-permute-start.15 = (bf16[16,4224]{1,0:T(8,128)(2,1)S(1)}, bf16[16,4224]{1,0:T(8,128)(2,1)S(1)}, u32[]{:S(2)}, u32[]{:S(2)}) collective-permute-start(bf16[16,4224]{1,0:T(8,128)(2,1)S(1)} %get-tuple-element.127), channel_id=1, source_target_pairs={{0,4},{2,6},{4,0},{6,2},{1,5},{3,7},{5,1},{7,3},{8,12},{10,14},{12... | collective-permute-start | bytes 405512 | tf_op jit(solution)/shard_map/ppermute | solution.py:564
  49.9 9.0 %collective-permute-start.16 = (bf16[16,4224]{1,0:T(8,128)(2,1)S(1)}, bf16[16,4224]{1,0:T(8,128)(2,1)S(1)}, u32[]{:S(2)}, u32[]{:S(2)}) collective-permute-start(bf16[16,4224]{1,0:T(8,128)(2,1)S(1)} %get-tuple-element.128), channel_id=1, source_target_pairs={{0,6},{2,4},{4,2},{6,0},{1,7},{3,5},{5,3},{7,1},{8,14},{10,12},{12... | collective-permute-start | bytes 405512 | tf_op jit(solution)/shard_map/ppermute | solution.py:564
  52.6 9.6 %collective-permute-start.21 = (bf16[16,4096]{1,0:T(8,128)(2,1)S(1)}, bf16[16,4096]{1,0:T(8,128)(2,1)S(1)}, u32[]{:S(2)}, u32[]{:S(2)}) collective-permute-start(bf16[16,4096]{1,0:T(8,128)(2,1)S(1)} %get-tuple-element.142), channel_id=1, source_target_pairs={{0,2},{2,0},{4,6},{6,4},{1,3},{3,1},{5,7},{7,5},{8,10},{10,8},{12,... | collective-permute-start | bytes 393224 | tf_op jit(solution)/shard_map/ppermute | solution.py:564
  54.2 9.9 %collective-permute-start.22 = (bf16[16,4096]{1,0:T(8,128)(2,1)S(1)}, bf16[16,4096]{1,0:T(8,128)(2,1)S(1)}, u32[]{:S(2)}, u32[]{:S(2)}) collective-permute-start(bf16[16,4096]{1,0:T(8,128)(2,1)S(1)} %get-tuple-element.143), channel_id=1, source_target_pairs={{0,4},{2,6},{4,0},{6,2},{1,5},{3,7},{5,1},{7,3},{8,12},{10,14},{12... | collective-permute-start | bytes 393224 | tf_op jit(solution)/shard_map/ppermute | solution.py:564
  54.5 12.5 %collective-permute-start.23 = (bf16[16,4096]{1,0:T(8,128)(2,1)S(1)}, bf16[16,4096]{1,0:T(8,128)(2,1)S(1)}, u32[]{:S(2)}, u32[]{:S(2)}) collective-permute-start(bf16[16,4096]{1,0:T(8,128)(2,1)S(1)} %get-tuple-element.144), channel_id=1, source_target_pairs={{0,6},{2,4},{4,2},{6,0},{1,7},{3,5},{5,3},{7,1},{8,14},{10,12},{12... | collective-permute-start | bytes 393224 | tf_op jit(solution)/shard_map/ppermute | solution.py:564
  59.6 26.6 %collective-permute-start.20 = (bf16[32,4224]{1,0:T(8,128)(2,1)S(1)}, bf16[32,4224]{1,0:T(8,128)(2,1)S(1)}, u32[]{:S(2)}, u32[]{:S(2)}) collective-permute-start(bf16[32,4224]{1,0:T(8,128)(2,1)S(1)} %get-tuple-element.137), channel_id=1, source_target_pairs={{0,8},{8,0},{1,9},{9,1},{2,10},{10,2},{3,11},{11,3},{4,12},{12,4},... | collective-permute-start | bytes 811016 | tf_op jit(solution)/shard_map/ppermute | solution.py:638
  61.5 22.7 %collective-permute-start.17 = (bf16[16,8320]{1,0:T(8,128)(2,1)S(1)}, bf16[16,8320]{1,0:T(8,128)(2,1)S(1)}, u32[]{:S(2)}, u32[]{:S(2)}) collective-permute-start(bf16[16,8320]{1,0:T(8,128)(2,1)S(1)} %get-tuple-element.130), channel_id=1, source_target_pairs={{0,2},{2,0},{4,6},{6,4},{1,3},{3,1},{5,7},{7,5},{8,10},{10,8},{12,... | collective-permute-start | bytes 798728 | tf_op jit(solution)/shard_map/ppermute | solution.py:564
  62.2 22.0 %collective-permute-start.18 = (bf16[16,8320]{1,0:T(8,128)(2,1)S(1)}, bf16[16,8320]{1,0:T(8,128)(2,1)S(1)}, u32[]{:S(2)}, u32[]{:S(2)}) collective-permute-start(bf16[16,8320]{1,0:T(8,128)(2,1)S(1)} %get-tuple-element.131), channel_id=1, source_target_pairs={{0,4},{2,6},{4,0},{6,2},{1,5},{3,7},{5,1},{7,3},{8,12},{10,14},{12... | collective-permute-start | bytes 798728 | tf_op jit(solution)/shard_map/ppermute | solution.py:564
  64.1 22.2 %collective-permute-start.19 = (bf16[16,8320]{1,0:T(8,128)(2,1)S(1)}, bf16[16,8320]{1,0:T(8,128)(2,1)S(1)}, u32[]{:S(2)}, u32[]{:S(2)}) collective-permute-start(bf16[16,8320]{1,0:T(8,128)(2,1)S(1)} %get-tuple-element.132), channel_id=1, source_target_pairs={{0,6},{2,4},{4,2},{6,0},{1,7},{3,5},{5,3},{7,1},{8,14},{10,12},{12... | collective-permute-start | bytes 798728 | tf_op jit(solution)/shard_map/ppermute | solution.py:564
  67.3 16.8 %collective-permute-start.24 = (bf16[32,4096]{1,0:T(8,128)(2,1)S(1)}, bf16[32,4096]{1,0:T(8,128)(2,1)S(1)}, u32[]{:S(2)}, u32[]{:S(2)}) collective-permute-start(bf16[32,4096]{1,0:T(8,128)(2,1)S(1)} %rest_of_mix.1), channel_id=1, source_target_pairs={{0,8},{8,0},{1,9},{9,1},{2,10},{10,2},{3,11},{11,3},{4,12},{12,4},... | collective-permute-start | bytes 786440 | tf_op jit(solution)/shard_map/ppermute | solution.py:640

commit v7 on v6

--- a/solution.py
+++ b/solution.py
@@ -628,7 +628,6 @@
     theirs = lax.ppermute(mine, "ori", swap)
     far_means, weights, inverse = weighted_means(mine, theirs, records_far, *views, given[0])
     near_theirs = lax.ppermute(near_mine, "ori", swap)
-    near_theirs, far_means = lax.optimization_barrier((near_theirs, far_means))
     back_far = trade(far_means, peers)
     rest_means = rest_of_means(weights, inverse, *views, given[1], len(far_means))
     back_rest = trade(rest_means, peers)

time: 88.2 us -> 88.2 us (level)
  no operation moved by 1% of the time
where the time goes in v7:
time: 88.2 us; the launch traced here: 88 us
  waiting for transfers between devices  39.1 us (44%)
  starting transfers between devices  30 us (34%)
  Pallas kernels  18.7 us (21%)
    ppermute x18, starting transfers between devices, trade(): lax.ppermute(pieces[flip], 'lo', [(i, i ^ flip) for i in range(peers)])  23.4 us
    ppermute x1, waiting for transfers between devices, on_device(): rest_part = lax.ppermute(rest_mix, 'hi', across)  16.7 us
    ppermute x2, waiting for transfers between devices, on_device(): far_payload = [lax.ppermute(chunk, 'hi', across) for chunk in payload]  11.5 us
    ppermute x18, waiting for transfers between devices, trade(): lax.ppermute(pieces[flip], 'lo', [(i, i ^ flip) for i in range(peers)])  9.77 us
    ppermute x2, starting transfers between devices, on_device(): far_payload = [lax.ppermute(chunk, 'hi', across) for chunk in payload]  3.65 us
    pallas_call x2, Pallas kernels, weighted_means(): pl.pallas_call(functools.partial(mean_kernel, chunk=chunk, pieces=pieces)...  3.6 us
    pallas_call x3, Pallas kernels, half_scores(): pl.pallas_call(functools.partial(score_kernel, pieces=len(records), spans...  3.58 us
    pallas_call x3, Pallas kernels, pack(): pl.pallas_call(functools.partial(pack_kernel, sources=len(chunks), classe...  3.36 us
  transfers between devices with their start and end apart: 25, of which 10 were waited for; matrix products, arithmetic and copies ran while one was open for 0% of the time, Pallas kernels for 18%

profile of v7, /device:TPU:0, one launch (start us, length us, event | category | flops | bytes accessed | tf_op | source)
XLA Modules:
  0.0 88.0 jit_solution(10316041537159400628)
XLA Ops:
  0.5 1.1 %make_payload.1 = (bf16[32,5376]{1,0:T(8,128)(2,1)S(1)}, bf16[32,3072]{1,0:T(8,128)(2,1)S(1)}) custom-call(s32[1]{0:T(128)} %bitcast.2.core_ref, bf16[32,16384]{1,0:T(8,128)(2,1)} %x_ref.1, bf16[1,32]{1,0:T(2,128)(2,1)} %bitcast.6, s32[2,32]{1,0:T(2,128)} %bitcast.5, s32[32,128]{1,0:T(8,128)} %keep_ref.1), custom_call_target="tpu_custom_call" | custom-call | tf_op jit(solution)/shard_map/make_payload/pallas_call | solution.py:143
  1.6 3.7 %collective-permute-start.1 = (bf16[32,5376]{1,0:T(8,128)(2,1)S(1)}, bf16[32,5376]{1,0:T(8,128)(2,1)S(1)}, u32[]{:S(2)}, u32[]{:S(2)}) collective-permute-start(bf16[32,5376]{1,0:T(8,128)(2,1)S(1)} %get-tuple-element.70.refs_0_), channel_id=1, source_target_pairs={{0,8},{8,0},{1,9},{9,1},{2,10},{10,2},{3,11},{11,3},{4,12},{12,4},... | collective-permute-start | bytes 1032200 | tf_op jit(solution)/shard_map/ppermute | solution.py:602
  5.3 1.3 %pack.2 = (bf16[16,8448]{1,0:T(8,128)(2,1)S(1)}, bf16[16,8448]{1,0:T(8,128)(2,1)S(1)}, bf16[16,8448]{1,0:T(8,128)(2,1)S(1)}, bf16[16,8448]{1,0:T(8,128)(2,1)S(1)}, f32[32,64]{1,0:T(8,128)S(1)}) custom-call(s32[2]{0:T(128)S(1)} %pad_add_fusion.place_ref, bf16[32,5376]{1,0:T(8,128)(2,1)S(1)} %get-tuple-element.70.refs_0_, ...), custom_call_target="tpu_custom_call" | custom-call | tf_op jit(solution)/shard_map/pack/pallas_call | solution.py:223
  6.6 1.6 %collective-permute-start.3 = (bf16[16,8448]{1,0:T(8,128)(2,1)S(1)}, bf16[16,8448]{1,0:T(8,128)(2,1)S(1)}, u32[]{:S(2)}, u32[]{:S(2)}) collective-permute-start(bf16[16,8448]{1,0:T(8,128)(2,1)S(1)} %get-tuple-element.76), channel_id=1, source_target_pairs={{0,2},{2,0},{4,6},{6,4},{1,3},{3,1},{5,7},{7,5},{8,10},{10,8},{12,... | collective-permute-start | bytes 811016 | tf_op jit(solution)/shard_map/ppermute | solution.py:564
  8.2 1.6 %collective-permute-start.5 = (bf16[16,8448]{1,0:T(8,128)(2,1)S(1)}, bf16[16,8448]{1,0:T(8,128)(2,1)S(1)}, u32[]{:S(2)}, u32[]{:S(2)}) collective-permute-start(bf16[16,8448]{1,0:T(8,128)(2,1)S(1)} %get-tuple-element.89), channel_id=1, source_target_pairs={{0,4},{2,6},{4,0},{6,2},{1,5},{3,7},{5,1},{7,3},{8,12},{10,14},{12... | collective-permute-start | bytes 811016 | tf_op jit(solution)/shard_map/ppermute | solution.py:564
  10.2 3.3 %make_views.1 = (bf16[128,8448]{1,0:T(8,128)(2,1)S(1)}, bf16[128,8448]{1,0:T(8,128)(2,1)S(1)}, f32[1,128]{1,0:T(1,128)S(1)}) custom-call(s32[1]{0:T(128)} %bitcast.2.core_ref, bf16[1,128,16384]{2,1,0:T(8,128)(2,1)} %mine_ref.1, bf16[1,128,16384]{2,1,0:T(8,128)(2,1)} %collective-permute-done.2.theirs_ref), custom_call_target="tpu_custom_call" | custom-call | tf_op jit(solution)/shard_map/make_views/pallas_call | solution.py:279
  13.5 8.0 %collective-permute-done.1.refs_0_ = bf16[32,5376]{1,0:T(8,128)(2,1)S(1)} collective-permute-done((bf16[32,5376]{1,0:T(8,128)(2,1)S(1)}, bf16[32,5376]{1,0:T(8,128)(2,1)S(1)}, u32[]{:S(2)}, u32[]{:S(2)}) %collective-permute-start.1) | collective-permute-done | bytes 344096 | tf_op jit(solution)/shard_map/ppermute | solution.py:602
  21.4 1.2 %pack.3 = (bf16[16,5376]{1,0:T(8,128)(2,1)S(1)}, bf16[16,5376]{1,0:T(8,128)(2,1)S(1)}, bf16[16,5376]{1,0:T(8,128)(2,1)S(1)}, bf16[16,5376]{1,0:T(8,128)(2,1)S(1)}, f32[32,64]{1,0:T(8,128)S(1)}) custom-call(s32[2]{0:T(128)S(1)} %pad_add_fusion.place_ref, bf16[32,5376]{1,0:T(8,128)(2,1)S(1)} %collective-permute-done.1.refs_0_), custom_call_target="tpu_custom_call" | custom-call | tf_op jit(solution)/shard_map/pack/pallas_call | solution.py:223
  22.7 1.6 %collective-permute-start.4 = (bf16[16,5376]{1,0:T(8,128)(2,1)S(1)}, bf16[16,5376]{1,0:T(8,128)(2,1)S(1)}, u32[]{:S(2)}, u32[]{:S(2)}) collective-permute-start(bf16[16,5376]{1,0:T(8,128)(2,1)S(1)} %get-tuple-element.81), channel_id=1, source_target_pairs={{0,2},{2,0},{4,6},{6,4},{1,3},{3,1},{5,7},{7,5},{8,10},{10,8},{12,... | collective-permute-start | bytes 516104 | tf_op jit(solution)/shard_map/ppermute | solution.py:564
  24.3 4.0 %collective-permute-start.11 = (bf16[16,5376]{1,0:T(8,128)(2,1)S(1)}, bf16[16,5376]{1,0:T(8,128)(2,1)S(1)}, u32[]{:S(2)}, u32[]{:S(2)}) collective-permute-start(bf16[16,5376]{1,0:T(8,128)(2,1)S(1)} %get-tuple-element.113), channel_id=1, source_target_pairs={{0,4},{2,6},{4,0},{6,2},{1,5},{3,7},{5,1},{7,3},{8,12},{10,14},{12... | collective-permute-start | bytes 516104 | tf_op jit(solution)/shard_map/ppermute | solution.py:564
  28.3 3.9 %collective-permute-done.4.refs_1_ = bf16[16,5376]{1,0:T(8,128)(2,1)S(1)} collective-permute-done((bf16[16,5376]{1,0:T(8,128)(2,1)S(1)}, bf16[16,5376]{1,0:T(8,128)(2,1)S(1)}, u32[]{:S(2)}, u32[]{:S(2)}) %collective-permute-start.4) | collective-permute-done | bytes 172064 | tf_op jit(solution)/shard_map/ppermute | solution.py:564
  32.2 3.5 %collective-permute-done.refs_0_ = bf16[32,3072]{1,0:T(8,128)(2,1)S(1)} collective-permute-done((bf16[32,3072]{1,0:T(8,128)(2,1)S(1)}, bf16[32,3072]{1,0:T(8,128)(2,1)S(1)}, u32[]{:S(2)}, u32[]{:S(2)}) %collective-permute-start) | collective-permute-done | bytes 196640 | tf_op jit(solution)/shard_map/ppermute | solution.py:602
  35.7 0.8 pack_rest.1
  37.3 2.8 %collective-permute-start.9 = (bf16[16,3072]{1,0:T(8,128)(2,1)S(1)}, bf16[16,3072]{1,0:T(8,128)(2,1)S(1)}, u32[]{:S(2)}, u32[]{:S(2)}) collective-permute-start(bf16[16,3072]{1,0:T(8,128)(2,1)S(1)} %get-tuple-element.101), channel_id=1, source_target_pairs={{0,6},{2,4},{4,2},{6,0},{1,7},{3,5},{5,3},{7,1},{8,14},{10,12},{12... | collective-permute-start | bytes 294920 | tf_op jit(solution)/shard_map/ppermute | solution.py:564
  40.1 1.7 %half_scores.3.mine_ref = f32[64,1280]{1,0:T(8,128)S(1)} custom-call(bf16[16,8448]{1,0:T(8,128)(2,1)S(1)} %get-tuple-element.91.refs_0_, bf16[16,8448]{1,0:T(8,128)(2,1)S(1)} %collective-permute-done.3.refs_1_, bf16[16,8448]{1,0:T(8,128)(2,1)S(1)} %collective-permute-done.5.refs_2_, bf16[16,8448]{1,0:T(8,128)(2,1)S(1)} %collective-permute-done.6.refs_3_, ...), custom_call_target="tpu_custom_call" | custom-call | tf_op jit(solution)/shard_map/half_scores/pallas_call | solution.py:340
  41.9 1.1 %half_scores.4.refs_7_ = f32[64,1280]{1,0:T(8,128)S(1)} custom-call(bf16[16,5376]{1,0:T(8,128)(2,1)S(1)} %get-tuple-element.111.refs_0_, bf16[16,5376]{1,0:T(8,128)(2,1)S(1)} %collective-permute-done.4.refs_1_, bf16[16,5376]{1,0:T(8,128)(2,1)S(1)} %collective-permute-done.11.refs_2_, bf16[16,5376]{1,0:T(8,128)(2,1)S(1)} %collective-permute-done.12.refs_3_, ...), custom_call_target="tpu_custom_call" | custom-call | tf_op jit(solution)/shard_map/half_scores/pallas_call | solution.py:340
  43.3 1.1 %collective-permute-done.9.refs_3_ = bf16[16,3072]{1,0:T(8,128)(2,1)S(1)} collective-permute-done((bf16[16,3072]{1,0:T(8,128)(2,1)S(1)}, bf16[16,3072]{1,0:T(8,128)(2,1)S(1)}, u32[]{:S(2)}, u32[]{:S(2)}) %collective-permute-start.9) | collective-permute-done | bytes 98336 | tf_op jit(solution)/shard_map/ppermute | solution.py:564
  45.7 1.1 %collective-permute-done.13.theirs_ref = f32[64,1280]{1,0:T(8,128)S(1)} collective-permute-done((f32[64,1280]{1,0:T(8,128)S(1)}, f32[64,1280]{1,0:T(8,128)S(1)}, u32[]{:S(2)}, u32[]{:S(2)}) %collective-permute-start.13) | collective-permute-done | bytes 327712 | tf_op jit(solution)/shard_map/ppermute | solution.py:628
  46.9 1.2 %weighted_means.3 = (bf16[16,4224]{1,0:T(8,128)(2,1)S(1)}, bf16[16,4224]{1,0:T(8,128)(2,1)S(1)}, bf16[16,4224]{1,0:T(8,128)(2,1)S(1)}, bf16[16,4224]{1,0:T(8,128...) custom-call(f32[64,1280]{1,0:T(8,128)S(1)} %half_scores.5.mine_ref, ...), custom_call_target="tpu_custom_call" | custom-call | tf_op jit(solution)/shard_map/weighted_means/pallas_call | solution.py:421
  48.0 1.6 %collective-permute-start.14 = (bf16[16,4224]{1,0:T(8,128)(2,1)S(1)}, bf16[16,4224]{1,0:T(8,128)(2,1)S(1)}, u32[]{:S(2)}, u32[]{:S(2)}) collective-permute-start(bf16[16,4224]{1,0:T(8,128)(2,1)S(1)} %get-tuple-element.116), channel_id=1, source_target_pairs={{0,2},{2,0},{4,6},{6,4},{1,3},{3,1},{5,7},{7,5},{8,10},{10,8},{12,... | collective-permute-start | bytes 405512 | tf_op jit(solution)/shard_map/ppermute | solution.py:564
  49.9 1.7 %collective-permute-start.16 = (bf16[16,4224]{1,0:T(8,128)(2,1)S(1)}, bf16[16,4224]{1,0:T(8,128)(2,1)S(1)}, u32[]{:S(2)}, u32[]{:S(2)}) collective-permute-start(bf16[16,4224]{1,0:T(8,128)(2,1)S(1)} %get-tuple-element.118), channel_id=1, source_target_pairs={{0,6},{2,4},{4,2},{6,0},{1,7},{3,5},{5,3},{7,1},{8,14},{10,12},{12... | collective-permute-start | bytes 405512 | tf_op jit(solution)/shard_map/ppermute | solution.py:564
  51.6 1.0 %rest_of_means.1 = (bf16[16,4096]{1,0:T(8,128)(2,1)S(1)}, bf16[16,4096]{1,0:T(8,128)(2,1)S(1)}, bf16[16,4096]{1,0:T(8,128)(2,1)S(1)}, bf16[16,4096]{1,0:T(8,128)(2,1)S(1)}) custom-call(bf16[320,256]{1,0:T(8,128)(2,1)S(1)} %get-tuple-element.129.weight_ref, f32[64,128]{1,0:T(8,128)S(1)} %get-tuple-element.130.inverse_ref, ...), custom_call_target="tpu_custom_call" | custom-call | tf_op jit(solution)/shard_map/rest_of_means/pallas_call | solution.py:438
  52.6 1.6 %collective-permute-start.21 = (bf16[16,4096]{1,0:T(8,128)(2,1)S(1)}, bf16[16,4096]{1,0:T(8,128)(2,1)S(1)}, u32[]{:S(2)}, u32[]{:S(2)}) collective-permute-start(bf16[16,4096]{1,0:T(8,128)(2,1)S(1)} %get-tuple-element.132), channel_id=1, source_target_pairs={{0,2},{2,0},{4,6},{6,4},{1,3},{3,1},{5,7},{7,5},{8,10},{10,8},{12,... | collective-permute-start | bytes 393224 | tf_op jit(solution)/shard_map/ppermute | solution.py:564
  54.5 1.7 %collective-permute-start.23 = (bf16[16,4096]{1,0:T(8,128)(2,1)S(1)}, bf16[16,4096]{1,0:T(8,128)(2,1)S(1)}, u32[]{:S(2)}, u32[]{:S(2)}) collective-permute-start(bf16[16,4096]{1,0:T(8,128)(2,1)S(1)} %get-tuple-element.134), channel_id=1, source_target_pairs={{0,6},{2,4},{4,2},{6,0},{1,7},{3,5},{5,3},{7,1},{8,14},{10,12},{12... | collective-permute-start | bytes 393224 | tf_op jit(solution)/shard_map/ppermute | solution.py:564
  56.2 2.4 %weighted_means.2 = (bf16[16,8320]{1,0:T(8,128)(2,1)S(1)}, bf16[16,8320]{1,0:T(8,128)(2,1)S(1)}, bf16[16,8320]{1,0:T(8,128)(2,1)S(1)}, bf16[16,8320]{1,0:T(8,128...) custom-call(f32[64,1280]{1,0:T(8,128)S(1)} %half_scores.3.mine_ref, ...), custom_call_target="tpu_custom_call" | custom-call | tf_op jit(solution)/shard_map/weighted_means/pallas_call | solution.py:421
  59.6 1.8 %collective-permute-start.20 = (bf16[32,4224]{1,0:T(8,128)(2,1)S(1)}, bf16[32,4224]{1,0:T(8,128)(2,1)S(1)}, u32[]{:S(2)}, u32[]{:S(2)}) collective-permute-start(bf16[32,4224]{1,0:T(8,128)(2,1)S(1)} %get-tuple-element.127), channel_id=1, source_target_pairs={{0,8},{8,0},{1,9},{9,1},{2,10},{10,2},{3,11},{11,3},{4,12},{12,4},... | collective-permute-start | bytes 811016 | tf_op jit(solution)/shard_map/ppermute | solution.py:637
  62.2 1.9 %collective-permute-start.18 = (bf16[16,8320]{1,0:T(8,128)(2,1)S(1)}, bf16[16,8320]{1,0:T(8,128)(2,1)S(1)}, u32[]{:S(2)}, u32[]{:S(2)}) collective-permute-start(bf16[16,8320]{1,0:T(8,128)(2,1)S(1)} %get-tuple-element.121), channel_id=1, source_target_pairs={{0,4},{2,6},{4,0},{6,2},{1,5},{3,7},{5,1},{7,3},{8,12},{10,14},{12... | collective-permute-start | bytes 798728 | tf_op jit(solution)/shard_map/ppermute | solution.py:564
  64.1 0.9 %collective-permute-start.19 = (bf16[16,8320]{1,0:T(8,128)(2,1)S(1)}, bf16[16,8320]{1,0:T(8,128)(2,1)S(1)}, u32[]{:S(2)}, u32[]{:S(2)}) collective-permute-start(bf16[16,8320]{1,0:T(8,128)(2,1)S(1)} %get-tuple-element.122), channel_id=1, source_target_pairs={{0,6},{2,4},{4,2},{6,0},{1,7},{3,5},{5,3},{7,1},{8,14},{10,12},{12... | collective-permute-start | bytes 798728 | tf_op jit(solution)/shard_map/ppermute | solution.py:564
  65.0 2.0 %collective-permute-done.23.refs_3_ = bf16[16,4096]{1,0:T(8,128)(2,1)S(1)} collective-permute-done((bf16[16,4096]{1,0:T(8,128)(2,1)S(1)}, bf16[16,4096]{1,0:T(8,128)(2,1)S(1)}, u32[]{:S(2)}, u32[]{:S(2)}) %collective-permute-start.23) | collective-permute-done | bytes 131104 | tf_op jit(solution)/shard_map/ppermute | solution.py:564
  67.4 16.7 %collective-permute-done.24.refs_5_ = bf16[32,4096]{1,0:T(8,128)(2,1)S(1)} collective-permute-done((bf16[32,4096]{1,0:T(8,128)(2,1)S(1)}, bf16[32,4096]{1,0:T(8,128)(2,1)S(1)}, u32[]{:S(2)}, u32[]{:S(2)}) %collective-permute-start.24) | collective-permute-done | bytes 262176 | tf_op jit(solution)/shard_map/ppermute | solution.py:639
  84.2 2.1 %collective-permute-done.19.refs_3_ = bf16[16,8320]{1,0:T(8,128)(2,1)S(1)} collective-permute-done((bf16[16,8320]{1,0:T(8,128)(2,1)S(1)}, bf16[16,8320]{1,0:T(8,128)(2,1)S(1)}, u32[]{:S(2)}, u32[]{:S(2)}) %collective-permute-start.19) | collective-permute-done | bytes 266272 | tf_op jit(solution)/shard_map/ppermute | solution.py:564
  86.3 1.8 %final_mix.1 = bf16[32,8192]{1,0:T(8,128)(2,1)} custom-call(f32[32,64]{1,0:T(8,128)S(1)} %get-tuple-element.72.choice_ref, bf16[16,8320]{1,0:T(8,128)(2,1)S(1)} %get-tuple-element.119.refs_0_, bf16[16,8320]{1,0:T(8,128)(2,1)S(1)} %collective-permute-done.17.refs_1_, bf16[16,8320]{1,0:T(8,128)(2,1)S(1)} %collective-permute-done.18.refs_2_, ...), custom_call_target="tpu_custom_call" | custom-call | tf_op jit(solution)/shard_map/final_mix/pallas_call | solution.py:547
  (33 shorter events, 6.2 us)
Async XLA Ops:
  0.0 10.2 %collective-permute-start.2 = (bf16[1,128,16384]{2,1,0:T(8,128)(2,1)}, bf16[1,128,16384]{2,1,0:T(8,128)(2,1)}, u32[]{:S(2)}, u32[]{:S(2)}) collective-permute-start(bf16[1,128,16384]{2,1,0:T(8,128)(2,1)} %mine_ref.1), channel_id=1, source_target_pairs={{0,1},{1,0},{2,3},{3,2},{4,5},{5,4},{6,7},{7,6},{8,9},{9,8},{10,11... | collective-permute-start | bytes 12582920 | tf_op jit(solution)/shard_map/ppermute | solution.py:607
  1.6 19.9 %collective-permute-start.1 = (bf16[32,5376]{1,0:T(8,128)(2,1)S(1)}, bf16[32,5376]{1,0:T(8,128)(2,1)S(1)}, u32[]{:S(2)}, u32[]{:S(2)}) collective-permute-start(bf16[32,5376]{1,0:T(8,128)(2,1)S(1)} %get-tuple-element.70.refs_0_), channel_id=1, source_target_pairs={{0,8},{8,0},{1,9},{9,1},{2,10},{10,2},{3,11},{11,3},{4,12},{12,4},... | collective-permute-start | bytes 1032200 | tf_op jit(solution)/shard_map/ppermute | solution.py:602
  6.6 16.0 %collective-permute-start.3 = (bf16[16,8448]{1,0:T(8,128)(2,1)S(1)}, bf16[16,8448]{1,0:T(8,128)(2,1)S(1)}, u32[]{:S(2)}, u32[]{:S(2)}) collective-permute-start(bf16[16,8448]{1,0:T(8,128)(2,1)S(1)} %get-tuple-element.76), channel_id=1, source_target_pairs={{0,2},{2,0},{4,6},{6,4},{1,3},{3,1},{5,7},{7,5},{8,10},{10,8},{12,... | collective-permute-start | bytes 811016 | tf_op jit(solution)/shard_map/ppermute | solution.py:564
  8.2 28.4 %collective-permute-start.5 = (bf16[16,8448]{1,0:T(8,128)(2,1)S(1)}, bf16[16,8448]{1,0:T(8,128)(2,1)S(1)}, u32[]{:S(2)}, u32[]{:S(2)}) collective-permute-start(bf16[16,8448]{1,0:T(8,128)(2,1)S(1)} %get-tuple-element.89), channel_id=1, source_target_pairs={{0,4},{2,6},{4,0},{6,2},{1,5},{3,7},{5,1},{7,3},{8,12},{10,14},{12... | collective-permute-start | bytes 811016 | tf_op jit(solution)/shard_map/ppermute | solution.py:564
  9.8 26.8 %collective-permute-start.6 = (bf16[16,8448]{1,0:T(8,128)(2,1)S(1)}, bf16[16,8448]{1,0:T(8,128)(2,1)S(1)}, u32[]{:S(2)}, u32[]{:S(2)}) collective-permute-start(bf16[16,8448]{1,0:T(8,128)(2,1)S(1)} %get-tuple-element.90), channel_id=1, source_target_pairs={{0,6},{2,4},{4,2},{6,0},{1,7},{3,5},{5,3},{7,1},{8,14},{10,12},{12... | collective-permute-start | bytes 811016 | tf_op jit(solution)/shard_map/ppermute | solution.py:564
  22.7 9.6 %collective-permute-start.4 = (bf16[16,5376]{1,0:T(8,128)(2,1)S(1)}, bf16[16,5376]{1,0:T(8,128)(2,1)S(1)}, u32[]{:S(2)}, u32[]{:S(2)}) collective-permute-start(bf16[16,5376]{1,0:T(8,128)(2,1)S(1)} %get-tuple-element.81), channel_id=1, source_target_pairs={{0,2},{2,0},{4,6},{6,4},{1,3},{3,1},{5,7},{7,5},{8,10},{10,8},{12,... | collective-permute-start | bytes 516104 | tf_op jit(solution)/shard_map/ppermute | solution.py:564
  24.3 11.5 %collective-permute-start = (bf16[32,3072]{1,0:T(8,128)(2,1)S(1)}, bf16[32,3072]{1,0:T(8,128)(2,1)S(1)}, u32[]{:S(2)}, u32[]{:S(2)}) collective-permute-start(bf16[32,3072]{1,0:T(8,128)(2,1)S(1)} %get-tuple-element.71.refs_1_), channel_id=1, source_target_pairs={{0,8},{8,0},{1,9},{9,1},{2,10},{10,2},{3,11},{11,3},{4,12},{12,4},... | collective-permute-start | bytes 589832 | tf_op jit(solution)/shard_map/ppermute | solution.py:602
  24.3 17.6 %collective-permute-start.11 = (bf16[16,5376]{1,0:T(8,128)(2,1)S(1)}, bf16[16,5376]{1,0:T(8,128)(2,1)S(1)}, u32[]{:S(2)}, u32[]{:S(2)}) collective-permute-start(bf16[16,5376]{1,0:T(8,128)(2,1)S(1)} %get-tuple-element.113), channel_id=1, source_target_pairs={{0,4},{2,6},{4,0},{6,2},{1,5},{3,7},{5,1},{7,3},{8,12},{10,14},{12... | collective-permute-start | bytes 516104 | tf_op jit(solution)/shard_map/ppermute | solution.py:564
  32.2 9.6 %collective-permute-start.12 = (bf16[16,5376]{1,0:T(8,128)(2,1)S(1)}, bf16[16,5376]{1,0:T(8,128)(2,1)S(1)}, u32[]{:S(2)}, u32[]{:S(2)}) collective-permute-start(bf16[16,5376]{1,0:T(8,128)(2,1)S(1)} %get-tuple-element.114), channel_id=1, source_target_pairs={{0,6},{2,4},{4,2},{6,0},{1,7},{3,5},{5,3},{7,1},{8,14},{10,12},{12... | collective-permute-start | bytes 516104 | tf_op jit(solution)/shard_map/ppermute | solution.py:564
  36.6 6.7 %collective-permute-start.7 = (bf16[16,3072]{1,0:T(8,128)(2,1)S(1)}, bf16[16,3072]{1,0:T(8,128)(2,1)S(1)}, u32[]{:S(2)}, u32[]{:S(2)}) collective-permute-start(bf16[16,3072]{1,0:T(8,128)(2,1)S(1)} %get-tuple-element.99), channel_id=1, source_target_pairs={{0,2},{2,0},{4,6},{6,4},{1,3},{3,1},{5,7},{7,5},{8,10},{10,8},{12,... | collective-permute-start | bytes 294920 | tf_op jit(solution)/shard_map/ppermute | solution.py:564
  37.3 6.0 %collective-permute-start.8 = (bf16[16,3072]{1,0:T(8,128)(2,1)S(1)}, bf16[16,3072]{1,0:T(8,128)(2,1)S(1)}, u32[]{:S(2)}, u32[]{:S(2)}) collective-permute-start(bf16[16,3072]{1,0:T(8,128)(2,1)S(1)} %get-tuple-element.100), channel_id=1, source_target_pairs={{0,4},{2,6},{4,0},{6,2},{1,5},{3,7},{5,1},{7,3},{8,12},{10,14},{12... | collective-permute-start | bytes 294920 | tf_op jit(solution)/shard_map/ppermute | solution.py:564
  37.3 7.1 %collective-permute-start.9 = (bf16[16,3072]{1,0:T(8,128)(2,1)S(1)}, bf16[16,3072]{1,0:T(8,128)(2,1)S(1)}, u32[]{:S(2)}, u32[]{:S(2)}) collective-permute-start(bf16[16,3072]{1,0:T(8,128)(2,1)S(1)} %get-tuple-element.101), channel_id=1, source_target_pairs={{0,6},{2,4},{4,2},{6,0},{1,7},{3,5},{5,3},{7,1},{8,14},{10,12},{12... | collective-permute-start | bytes 294920 | tf_op jit(solution)/shard_map/ppermute | solution.py:564
  45.2 1.7 %collective-permute-start.13 = (f32[64,1280]{1,0:T(8,128)S(1)}, f32[64,1280]{1,0:T(8,128)S(1)}, u32[]{:S(2)}, u32[]{:S(2)}) collective-permute-start(f32[64,1280]{1,0:T(8,128)S(1)} %half_scores.5.mine_ref), channel_id=1, source_target_pairs={{0,1},{1,0},{2,3},{3,2},{4,5},{5,4},{6,7},{7,6},{8,9},{9,8},{10,11... | collective-permute-start | bytes 983048 | tf_op jit(solution)/shard_map/ppermute | solution.py:628
  45.2 8.9 %collective-permute-start.10 = (f32[64,1280]{1,0:T(8,128)S(1)}, f32[64,1280]{1,0:T(8,128)S(1)}, u32[]{:S(2)}, u32[]{:S(2)}) collective-permute-start(f32[64,1280]{1,0:T(8,128)S(1)} %half_scores.3.mine_ref), channel_id=1, source_target_pairs={{0,1},{1,0},{2,3},{3,2},{4,5},{5,4},{6,7},{7,6},{8,9},{9,8},{10,11... | collective-permute-start | bytes 983048 | tf_op jit(solution)/shard_map/ppermute | solution.py:630
  48.0 6.4 %collective-permute-start.14 = (bf16[16,4224]{1,0:T(8,128)(2,1)S(1)}, bf16[16,4224]{1,0:T(8,128)(2,1)S(1)}, u32[]{:S(2)}, u32[]{:S(2)}) collective-permute-start(bf16[16,4224]{1,0:T(8,128)(2,1)S(1)} %get-tuple-element.116), channel_id=1, source_target_pairs={{0,2},{2,0},{4,6},{6,4},{1,3},{3,1},{5,7},{7,5},{8,10},{10,8},{12,... | collective-permute-start | bytes 405512 | tf_op jit(solution)/shard_map/ppermute | solution.py:564
  49.6 9.0 %collective-permute-start.15 = (bf16[16,4224]{1,0:T(8,128)(2,1)S(1)}, bf16[16,4224]{1,0:T(8,128)(2,1)S(1)}, u32[]{:S(2)}, u32[]{:S(2)}) collective-permute-start(bf16[16,4224]{1,0:T(8,128)(2,1)S(1)} %get-tuple-element.117), channel_id=1, source_target_pairs={{0,4},{2,6},{4,0},{6,2},{1,5},{3,7},{5,1},{7,3},{8,12},{10,14},{12... | collective-permute-start | bytes 405512 | tf_op jit(solution)/shard_map/ppermute | solution.py:564
  49.9 9.0 %collective-permute-start.16 = (bf16[16,4224]{1,0:T(8,128)(2,1)S(1)}, bf16[16,4224]{1,0:T(8,128)(2,1)S(1)}, u32[]{:S(2)}, u32[]{:S(2)}) collective-permute-start(bf16[16,4224]{1,0:T(8,128)(2,1)S(1)} %get-tuple-element.118), channel_id=1, source_target_pairs={{0,6},{2,4},{4,2},{6,0},{1,7},{3,5},{5,3},{7,1},{8,14},{10,12},{12... | collective-permute-start | bytes 405512 | tf_op jit(solution)/shard_map/ppermute | solution.py:564
  52.6 9.6 %collective-permute-start.21 = (bf16[16,4096]{1,0:T(8,128)(2,1)S(1)}, bf16[16,4096]{1,0:T(8,128)(2,1)S(1)}, u32[]{:S(2)}, u32[]{:S(2)}) collective-permute-start(bf16[16,4096]{1,0:T(8,128)(2,1)S(1)} %get-tuple-element.132), channel_id=1, source_target_pairs={{0,2},{2,0},{4,6},{6,4},{1,3},{3,1},{5,7},{7,5},{8,10},{10,8},{12,... | collective-permute-start | bytes 393224 | tf_op jit(solution)/shard_map/ppermute | solution.py:564
  54.2 9.9 %collective-permute-start.22 = (bf16[16,4096]{1,0:T(8,128)(2,1)S(1)}, bf16[16,4096]{1,0:T(8,128)(2,1)S(1)}, u32[]{:S(2)}, u32[]{:S(2)}) collective-permute-start(bf16[16,4096]{1,0:T(8,128)(2,1)S(1)} %get-tuple-element.133), channel_id=1, source_target_pairs={{0,4},{2,6},{4,0},{6,2},{1,5},{3,7},{5,1},{7,3},{8,12},{10,14},{12... | collective-permute-start | bytes 393224 | tf_op jit(solution)/shard_map/ppermute | solution.py:564
  54.5 12.5 %collective-permute-start.23 = (bf16[16,4096]{1,0:T(8,128)(2,1)S(1)}, bf16[16,4096]{1,0:T(8,128)(2,1)S(1)}, u32[]{:S(2)}, u32[]{:S(2)}) collective-permute-start(bf16[16,4096]{1,0:T(8,128)(2,1)S(1)} %get-tuple-element.134), channel_id=1, source_target_pairs={{0,6},{2,4},{4,2},{6,0},{1,7},{3,5},{5,3},{7,1},{8,14},{10,12},{12... | collective-permute-start | bytes 393224 | tf_op jit(solution)/shard_map/ppermute | solution.py:564
  59.6 26.6 %collective-permute-start.20 = (bf16[32,4224]{1,0:T(8,128)(2,1)S(1)}, bf16[32,4224]{1,0:T(8,128)(2,1)S(1)}, u32[]{:S(2)}, u32[]{:S(2)}) collective-permute-start(bf16[32,4224]{1,0:T(8,128)(2,1)S(1)} %get-tuple-element.127), channel_id=1, source_target_pairs={{0,8},{8,0},{1,9},{9,1},{2,10},{10,2},{3,11},{11,3},{4,12},{12,4},... | collective-permute-start | bytes 811016 | tf_op jit(solution)/shard_map/ppermute | solution.py:637
  61.5 22.7 %collective-permute-start.17 = (bf16[16,8320]{1,0:T(8,128)(2,1)S(1)}, bf16[16,8320]{1,0:T(8,128)(2,1)S(1)}, u32[]{:S(2)}, u32[]{:S(2)}) collective-permute-start(bf16[16,8320]{1,0:T(8,128)(2,1)S(1)} %get-tuple-element.120), channel_id=1, source_target_pairs={{0,2},{2,0},{4,6},{6,4},{1,3},{3,1},{5,7},{7,5},{8,10},{10,8},{12,... | collective-permute-start | bytes 798728 | tf_op jit(solution)/shard_map/ppermute | solution.py:564
  62.2 22.0 %collective-permute-start.18 = (bf16[16,8320]{1,0:T(8,128)(2,1)S(1)}, bf16[16,8320]{1,0:T(8,128)(2,1)S(1)}, u32[]{:S(2)}, u32[]{:S(2)}) collective-permute-start(bf16[16,8320]{1,0:T(8,128)(2,1)S(1)} %get-tuple-element.121), channel_id=1, source_target_pairs={{0,4},{2,6},{4,0},{6,2},{1,5},{3,7},{5,1},{7,3},{8,12},{10,14},{12... | collective-permute-start | bytes 798728 | tf_op jit(solution)/shard_map/ppermute | solution.py:564
  64.1 22.2 %collective-permute-start.19 = (bf16[16,8320]{1,0:T(8,128)(2,1)S(1)}, bf16[16,8320]{1,0:T(8,128)(2,1)S(1)}, u32[]{:S(2)}, u32[]{:S(2)}) collective-permute-start(bf16[16,8320]{1,0:T(8,128)(2,1)S(1)} %get-tuple-element.122), channel_id=1, source_target_pairs={{0,6},{2,4},{4,2},{6,0},{1,7},{3,5},{5,3},{7,1},{8,14},{10,12},{12... | collective-permute-start | bytes 798728 | tf_op jit(solution)/shard_map/ppermute | solution.py:564
  67.3 16.8 %collective-permute-start.24 = (bf16[32,4096]{1,0:T(8,128)(2,1)S(1)}, bf16[32,4096]{1,0:T(8,128)(2,1)S(1)}, u32[]{:S(2)}, u32[]{:S(2)}) collective-permute-start(bf16[32,4096]{1,0:T(8,128)(2,1)S(1)} %rest_of_mix.1), channel_id=1, source_target_pairs={{0,8},{8,0},{1,9},{9,1},{2,10},{10,2},{3,11},{11,3},{4,12},{12,4},... | collective-permute-start | bytes 786440 | tf_op jit(solution)/shard_map/ppermute | solution.py:639
